TPU v7x, 512 devices: a whole 4x8x8 slice. The times are simulated.
512 devices in a mesh: tm: 16 (over z, core), sx: 8 (over y), sy: 4 (over x).
Axes of the slice: x: 4, y: 8, z: 8, core: 2. Of those that a mesh axis runs over, the one named last changes fastest.
Arguments:
- wall_temp: bfloat16 [64, 32768, 128], P('tm', ('sx', 'sy')), may hold values from -6 to 6
- owner_map: int32 [32768, 1], P(('sx', 'sy')), may hold values from 0 to 31; in each aligned block of 1024 rows (0 to 1023, 1024 to 2047, ...) at most 64 rows name the same one
- stencil_column: int32 [32768], P(('sx', 'sy')), may hold values from 0 to 255
- material: int32 [128, 64, 128], P('sx', 'sy'), may hold values from 0 to 3
- conductivity: float32 [4], replicated, may hold values from 0.1 to 1
- capacity: float32 [4], replicated, may hold values from 0.2 to 1
Outputs:
- temperature: float32 [32, 2, 128, 64, 128], P('tm', None, 'sx', 'sy')
Inputs may be any that keep to these rules, and one draw needn't show every extreme that they name: `owner_map`: among the 1024 patches of one device (aligned blocks of rows), no owner is named more than 64 times, a bound that some block reaches.
All inputs are finite; a program needn't handle non-finite values.
Results may differ from a plain program's by a relative error of at most 0.0034.
Values may be sent and summed in bfloat16 or wider, within the bound.
No kernel may reach another device: no remote copies, remote signals or barrier semaphores. Data moves between devices by JAX's collectives and lax.ppermute only.
A program may use at most 64 MiB of HBM per device.

v0:
```python
import math

import jax
import jax.numpy as jnp
from jax import lax
from jax.sharding import PartitionSpec as P

TIME = 64
HARM = 32
NMAT = 4
SWEEPS = 4


omega_step = 0.1


def with_halo(block, sides, width):
    for axis, dim in sides:
        count = lax.axis_size(axis)
        forward = [(i, i + 1) for i in range(count - 1)]
        backward = [(target, source) for source, target in forward]
        low = lax.ppermute(
            lax.slice_in_dim(block, block.shape[dim] - width, None, axis=dim), axis, forward
        )
        high = lax.ppermute(lax.slice_in_dim(block, 0, width, axis=dim), axis, backward)
        block = jnp.concatenate([low, block, high], axis=dim)
    return block


def dft_table():
    freq_index = jnp.arange(HARM, dtype=jnp.int32)
    time_index = jnp.arange(TIME, dtype=jnp.int32)
    phase_int = freq_index[:, None] * time_index[None, :] % TIME
    angles = phase_int.astype(jnp.float32) * jnp.float32(2.0 * math.pi / TIME)
    amplitude = jnp.float32(2.0 / math.sqrt(TIME))
    table_rows = jnp.stack([amplitude * jnp.cos(angles), -amplitude * jnp.sin(angles)], axis=1)
    return table_rows.reshape(2 * HARM, TIME).astype(jnp.bfloat16)


def lookup(material, table):
    values = jnp.zeros(material.shape, jnp.float32)
    for material_id in range(NMAT):
        values = jnp.where(material == material_id, table[material_id], values)
    return values


def face_value(conduct, other):
    other = jnp.where(other > 0, other, conduct)
    return 2.0 * conduct * other / (conduct + other)


def face_values(conduct, padded):
    next_x = face_value(conduct, padded[2:, 1:-1, 1:-1])
    prev_x = face_value(conduct, padded[:-2, 1:-1, 1:-1])
    next_y = face_value(conduct, padded[1:-1, 2:, 1:-1])
    prev_y = face_value(conduct, padded[1:-1, :-2, 1:-1])
    next_z = face_value(conduct, padded[1:-1, 1:-1, 2:])
    prev_z = face_value(conduct, padded[1:-1, 1:-1, :-2])
    total = next_x + prev_x + next_y + prev_y + next_z + prev_z
    return ((next_x, prev_x, next_y, prev_y, next_z, prev_z), total)


def relax_sweep(padded, source, faces, real_den, imag_den):
    next_x, prev_x, next_y, prev_y, next_z, prev_z = faces
    nearby = next_x * padded[..., 2:, 1:-1, 1:-1] + prev_x * padded[..., :-2, 1:-1, 1:-1]
    nearby = nearby + next_y * padded[..., 1:-1, 2:, 1:-1] + prev_y * padded[..., 1:-1, :-2, 1:-1]
    nearby = nearby + next_z * padded[..., 1:-1, 1:-1, 2:] + prev_z * padded[..., 1:-1, 1:-1, :-2]
    numerator = source + nearby
    real_num = numerator[..., 0, :, :, :]
    imag_num = numerator[..., 1, :, :, :]
    modulus = real_den * real_den + imag_den * imag_den
    real_out = (real_num * real_den + imag_num * imag_den) / modulus
    imag_out = (imag_num * real_den - real_num * imag_den) / modulus
    return jnp.stack([real_out, imag_out], axis=-4)


def to_harmonics(payload):
    transform_rows = dft_table()
    gathered = lax.all_to_all(payload, "tm", split_axis=1, concat_axis=0, tiled=True)
    flattened = gathered.reshape(TIME, gathered.shape[1] * gathered.shape[2])
    harmonic = jnp.dot(transform_rows, flattened, preferred_element_type=jnp.float32)
    harmonic = harmonic.astype(jnp.bfloat16).reshape(2 * HARM, gathered.shape[1], gathered.shape[2])
    return lax.all_to_all(harmonic, "tm", split_axis=0, concat_axis=1, tiled=True)


def to_owners(payload, owner_map, stencil_column):
    owners = lax.axis_size("sx") * lax.axis_size("sy")
    capacity_slots = 2 * payload.shape[1] // owners
    owner_ids = owner_map[:, 0]
    onehot = (owner_ids[:, None] == jnp.arange(owners, dtype=jnp.int32)[None, :]).astype(jnp.int32)
    rank_all = jnp.cumsum(onehot, axis=0) - onehot
    rank_own = jnp.sum(rank_all * onehot, axis=1)
    slot_index = owner_ids * capacity_slots + rank_own
    buffer = jnp.zeros((payload.shape[0], owners * capacity_slots, payload.shape[2]), jnp.bfloat16)
    buffer = buffer.at[:, slot_index, :].set(payload)
    columns = (
        jnp.full((1, owners * capacity_slots), -1, jnp.int32).at[0, slot_index].set(stencil_column)
    )
    return (
        lax.all_to_all(buffer, ("sx", "sy"), split_axis=1, concat_axis=1, tiled=True),
        lax.all_to_all(columns, ("sx", "sy"), split_axis=1, concat_axis=1, tiled=True),
    )


def body(wall_temp, owner_map, stencil_column, material, conductivity, capacity):
    received, columns = to_owners(wall_temp, owner_map, stencil_column)
    harmonic = to_harmonics(received)
    size_x, size_y, size_z = material.shape
    local_harms = harmonic.shape[0] // 2
    column_hits = (jnp.arange(size_x * size_y, dtype=jnp.int32)[:, None] == columns).astype(
        jnp.bfloat16
    )
    source = jnp.einsum("ps,csz->cpz", column_hits, harmonic, preferred_element_type=jnp.float32)
    source = source.reshape(local_harms, 2, size_x, size_y, size_z)
    conduct = lookup(material, conductivity)
    heat_cap = lookup(material, capacity)
    rim = with_halo(conduct.astype(jnp.bfloat16), (("sx", 0), ("sy", 1)), 1).astype(conduct.dtype)
    rim = jnp.pad(rim, ((0, 0), (0, 0), (1, 1)), mode="edge")
    faces, real_den = face_values(conduct, rim)
    harm_index = lax.axis_index("tm") * local_harms + jnp.arange(local_harms, dtype=jnp.int32)
    imag_den = omega_step * harm_index.astype(jnp.float32)[:, None, None, None] * heat_cap
    start = jnp.zeros((local_harms, 2, size_x + 2, size_y + 2, size_z + 2), jnp.float32)
    field = relax_sweep(start, source, faces, real_den, imag_den)
    for sweep in range(SWEEPS - 1):
        padded = with_halo(field, (("sx", 2), ("sy", 3)), 1)
        padded = jnp.pad(padded, ((0, 0), (0, 0), (0, 0), (0, 0), (1, 1)))
        field = relax_sweep(padded, source, faces, real_den, imag_den)
    return field


def solution(mesh):
    in_specs = (
        P("tm", ("sx", "sy"), None),
        P(("sx", "sy"), None),
        P(("sx", "sy")),
        P("sx", "sy", None),
        P(),
        P(),
    )
    out_specs = P("tm", None, "sx", "sy", None)
    return jax.shard_map(body, mesh=mesh, in_specs=in_specs, out_specs=out_specs, check_vma=False)
```

profile of v0, /device:TPU:38, one launch (start us, length us, event | category | flops | bytes accessed | tf_op | source)
XLA Modules:
  0.0 294.0 jit_solution(12163400607939909155)
XLA Ops:
  0.8 9.0 %reduce-window.6 = s32[32,8,128]{2,1,0:T(8,128)S(1)} reduce-window(s32[32,8,128]{2,1,0:T(8,128)S(1)} %fusion.63, s32[]{:T(128)} %constant.17.clone.1), window={size=1x1x128 pad=0_0x0_0x127_0}, to_apply=%region_0.0 | reduce-window | flops 4161536 | bytes 262148 | tf_op jit(solution)/shard_map/reduce-window
  13.1 26.6 %scatter_fusion = bf16[4,2048,128]{2,0,1:T(4,128)(2,1)S(1)} fusion(bf16[4,2048,128]{2,0,1:T(4,128)(2,1)S(1)} %broadcast_in_dim.29, s32[1024]{0:T(1024)S(1)} %bitcast.72, bf16[1024,4,128]{2,1,0:T(4,128)(2,1)S(1)} %copy.34), kind=kCustom, calls=%fused_computation | custom fusion | bytes 3149824 | tf_op jit(solution)/shard_map/scatter | solution.py:95
  39.7 54.7 %all_to_all.47 = bf16[4,2048,128]{2,0,1:T(4,128)(2,1)} all-to-all(bf16[4,2048,128]{2,0,1:T(4,128)(2,1)S(1)} %scatter_fusion), channel_id=1, replica_groups=mesh['tm'=16,'sx'=8,'sy'=4] {'sx','sy'}, dimensions={1} | all-to-all | bytes 4194304 | tf_op jit(solution)/shard_map/all_to_all | solution.py:100
  94.4 10.6 %all-to-all-start.1 = ((bf16[4,2048,128]{2,0,1:T(4,128)(2,1)}), bf16[4,2048,128]{2,0,1:T(4,128)(2,1)S(1)}, u32[]{:S(2)}, u32[]{:S(2)}) async-start(bf16[4,2048,128]{2,0,1:T(4,128)(2,1)} %all_to_all.47), calls=%async_computation.1 | async-start | bytes 4194304 | tf_op jit(solution)/shard_map/all_to_all | solution.py:79
  105.3 4.5 %scatter_custom_fusion.1 = s32[2048]{0:T(1024)S(1)} fusion(s32[1024]{0:T(1024)S(1)} %broadcast_select_fusion, s32[1024]{0:T(1024)} %param.8, s32[]{:T(128)} %constant.25.clone.1), kind=kCustom, calls=%fused_computation.197 | custom fusion | bytes 8704
  110.5 43.7 %all-to-all-done.1 = bf16[4,2048,128]{2,0,1:T(4,128)(2,1)S(1)} async-done(((bf16[4,2048,128]{2,0,1:T(4,128)(2,1)}), bf16[4,2048,128]{2,0,1:T(4,128)(2,1)S(1)}, u32[]{:S(2)}, u32[]{:S(2)}) %all-to-all-start.1) | async-done | bytes 2097184 | tf_op jit(solution)/shard_map/all_to_all | solution.py:79
  154.1 11.1 %all-to-all-start.3 = ((s32[1,32,64]{2,0,1:T(1,128)}), s32[1,32,64]{2,0,1:T(1,128)S(1)}, u32[]{:S(2)}, u32[]{:S(2)}) async-start(s32[1,32,64]{2,0,1:T(1,128)} %all_to_all.41), calls=%async_computation.3 | async-start | bytes 32768 | tf_op jit(solution)/shard_map/all_to_all | solution.py:101
  169.4 4.9 %all-to-all-start.2 = ((bf16[64,128,128]{2,1,0:T(8,128)(2,1)}), bf16[64,128,128]{2,1,0:T(8,128)(2,1)S(1)}, u32[]{:S(2)}, u32[]{:S(2)}) async-start(bf16[64,128,128]{2,1,0:T(8,128)(2,1)} %bitcast.29), calls=%async_computation.2 | async-start | bytes 4194304 | tf_op jit(solution)/shard_map/all_to_all | solution.py:83
  180.8 3.5 %collective-permute-start.1 = (bf16[1,16,128]{2,1,0:T(8,128)(2,1)S(1)}, bf16[1,16,128]{2,1,0:T(8,128)(2,1)S(1)}, u32[]{:S(2)}, u32[]{:S(2)}) collective-permute-start(bf16[1,16,128]{2,1,0:T(8,128)(2,1)S(1)} %get-tuple-element.43), channel_id=1, source_target_pairs={{4,0},{8,4},{12,8},{16,12},{20,16},{24,20},{28,24},{5,1},{9,5},{13... | collective-permute-start | bytes 12296 | tf_op jit(solution)/shard_map/ppermute | solution.py:25
  186.7 4.4 %collective-permute-done = bf16[1,16,128]{2,1,0:T(8,128)(2,1)S(1)} collective-permute-done((bf16[1,16,128]{2,1,0:T(8,128)(2,1)S(1)}, bf16[1,16,128]{2,1,0:T(8,128)(2,1)S(1)}, u32[]{:S(2)}, u32[]{:S(2)}) %collective-permute-start) | collective-permute-done | bytes 4128 | tf_op jit(solution)/shard_map/ppermute | solution.py:22
  194.9 4.2 %collective-permute-done.2 = bf16[18,1,128]{2,1,0:T(2,128)(2,1)S(1)} collective-permute-done((bf16[18,1,128]{2,1,0:T(2,128)(2,1)S(1)}, bf16[18,1,128]{2,1,0:T(2,128)(2,1)S(1)}, u32[]{:S(2)}, u32[]{:S(2)}) %collective-permute-start.2) | collective-permute-done | bytes 4640 | tf_op jit(solution)/shard_map/ppermute | solution.py:22
  203.4 20.1 %all-to-all-done.2 = bf16[64,128,128]{2,1,0:T(8,128)(2,1)S(1)} async-done(((bf16[64,128,128]{2,1,0:T(8,128)(2,1)}), bf16[64,128,128]{2,1,0:T(8,128)(2,1)S(1)}, u32[]{:S(2)}, u32[]{:S(2)}) %all-to-all-start.2) | async-done | bytes 2097184 | tf_op jit(solution)/shard_map/all_to_all | solution.py:83
  223.5 2.9 copy.36
  232.3 3.5 %collective-permute-start.4 = (f32[2,2,1,16,128]{4,3,2,1,0:T(8,128)S(1)}, f32[2,2,1,16,128]{4,3,2,1,0:T(8,128)S(1)}, u32[]{:S(2)}, u32[]{:S(2)}) collective-permute-start(f32[2,2,1,16,128]{4,3,2,1,0:T(8,128)S(1)} %get-tuple-element.37), channel_id=1, source_target_pairs={{4,0},{8,4},{12,8},{16,12},{20,16},{24,20},{28,24},{5,1},{9,5},{13... | collective-permute-start | bytes 98312 | tf_op jit(solution)/shard_map/ppermute | solution.py:25
  238.2 4.7 %collective-permute-done.5 = f32[2,2,1,16,128]{4,3,2,1,0:T(8,128)S(1)} collective-permute-done((f32[2,2,1,16,128]{4,3,2,1,0:T(8,128)S(1)}, f32[2,2,1,16,128]{4,3,2,1,0:T(8,128)S(1)}, u32[]{:S(2)}, u32[]{:S(2)}) %collective-permute-start.5) | collective-permute-done | bytes 32800 | tf_op jit(solution)/shard_map/ppermute | solution.py:22
  247.0 4.2 %collective-permute-done.7 = f32[2,2,18,1,128]{4,3,2,1,0:T(1,128)S(1)} collective-permute-done((f32[2,2,18,1,128]{4,3,2,1,0:T(1,128)S(1)}, f32[2,2,18,1,128]{4,3,2,1,0:T(1,128)S(1)}, u32[]{:S(2)}, u32[]{:S(2)}) %collective-permute-start.7) | collective-permute-done | bytes 36896 | tf_op jit(solution)/shard_map/ppermute | solution.py:22
  254.8 3.8 %collective-permute-start.9 = (f32[2,2,1,16,128]{4,3,2,1,0:T(8,128)S(1)}, f32[2,2,1,16,128]{4,3,2,1,0:T(8,128)S(1)}, u32[]{:S(2)}, u32[]{:S(2)}) collective-permute-start(f32[2,2,1,16,128]{4,3,2,1,0:T(8,128)S(1)} %get-tuple-element.34), channel_id=1, source_target_pairs={{0,4},{4,8},{8,12},{12,16},{16,20},{20,24},{24,28},{1,5},{5,9},{9,... | collective-permute-start | bytes 98312 | tf_op jit(solution)/shard_map/ppermute | solution.py:22
  258.6 3.2 %collective-permute-done.9 = f32[2,2,1,16,128]{4,3,2,1,0:T(8,128)S(1)} collective-permute-done((f32[2,2,1,16,128]{4,3,2,1,0:T(8,128)S(1)}, f32[2,2,1,16,128]{4,3,2,1,0:T(8,128)S(1)}, u32[]{:S(2)}, u32[]{:S(2)}) %collective-permute-start.9) | collective-permute-done | bytes 32800 | tf_op jit(solution)/shard_map/ppermute | solution.py:22
  261.9 3.4 %collective-permute-start.10 = (f32[2,2,18,1,128]{4,3,2,1,0:T(1,128)S(1)}, f32[2,2,18,1,128]{4,3,2,1,0:T(1,128)S(1)}, u32[]{:S(2)}, u32[]{:S(2)}) collective-permute-start(f32[2,2,18,1,128]{4,3,2,1,0:T(1,128)S(1)} %get-tuple-element.29), channel_id=1, source_target_pairs={{1,0},{2,1},{3,2},{5,4},{6,5},{7,6},{9,8},{10,9},{11,10},{13,12},{... | collective-permute-start | bytes 110600 | tf_op jit(solution)/shard_map/ppermute | solution.py:25
  266.9 4.2 %collective-permute-done.11 = f32[2,2,18,1,128]{4,3,2,1,0:T(1,128)S(1)} collective-permute-done((f32[2,2,18,1,128]{4,3,2,1,0:T(1,128)S(1)}, f32[2,2,18,1,128]{4,3,2,1,0:T(1,128)S(1)}, u32[]{:S(2)}, u32[]{:S(2)}) %collective-permute-start.11) | collective-permute-done | bytes 36896 | tf_op jit(solution)/shard_map/ppermute | solution.py:22
  274.9 3.7 %collective-permute-start.13 = (f32[2,2,1,16,128]{4,3,2,1,0:T(8,128)S(1)}, f32[2,2,1,16,128]{4,3,2,1,0:T(8,128)S(1)}, u32[]{:S(2)}, u32[]{:S(2)}) collective-permute-start(f32[2,2,1,16,128]{4,3,2,1,0:T(8,128)S(1)} %get-tuple-element.32), channel_id=1, source_target_pairs={{0,4},{4,8},{8,12},{12,16},{16,20},{20,24},{24,28},{1,5},{5,9},{9,... | collective-permute-start | bytes 98312 | tf_op jit(solution)/shard_map/ppermute | solution.py:22
  278.6 3.3 %collective-permute-done.13 = f32[2,2,1,16,128]{4,3,2,1,0:T(8,128)S(1)} collective-permute-done((f32[2,2,1,16,128]{4,3,2,1,0:T(8,128)S(1)}, f32[2,2,1,16,128]{4,3,2,1,0:T(8,128)S(1)}, u32[]{:S(2)}, u32[]{:S(2)}) %collective-permute-start.13) | collective-permute-done | bytes 32800 | tf_op jit(solution)/shard_map/ppermute | solution.py:22
  281.9 3.4 %collective-permute-start.14 = (f32[2,2,18,1,128]{4,3,2,1,0:T(1,128)S(1)}, f32[2,2,18,1,128]{4,3,2,1,0:T(1,128)S(1)}, u32[]{:S(2)}, u32[]{:S(2)}) collective-permute-start(f32[2,2,18,1,128]{4,3,2,1,0:T(1,128)S(1)} %get-tuple-element.27), channel_id=1, source_target_pairs={{1,0},{2,1},{3,2},{5,4},{6,5},{7,6},{9,8},{10,9},{11,10},{13,12},{... | collective-permute-start | bytes 110600 | tf_op jit(solution)/shard_map/ppermute | solution.py:25
  286.9 4.2 %collective-permute-done.15 = f32[2,2,18,1,128]{4,3,2,1,0:T(1,128)S(1)} collective-permute-done((f32[2,2,18,1,128]{4,3,2,1,0:T(1,128)S(1)}, f32[2,2,18,1,128]{4,3,2,1,0:T(1,128)S(1)}, u32[]{:S(2)}, u32[]{:S(2)}) %collective-permute-start.15) | collective-permute-done | bytes 36896 | tf_op jit(solution)/shard_map/ppermute | solution.py:22
  (91 shorter events, 51.8 us)
Async XLA Ops:
  0.0 11.7 %copy-start = (bf16[4,1024,128]{2,1,0:T(8,128)(2,1)S(1)}, bf16[4,1024,128]{2,1,0:T(8,128)(2,1)}, u32[]{:S(2)}) copy-start(bf16[4,1024,128]{2,1,0:T(8,128)(2,1)} %param.6) | copy-start | bytes 3145732
  94.4 10.7 %copy-start.5 = (s32[2]{0:T(128)S(1)}, s32[2]{0:T(128)}, u32[]{:S(2)}) copy-start(s32[2]{0:T(128)} %constant.69) | copy-start | bytes 28
  94.4 10.8 %copy-start.4 = (s32[2]{0:T(128)S(1)}, s32[2]{0:T(128)}, u32[]{:S(2)}) copy-start(s32[2]{0:T(128)} %constant.66) | copy-start | bytes 28
  94.4 59.7 %all-to-all-start.1 = ((bf16[4,2048,128]{2,0,1:T(4,128)(2,1)}), bf16[4,2048,128]{2,0,1:T(4,128)(2,1)S(1)}, u32[]{:S(2)}, u32[]{:S(2)}) async-start(bf16[4,2048,128]{2,0,1:T(4,128)(2,1)} %all_to_all.47), calls=%async_computation.1 | async-start | bytes 4194304 | tf_op jit(solution)/shard_map/all_to_all | solution.py:79
  154.1 15.3 %all-to-all-start.3 = ((s32[1,32,64]{2,0,1:T(1,128)}), s32[1,32,64]{2,0,1:T(1,128)S(1)}, u32[]{:S(2)}, u32[]{:S(2)}) async-start(s32[1,32,64]{2,0,1:T(1,128)} %all_to_all.41), calls=%async_computation.3 | async-start | bytes 32768 | tf_op jit(solution)/shard_map/all_to_all | solution.py:101
  169.4 5.5 %copy-start.3 = (f32[4]{0:T(128)S(1)}, f32[4]{0:T(128)}, u32[]{:S(2)}) copy-start(f32[4]{0:T(128)} %param.10) | copy-start | bytes 52
  169.4 6.2 %copy-start.1 = (s32[16,16,128]{2,1,0:T(8,128)S(1)}, s32[16,16,128]{2,1,0:T(8,128)}, u32[]{:S(2)}) copy-start(s32[16,16,128]{2,1,0:T(8,128)} %param.9) | copy-start | bytes 393220
  169.4 54.1 %all-to-all-start.2 = ((bf16[64,128,128]{2,1,0:T(8,128)(2,1)}), bf16[64,128,128]{2,1,0:T(8,128)(2,1)S(1)}, u32[]{:S(2)}, u32[]{:S(2)}) async-start(bf16[64,128,128]{2,1,0:T(8,128)(2,1)} %bitcast.29), calls=%async_computation.2 | async-start | bytes 4194304 | tf_op jit(solution)/shard_map/all_to_all | solution.py:83
  180.8 5.9 %collective-permute-start.1 = (bf16[1,16,128]{2,1,0:T(8,128)(2,1)S(1)}, bf16[1,16,128]{2,1,0:T(8,128)(2,1)S(1)}, u32[]{:S(2)}, u32[]{:S(2)}) collective-permute-start(bf16[1,16,128]{2,1,0:T(8,128)(2,1)S(1)} %get-tuple-element.43), channel_id=1, source_target_pairs={{4,0},{8,4},{12,8},{16,12},{20,16},{24,20},{28,24},{5,1},{9,5},{13... | collective-permute-start | bytes 12296 | tf_op jit(solution)/shard_map/ppermute | solution.py:25
  184.3 6.7 %collective-permute-start = (bf16[1,16,128]{2,1,0:T(8,128)(2,1)S(1)}, bf16[1,16,128]{2,1,0:T(8,128)(2,1)S(1)}, u32[]{:S(2)}, u32[]{:S(2)}) collective-permute-start(bf16[1,16,128]{2,1,0:T(8,128)(2,1)S(1)} %get-tuple-element.42), channel_id=1, source_target_pairs={{0,4},{4,8},{8,12},{12,16},{16,20},{20,24},{24,28},{1,5},{5,9},{9,... | collective-permute-start | bytes 12296 | tf_op jit(solution)/shard_map/ppermute | solution.py:22
  191.1 3.8 %collective-permute-start.3 = (bf16[18,1,128]{2,1,0:T(2,128)(2,1)S(1)}, bf16[18,1,128]{2,1,0:T(2,128)(2,1)S(1)}, u32[]{:S(2)}, u32[]{:S(2)}) collective-permute-start(bf16[18,1,128]{2,1,0:T(2,128)(2,1)S(1)} %get-tuple-element.41), channel_id=1, source_target_pairs={{1,0},{2,1},{3,2},{5,4},{6,5},{7,6},{9,8},{10,9},{11,10},{13,12},{... | collective-permute-start | bytes 13832 | tf_op jit(solution)/shard_map/ppermute | solution.py:25
  193.6 5.6 %collective-permute-start.2 = (bf16[18,1,128]{2,1,0:T(2,128)(2,1)S(1)}, bf16[18,1,128]{2,1,0:T(2,128)(2,1)S(1)}, u32[]{:S(2)}, u32[]{:S(2)}) collective-permute-start(bf16[18,1,128]{2,1,0:T(2,128)(2,1)S(1)} %get-tuple-element.40), channel_id=1, source_target_pairs={{0,1},{1,2},{2,3},{4,5},{5,6},{6,7},{8,9},{9,10},{10,11},{12,13},{... | collective-permute-start | bytes 13832 | tf_op jit(solution)/shard_map/ppermute | solution.py:22
  232.3 5.9 %collective-permute-start.4 = (f32[2,2,1,16,128]{4,3,2,1,0:T(8,128)S(1)}, f32[2,2,1,16,128]{4,3,2,1,0:T(8,128)S(1)}, u32[]{:S(2)}, u32[]{:S(2)}) collective-permute-start(f32[2,2,1,16,128]{4,3,2,1,0:T(8,128)S(1)} %get-tuple-element.37), channel_id=1, source_target_pairs={{4,0},{8,4},{12,8},{16,12},{20,16},{24,20},{28,24},{5,1},{9,5},{13... | collective-permute-start | bytes 98312 | tf_op jit(solution)/shard_map/ppermute | solution.py:25
  235.8 7.0 %collective-permute-start.5 = (f32[2,2,1,16,128]{4,3,2,1,0:T(8,128)S(1)}, f32[2,2,1,16,128]{4,3,2,1,0:T(8,128)S(1)}, u32[]{:S(2)}, u32[]{:S(2)}) collective-permute-start(f32[2,2,1,16,128]{4,3,2,1,0:T(8,128)S(1)} %get-tuple-element.36), channel_id=1, source_target_pairs={{0,4},{4,8},{8,12},{12,16},{16,20},{20,24},{24,28},{1,5},{5,9},{9,... | collective-permute-start | bytes 98312 | tf_op jit(solution)/shard_map/ppermute | solution.py:22
  242.9 4.1 %collective-permute-start.6 = (f32[2,2,18,1,128]{4,3,2,1,0:T(1,128)S(1)}, f32[2,2,18,1,128]{4,3,2,1,0:T(1,128)S(1)}, u32[]{:S(2)}, u32[]{:S(2)}) collective-permute-start(f32[2,2,18,1,128]{4,3,2,1,0:T(1,128)S(1)} %get-tuple-element.31), channel_id=1, source_target_pairs={{1,0},{2,1},{3,2},{5,4},{6,5},{7,6},{9,8},{10,9},{11,10},{13,12},{... | collective-permute-start | bytes 110600 | tf_op jit(solution)/shard_map/ppermute | solution.py:25
  245.4 5.9 %collective-permute-start.7 = (f32[2,2,18,1,128]{4,3,2,1,0:T(1,128)S(1)}, f32[2,2,18,1,128]{4,3,2,1,0:T(1,128)S(1)}, u32[]{:S(2)}, u32[]{:S(2)}) collective-permute-start(f32[2,2,18,1,128]{4,3,2,1,0:T(1,128)S(1)} %get-tuple-element.30), channel_id=1, source_target_pairs={{0,1},{1,2},{2,3},{4,5},{5,6},{6,7},{8,9},{9,10},{10,11},{12,13},{... | collective-permute-start | bytes 110600 | tf_op jit(solution)/shard_map/ppermute | solution.py:22
  252.8 5.9 %collective-permute-start.8 = (f32[2,2,1,16,128]{4,3,2,1,0:T(8,128)S(1)}, f32[2,2,1,16,128]{4,3,2,1,0:T(8,128)S(1)}, u32[]{:S(2)}, u32[]{:S(2)}) collective-permute-start(f32[2,2,1,16,128]{4,3,2,1,0:T(8,128)S(1)} %get-tuple-element.35), channel_id=1, source_target_pairs={{4,0},{8,4},{12,8},{16,12},{20,16},{24,20},{28,24},{5,1},{9,5},{13... | collective-permute-start | bytes 98312 | tf_op jit(solution)/shard_map/ppermute | solution.py:25
  254.8 7.0 %collective-permute-start.9 = (f32[2,2,1,16,128]{4,3,2,1,0:T(8,128)S(1)}, f32[2,2,1,16,128]{4,3,2,1,0:T(8,128)S(1)}, u32[]{:S(2)}, u32[]{:S(2)}) collective-permute-start(f32[2,2,1,16,128]{4,3,2,1,0:T(8,128)S(1)} %get-tuple-element.34), channel_id=1, source_target_pairs={{0,4},{4,8},{8,12},{12,16},{16,20},{20,24},{24,28},{1,5},{5,9},{9,... | collective-permute-start | bytes 98312 | tf_op jit(solution)/shard_map/ppermute | solution.py:22
  261.9 5.0 %collective-permute-start.10 = (f32[2,2,18,1,128]{4,3,2,1,0:T(1,128)S(1)}, f32[2,2,18,1,128]{4,3,2,1,0:T(1,128)S(1)}, u32[]{:S(2)}, u32[]{:S(2)}) collective-permute-start(f32[2,2,18,1,128]{4,3,2,1,0:T(1,128)S(1)} %get-tuple-element.29), channel_id=1, source_target_pairs={{1,0},{2,1},{3,2},{5,4},{6,5},{7,6},{9,8},{10,9},{11,10},{13,12},{... | collective-permute-start | bytes 110600 | tf_op jit(solution)/shard_map/ppermute | solution.py:25
  265.3 5.9 %collective-permute-start.11 = (f32[2,2,18,1,128]{4,3,2,1,0:T(1,128)S(1)}, f32[2,2,18,1,128]{4,3,2,1,0:T(1,128)S(1)}, u32[]{:S(2)}, u32[]{:S(2)}) collective-permute-start(f32[2,2,18,1,128]{4,3,2,1,0:T(1,128)S(1)} %get-tuple-element.28), channel_id=1, source_target_pairs={{0,1},{1,2},{2,3},{4,5},{5,6},{6,7},{8,9},{9,10},{10,11},{12,13},{... | collective-permute-start | bytes 110600 | tf_op jit(solution)/shard_map/ppermute | solution.py:22
  272.7 5.9 %collective-permute-start.12 = (f32[2,2,1,16,128]{4,3,2,1,0:T(8,128)S(1)}, f32[2,2,1,16,128]{4,3,2,1,0:T(8,128)S(1)}, u32[]{:S(2)}, u32[]{:S(2)}) collective-permute-start(f32[2,2,1,16,128]{4,3,2,1,0:T(8,128)S(1)} %get-tuple-element.33), channel_id=1, source_target_pairs={{4,0},{8,4},{12,8},{16,12},{20,16},{24,20},{28,24},{5,1},{9,5},{13... | collective-permute-start | bytes 98312 | tf_op jit(solution)/shard_map/ppermute | solution.py:25
  274.9 7.0 %collective-permute-start.13 = (f32[2,2,1,16,128]{4,3,2,1,0:T(8,128)S(1)}, f32[2,2,1,16,128]{4,3,2,1,0:T(8,128)S(1)}, u32[]{:S(2)}, u32[]{:S(2)}) collective-permute-start(f32[2,2,1,16,128]{4,3,2,1,0:T(8,128)S(1)} %get-tuple-element.32), channel_id=1, source_target_pairs={{0,4},{4,8},{8,12},{12,16},{16,20},{20,24},{24,28},{1,5},{5,9},{9,... | collective-permute-start | bytes 98312 | tf_op jit(solution)/shard_map/ppermute | solution.py:22
  281.9 5.0 %collective-permute-start.14 = (f32[2,2,18,1,128]{4,3,2,1,0:T(1,128)S(1)}, f32[2,2,18,1,128]{4,3,2,1,0:T(1,128)S(1)}, u32[]{:S(2)}, u32[]{:S(2)}) collective-permute-start(f32[2,2,18,1,128]{4,3,2,1,0:T(1,128)S(1)} %get-tuple-element.27), channel_id=1, source_target_pairs={{1,0},{2,1},{3,2},{5,4},{6,5},{7,6},{9,8},{10,9},{11,10},{13,12},{... | collective-permute-start | bytes 110600 | tf_op jit(solution)/shard_map/ppermute | solution.py:25
  285.3 5.9 %collective-permute-start.15 = (f32[2,2,18,1,128]{4,3,2,1,0:T(1,128)S(1)}, f32[2,2,18,1,128]{4,3,2,1,0:T(1,128)S(1)}, u32[]{:S(2)}, u32[]{:S(2)}) collective-permute-start(f32[2,2,18,1,128]{4,3,2,1,0:T(1,128)S(1)} %get-tuple-element.26), channel_id=1, source_target_pairs={{0,1},{1,2},{2,3},{4,5},{5,6},{6,7},{8,9},{9,10},{10,11},{12,13},{... | collective-permute-start | bytes 110600 | tf_op jit(solution)/shard_map/ppermute | solution.py:22
  (3 other events, 6.7 us)
where the time goes:
time: 295 us; the launch traced here: 294 us
  waiting for transfers between devices  97.1 us (33%)
  starting transfers between devices  67 us (23%)
  blocking collectives  54.7 us (19%)
  local copies, waits for them, and re-layouts  46.2 us (16%)
  other arithmetic  25.3 us (9%)
  matrix products  3.3 us (1%)
    all_to_all x1, blocking collectives, to_owners(): lax.all_to_all(buffer, ('sx', 'sy'), split_axis=1, concat_axis=1, tiled=T...  54.7 us
    all_to_all x1, waiting for transfers between devices, to_harmonics(): lax.all_to_all(payload, 'tm', split_axis=1, concat_axis=0, tiled=True)  43.7 us
    ppermute x8, waiting for transfers between devices, with_halo(): lax.ppermute(lax.slice_in_dim(block, block.shape[dim] - width, None, axis...  32.5 us
    scatter x1, local copies, waits for them, and re-layouts, to_owners(): buffer = buffer.at[:, slot_index, :].set(payload)  26.6 us
    ppermute x8, starting transfers between devices, with_halo(): lax.ppermute(lax.slice_in_dim(block, 0, width, axis=dim), axis, backward)  23 us
    all_to_all x1, waiting for transfers between devices, to_harmonics(): lax.all_to_all(harmonic, 'tm', split_axis=0, concat_axis=1, tiled=True)  20.1 us
    ppermute x8, starting transfers between devices, with_halo(): lax.ppermute(lax.slice_in_dim(block, block.shape[dim] - width, None, axis...  17.4 us
    all_to_all x1, starting transfers between devices, to_owners(): lax.all_to_all(columns, ('sx', 'sy'), split_axis=1, concat_axis=1, tiled=...  11.1 us
  transfers between devices with their start and end apart: 19, of which 13 were waited for; matrix products, arithmetic and copies ran while one was open for 7% of the time, Pallas kernels for 0%

commit v1 on v0

v1 whole, which is shorter than its diff:
```python
import math

import jax
import jax.numpy as jnp
import numpy as np
from jax import lax
from jax.experimental import pallas as pl
from jax.experimental.pallas import tpu as pltpu
from jax.sharding import PartitionSpec as P

TIME = 64
HARM = 32
NMAT = 4
CAP = 64
OWNERS = 32
WIDE = 3
Y0 = 8
YE = 32

omega_step = 0.1

F32 = jnp.float32
BF16 = jnp.bfloat16


def dft_table():
    freq_index = jnp.arange(HARM, dtype=jnp.int32)
    time_index = jnp.arange(TIME, dtype=jnp.int32)
    phase_int = freq_index[:, None] * time_index[None, :] % TIME
    angles = phase_int.astype(jnp.float32) * jnp.float32(2.0 * math.pi / TIME)
    amplitude = jnp.float32(2.0 / math.sqrt(TIME))
    table_rows = jnp.stack([amplitude * jnp.cos(angles), -amplitude * jnp.sin(angles)], axis=1)
    return table_rows.reshape(2 * HARM, TIME).astype(jnp.bfloat16)


def iota(shape, dim):
    return lax.broadcasted_iota(jnp.int32, shape, dim)


def pack_kernel(wall_ref, owner_ref, column_ref, out_ref, slot_ref):
    times, count, width = wall_ref.shape
    owner = owner_ref[...]
    hit = owner == iota((OWNERS, count), 0)
    hit_b = hit.astype(F32).astype(BF16)
    before = (iota((count, count), 0) < iota((count, count), 1)).astype(F32).astype(BF16)
    earlier = jnp.dot(hit_b, before, preferred_element_type=F32)
    rank = jnp.sum(jnp.where(hit, earlier, 0.0), axis=0, keepdims=True).astype(jnp.int32)
    slot_ref[...] = owner * CAP + rank
    at_rank = (rank == iota((2 * CAP, count), 0) % CAP).astype(F32).astype(BF16)
    marks = jnp.where(hit, (column_ref[...] + 1).astype(F32), 0.0).astype(BF16)
    columns = lax.dot_general(
        marks, at_rank, (((1,), (1,)), ((), ())), preferred_element_type=F32
    )
    out_ref[:, times * CAP :, :] = jnp.broadcast_to(
        columns[:, None, :], (OWNERS, out_ref.shape[1] - times * CAP, width)
    ).astype(BF16)
    group = 4

    def step(g, _):
        place = (slot_ref[...] - g * (group * CAP) == iota((group * CAP, count), 0)).astype(F32).astype(BF16)
        rows = jnp.concatenate([wall_ref[t] for t in range(times)], axis=1)
        moved = jnp.dot(place, rows, preferred_element_type=F32).astype(BF16)
        for t in range(times):
            out_ref[pl.ds(g * group, group), t * CAP : (t + 1) * CAP, :] = moved[
                :, t * width : (t + 1) * width
            ].reshape(group, CAP, width)
        return 0

    lax.fori_loop(0, OWNERS // group, step, 0)


def sum_kernel(rows_ref, out_ref, *, times, cells):
    width = rows_ref.shape[2]
    side = out_ref.shape[1] // times
    acc = jnp.zeros((cells, times * width), F32)
    low = iota((1, width), 1) < CAP
    for g in range(OWNERS // 4):
        marks, rows = [], []
        for pair in range(2):
            i = g * 4 + pair * 2
            even = rows_ref[i, times * CAP : times * CAP + 8, :].astype(F32)[0:1]
            odd = rows_ref[i + 1, times * CAP : times * CAP + 8, :].astype(F32)[0:1]
            column = jnp.where(low, even, odd).astype(jnp.int32) - 1
            marks.append((column == iota((cells, width), 0)).astype(F32).astype(BF16))
            for j in range(2):
                rows.append(
                    jnp.concatenate(
                        [rows_ref[i + j, t * CAP : (t + 1) * CAP, :] for t in range(times)], axis=1
                    )
                )
        acc = acc + jnp.dot(
            jnp.concatenate(marks, axis=1),
            jnp.concatenate(rows, axis=0),
            preferred_element_type=F32,
        )
    total = acc.astype(BF16)
    for t in range(times):
        out_ref[:, t * side : (t + 1) * side, :] = total[:, t * width : (t + 1) * width].reshape(
            cells // side, side, width
        )


def coef_kernel(omega_ref, conductivity_ref, capacity_ref, ids_ref, fx_ref, fy_ref, fz_ref, a_ref, b_ref, c_ref):
    ext_x, ye, width = ids_ref.shape
    harms = a_ref.shape[1]

    def conduct_step(i, _):
        ids = ids_ref[i]
        value = jnp.zeros((ye, width), F32)
        for m in range(NMAT):
            value = jnp.where(ids == m + 1, conductivity_ref[m], value)
        c_ref[i] = value
        return 0

    lax.fori_loop(0, ext_x, conduct_step, 0)

    def face(a, b):
        return jnp.where(b > 0, 2.0 * a * b / jnp.where(b > 0, a + b, 1.0), a)

    lane = iota((ye, width), 1)

    def fx_step(i, _):
        fx_ref[i] = face(c_ref[i], c_ref[i + 1])
        return 0

    lax.fori_loop(0, ext_x - 1, fx_step, 0)

    def step(i, _):
        c = c_ref[i + 1]
        next_x = fx_ref[i + 1]
        prev_x = face(c, c_ref[i])
        next_y = face(c, pltpu.roll(c, ye - 1, 0))
        prev_y = face(c, pltpu.roll(c, 1, 0))
        next_z = face(c, jnp.where(lane == width - 1, 0.0, pltpu.roll(c, width - 1, 1)))
        prev_z = face(c, jnp.where(lane == 0, 0.0, pltpu.roll(c, 1, 1)))
        real_den = next_x + prev_x + next_y + prev_y + next_z + prev_z
        fy_ref[i] = next_y
        fz_ref[i] = jnp.where(lane == width - 1, 0.0, next_z)
        ids = ids_ref[i + 1]
        heat = jnp.zeros((ye, width), F32)
        for m in range(NMAT):
            heat = jnp.where(ids == m + 1, capacity_ref[m], heat)
        inside = ids > 0
        for h in range(harms):
            imag_den = omega_ref[h] * heat
            modulus = real_den * real_den + imag_den * imag_den
            modulus = jnp.where(inside, modulus, 1.0)
            a_ref[i, h] = jnp.where(inside, real_den / modulus, 0.0)
            b_ref[i, h] = jnp.where(inside, imag_den / modulus, 0.0)
        return 0

    lax.fori_loop(0, ext_x - 2, step, 0)


def solve_kernel(mid_ref, xlo_ref, xhi_ref, ylo_ref, yhi_ref, fx_ref, fy_ref, fz_ref, a_ref, b_ref, out_ref, s_ref, f_ref, g_ref):
    size_x = mid_ref.shape[0]
    wide = xlo_ref.shape[0]
    ext_x, comps, ye, width = s_ref.shape
    harms = comps // 2
    side = mid_ref.shape[1] // comps

    s_ref[...] = jnp.zeros(s_ref.shape, F32)
    for ref, start in ((xlo_ref, 0), (mid_ref, wide), (xhi_ref, wide + size_x)):
        for c in range(comps):
            s_ref[start : start + ref.shape[0], c, Y0 : Y0 + side, :] = ref[
                :, c * side : (c + 1) * side, :
            ].astype(F32)
    for k in range(wide):
        for ref, start in ((ylo_ref, Y0 - wide + k), (yhi_ref, Y0 + side + k)):
            s_ref[:, :, start, :] = ref[k].astype(F32).reshape(ext_x, comps, width)

    def quotient(i, h, real_num, imag_num):
        a = a_ref[i, h]
        b = b_ref[i, h]
        return real_num * a + imag_num * b, imag_num * a - real_num * b

    def first(i, _):
        for h in range(harms):
            real_out, imag_out = quotient(i, h, s_ref[i, 2 * h], s_ref[i, 2 * h + 1])
            f_ref[i, 2 * h] = real_out
            f_ref[i, 2 * h + 1] = imag_out
        return 0

    lax.fori_loop(0, ext_x, first, 0)

    def numerator(src, i, c):
        here = src[i, c]
        fy = fy_ref[i]
        fz = fz_ref[i]
        total = s_ref[i, c] + fx_ref[i + 1] * src[i + 1, c] + fx_ref[i] * src[i - 1, c]
        total = total + fy * pltpu.roll(here, ye - 1, 0) + pltpu.roll(fy * here, 1, 0)
        return total + fz * pltpu.roll(here, width - 1, 1) + pltpu.roll(fz * here, 1, 1)

    def sweep(src, dst, margin):
        def step(i, _):
            for h in range(harms):
                real_out, imag_out = quotient(
                    i, h, numerator(src, i, 2 * h), numerator(src, i, 2 * h + 1)
                )
                dst[i, 2 * h] = real_out
                dst[i, 2 * h + 1] = imag_out
            return 0

        lax.fori_loop(margin, ext_x - margin, step, 0)

    sweep(f_ref, g_ref, 1)
    sweep(g_ref, f_ref, 2)

    def last(i, _):
        for h in range(harms):
            real_out, imag_out = quotient(
                i, h, numerator(f_ref, i, 2 * h), numerator(f_ref, i, 2 * h + 1)
            )
            out_ref[h, 0, i - wide] = real_out[Y0 : Y0 + side]
            out_ref[h, 1, i - wide] = imag_out[Y0 : Y0 + side]
        return 0

    lax.fori_loop(wide, wide + size_x, last, 0)


def swap(block, axis, dim, width):
    count = lax.axis_size(axis)
    forward = [(i, i + 1) for i in range(count - 1)]
    backward = [(target, source) for source, target in forward]
    size = block.shape[dim]
    low = lax.ppermute(lax.slice_in_dim(block, size - width, size, axis=dim), axis, forward)
    high = lax.ppermute(lax.slice_in_dim(block, 0, width, axis=dim), axis, backward)
    return low, high


def body(wall_temp, owner_map, stencil_column, material, conductivity, capacity):
    times, count, width = wall_temp.shape
    size_x, size_y, _ = material.shape
    steps = lax.axis_size("tm")
    comps = 2 * HARM // steps
    harms = comps // 2
    ext_x = size_x + 2 * WIDE
    params = pltpu.CompilerParams(vmem_limit_bytes=48 * 1024 * 1024)
    vmem = pl.BlockSpec(memory_space=pltpu.VMEM)
    smem = pl.BlockSpec(memory_space=pltpu.SMEM)

    packed = pl.pallas_call(
        pack_kernel,
        out_shape=jax.ShapeDtypeStruct((OWNERS, times * CAP + 16, width), BF16),
        in_specs=[vmem] * 3,
        out_specs=vmem,
        scratch_shapes=[pltpu.VMEM((1, count), jnp.int32)],
        compiler_params=params,
        name="pack",
    )(wall_temp, owner_map.reshape(1, count), stencil_column.reshape(1, count))
    received = lax.all_to_all(packed, ("sx", "sy"), split_axis=0, concat_axis=0, tiled=True)

    ids = (material + 1).astype(BF16)
    low, high = swap(ids, "sx", 0, WIDE + 1)
    ids = jnp.concatenate([low, ids, high], axis=0)
    low, high = swap(ids, "sy", 1, WIDE + 1)
    rim = jnp.zeros((ids.shape[0], Y0 - WIDE - 1, width), BF16)
    ids = jnp.concatenate([rim, low, ids, high, rim], axis=1).astype(jnp.int32)
    harm_index = lax.axis_index("tm") * harms + jnp.arange(harms, dtype=jnp.int32)
    omega = omega_step * harm_index.astype(F32)
    fx, fy, fz, quot_a, quot_b = pl.pallas_call(
        coef_kernel,
        out_shape=[
            jax.ShapeDtypeStruct((ext_x + 1, YE, width), F32),
            jax.ShapeDtypeStruct((ext_x, YE, width), F32),
            jax.ShapeDtypeStruct((ext_x, YE, width), F32),
            jax.ShapeDtypeStruct((ext_x, harms, YE, width), F32),
            jax.ShapeDtypeStruct((ext_x, harms, YE, width), F32),
        ],
        in_specs=[smem, smem, smem, vmem],
        out_specs=[vmem] * 5,
        scratch_shapes=[pltpu.VMEM((ext_x + 2, YE, width), F32)],
        compiler_params=params,
        name="coef",
    )(omega, conductivity, capacity, ids)

    cells = size_x * size_y
    sums = pl.pallas_call(
        lambda *refs: sum_kernel(*refs, times=times, cells=cells),
        out_shape=jax.ShapeDtypeStruct((size_x, times * size_y, width), BF16),
        in_specs=[vmem],
        out_specs=vmem,
        compiler_params=params,
        name="cell_sum",
    )(received)
    gathered = lax.all_to_all(sums, "tm", split_axis=0, concat_axis=0, tiled=True)
    weights = jnp.kron(dft_table(), jnp.eye(size_y, dtype=BF16))
    harmonic = jnp.dot(
        weights, gathered.reshape(TIME * size_y, width), preferred_element_type=F32
    ).astype(BF16)
    harmonic = harmonic.reshape(steps, comps * size_y, width)
    source = lax.all_to_all(harmonic, "tm", split_axis=0, concat_axis=0, tiled=True)

    xlo, xhi = swap(source, "sx", 0, WIDE)
    rows = jnp.concatenate([xlo, source, xhi], axis=0).reshape(ext_x, comps, size_y, width)
    rows = jnp.concatenate([rows[:, :, :WIDE], rows[:, :, size_y - WIDE :]], axis=2)
    rows = jnp.transpose(rows, (2, 0, 1, 3)).reshape(2 * WIDE, ext_x * comps, width)
    count_y = lax.axis_size("sy")
    forward = [(i, i + 1) for i in range(count_y - 1)]
    backward = [(target, start) for start, target in forward]
    ylo = lax.ppermute(rows[WIDE:], "sy", forward)
    yhi = lax.ppermute(rows[:WIDE], "sy", backward)
    field = pl.pallas_call(
        solve_kernel,
        out_shape=jax.ShapeDtypeStruct((harms, 2, size_x, size_y, width), F32),
        in_specs=[vmem] * 10,
        out_specs=vmem,
        scratch_shapes=[pltpu.VMEM((ext_x, comps, YE, width), F32)] * 3,
        compiler_params=params,
        name="solve",
    )(source, xlo, xhi, ylo, yhi, fx, fy, fz, quot_a, quot_b)
    return field


def solution(mesh):
    in_specs = (
        P("tm", ("sx", "sy"), None),
        P(("sx", "sy"), None),
        P(("sx", "sy")),
        P("sx", "sy", None),
        P(),
        P(),
    )
    out_specs = P("tm", None, "sx", "sy", None)
    return jax.shard_map(body, mesh=mesh, in_specs=in_specs, out_specs=out_specs, check_vma=False)
```

time: 295 us -> 167 us (0.57)
  the two profiles are of different devices: /device:TPU:38 before, /device:TPU:8 now
where the time goes in v1:
time: 167 us; the launch traced here: 166 us
  waiting for transfers between devices  59 us (35%)
  starting transfers between devices  50.1 us (30%)
  local copies, waits for them, and re-layouts  33.4 us (20%)
  Pallas kernels  15.7 us (9%)
  other arithmetic  6.31 us (4%)
    all_to_all x1, waiting for transfers between devices, body(): lax.all_to_all(packed, ('sx', 'sy'), split_axis=0, concat_axis=0, tiled=T...  52.3 us
    mul x1, local copies, waits for them, and re-layouts, body(): weights = jnp.kron(dft_table(), jnp.eye(size_y, dtype=BF16))  29.1 us
    ppermute x3, starting transfers between devices, swap(): lax.ppermute(lax.slice_in_dim(block, size - width, size, axis=dim), axis,...  11.1 us
    all_to_all x1, starting transfers between devices, body(): lax.all_to_all(sums, 'tm', split_axis=0, concat_axis=0, tiled=True)  10.4 us
    all_to_all x1, starting transfers between devices, body(): lax.all_to_all(packed, ('sx', 'sy'), split_axis=0, concat_axis=0, tiled=T...  10.2 us
    all_to_all x1, starting transfers between devices, body(): lax.all_to_all(harmonic, 'tm', split_axis=0, concat_axis=0, tiled=True)  7.34 us
    pallas_call x1, Pallas kernels, body(): pl.pallas_call(solve_kernel, out_shape=jax.ShapeDtypeStruct((harms, 2, si...  7.02 us
    mul x1, other arithmetic, body(): weights = jnp.kron(dft_table(), jnp.eye(size_y, dtype=BF16))  5.97 us
  transfers between devices with their start and end apart: 11, of which 4 were waited for; matrix products, arithmetic and copies ran while one was open for 21% of the time, Pallas kernels for 2%

profile of v1, /device:TPU:8, one launch (start us, length us, event | category | flops | bytes accessed | tf_op | source)
XLA Modules:
  0.0 166.3 jit_solution(3803235981673109655)
XLA Ops:
  0.0 1.2 copy-done.1
  2.6 4.1 %pack.1 = bf16[32,272,128]{2,1,0:T(8,128)(2,1)S(1)} custom-call(bf16[4,1024,128]{2,1,0:T(8,128)(2,1)S(1)} %copy-done.1, s32[1,1024]{1,0:T(1,128)S(1)} %bitcast.14, s32[1,1024]{1,0:T(1,128)S(1)} %bitcast.15), custom_call_target="tpu_custom_call" | custom-call | tf_op jit(solution)/shard_map/pack/pallas_call | solution.py:242
  6.7 1.4 copy-done
  8.1 10.2 %all-to-all-start = ((bf16[32,272,128]{2,1,0:T(8,128)(2,1)}), bf16[32,272,128]{2,1,0:T(8,128)(2,1)S(1)}, u32[]{:S(2)}, u32[]{:S(2)}) async-start(bf16[32,272,128]{2,1,0:T(8,128)(2,1)} %copy-done), calls=%async_computation | async-start | bytes 4456448 | tf_op jit(solution)/shard_map/all_to_all | solution.py:251
  18.4 52.3 %all-to-all-done.refs_0_ = bf16[32,272,128]{2,1,0:T(8,128)(2,1)S(1)} async-done(((bf16[32,272,128]{2,1,0:T(8,128)(2,1)}), bf16[32,272,128]{2,1,0:T(8,128)(2,1)S(1)}, u32[]{:S(2)}, u32[]{:S(2)}) %all-to-all-start) | async-done | bytes 2228256 | tf_op jit(solution)/shard_map/all_to_all | solution.py:251
  70.7 1.4 cell_sum.1
  72.1 10.4 %all-to-all-start.1 = ((bf16[16,64,128]{2,1,0:T(8,128)(2,1)}), bf16[16,64,128]{2,1,0:T(8,128)(2,1)S(1)}, u32[]{:S(2)}, u32[]{:S(2)}) async-start(bf16[16,64,128]{2,1,0:T(8,128)(2,1)} %cell_sum.1), calls=%async_computation.1 | async-start | bytes 524288 | tf_op jit(solution)/shard_map/all_to_all | solution.py:286
  82.6 6.0 %broadcast_multiply_fusion = bf16[64,16,64,16]{3,2,1,0:T(8,128)(2,1)} fusion(bf16[16,16]{1,0:T(8,128)(2,1)S(1)} %fusion.6, bf16[64,64]{1,0:T(8,128)(2,1)S(1)} %bitcast.20), kind=kLoop, calls=%fused_computation | loop fusion | flops 1048576 | bytes 2105856 | tf_op jit(solution)/shard_map/jit(kron)/mul | solution.py:287
  88.5 29.1 %mul.123 = bf16[1024,1024]{1,0:T(8,128)(2,1)S(1)} reshape(bf16[64,16,64,16]{3,2,1,0:T(8,128)(2,1)} %broadcast_multiply_fusion) | data formatting | bytes 4194304 | tf_op jit(solution)/shard_map/jit(kron)/mul | solution.py:287
  117.6 1.4 convolution_convert_fusion
  119.1 7.3 %all-to-all-start.2 = ((bf16[16,64,128]{2,1,0:T(8,128)(2,1)}), bf16[16,64,128]{2,1,0:T(8,128)(2,1)S(1)}, u32[]{:S(2)}, u32[]{:S(2)}) async-start(bf16[16,64,128]{2,1,0:T(8,128)(2,1)} %bitcast.4), calls=%async_computation.2 | async-start | bytes 524288 | tf_op jit(solution)/shard_map/all_to_all | solution.py:292
  126.5 3.9 %collective-permute-start.4 = (bf16[4,16,128]{2,1,0:T(8,128)(2,1)S(1)}, bf16[4,16,128]{2,1,0:T(8,128)(2,1)S(1)}, u32[]{:S(2)}, u32[]{:S(2)}) collective-permute-start(bf16[4,16,128]{2,1,0:T(8,128)(2,1)S(1)} %get-tuple-element.23), channel_id=1, source_target_pairs={{0,4},{4,8},{8,12},{12,16},{16,20},{20,24},{24,28},{1,5},{5,9},{9,... | collective-permute-start | bytes 49160 | tf_op jit(solution)/shard_map/ppermute | solution.py:226
  130.3 2.0 %collective-permute-start.5 = (bf16[4,16,128]{2,1,0:T(8,128)(2,1)S(1)}, bf16[4,16,128]{2,1,0:T(8,128)(2,1)S(1)}, u32[]{:S(2)}, u32[]{:S(2)}) collective-permute-start(bf16[4,16,128]{2,1,0:T(8,128)(2,1)S(1)} %get-tuple-element.24), channel_id=1, source_target_pairs={{4,0},{8,4},{12,8},{16,12},{20,16},{24,20},{28,24},{5,1},{9,5},{13... | collective-permute-start | bytes 49160 | tf_op jit(solution)/shard_map/ppermute | solution.py:227
  132.3 3.6 %collective-permute-done.5 = bf16[4,16,128]{2,1,0:T(8,128)(2,1)S(1)} collective-permute-done((bf16[4,16,128]{2,1,0:T(8,128)(2,1)S(1)}, bf16[4,16,128]{2,1,0:T(8,128)(2,1)S(1)}, u32[]{:S(2)}, u32[]{:S(2)}) %collective-permute-start.5) | collective-permute-done | bytes 16416 | tf_op jit(solution)/shard_map/ppermute | solution.py:227
  136.0 1.6 all-to-all-done.2.mid_ref
  137.6 3.9 %collective-permute-start = (bf16[3,64,128]{2,1,0:T(8,128)(2,1)S(1)}, bf16[3,64,128]{2,1,0:T(8,128)(2,1)S(1)}, u32[]{:S(2)}, u32[]{:S(2)}) collective-permute-start(bf16[3,64,128]{2,1,0:T(8,128)(2,1)S(1)} %get-tuple-element.18), channel_id=1, source_target_pairs={{0,4},{4,8},{8,12},{12,16},{16,20},{20,24},{24,28},{1,5},{5,9},{9,... | collective-permute-start | bytes 147464 | tf_op jit(solution)/shard_map/ppermute | solution.py:226
  141.5 2.0 %collective-permute-start.1 = (bf16[3,64,128]{2,1,0:T(8,128)(2,1)S(1)}, bf16[3,64,128]{2,1,0:T(8,128)(2,1)S(1)}, u32[]{:S(2)}, u32[]{:S(2)}) collective-permute-start(bf16[3,64,128]{2,1,0:T(8,128)(2,1)S(1)} %get-tuple-element.17), channel_id=1, source_target_pairs={{4,0},{8,4},{12,8},{16,12},{20,16},{24,20},{28,24},{5,1},{9,5},{13... | collective-permute-start | bytes 147464 | tf_op jit(solution)/shard_map/ppermute | solution.py:227
  143.5 3.4 %collective-permute-start.6 = (bf16[24,4,128]{2,1,0:T(4,128)(2,1)S(1)}, bf16[24,4,128]{2,1,0:T(4,128)(2,1)S(1)}, u32[]{:S(2)}, u32[]{:S(2)}) collective-permute-start(bf16[24,4,128]{2,1,0:T(4,128)(2,1)S(1)} %get-tuple-element.22), channel_id=1, source_target_pairs={{0,1},{1,2},{2,3},{4,5},{5,6},{6,7},{8,9},{9,10},{10,11},{12,13},{... | collective-permute-start | bytes 73736 | tf_op jit(solution)/shard_map/ppermute | solution.py:226
  146.9 1.3 collective-permute-start.7
  148.6 4.5 %collective-permute-start.2 = (bf16[3,88,128]{2,1,0:T(8,128)(2,1)S(1)}, bf16[3,88,128]{2,1,0:T(8,128)(2,1)S(1)}, u32[]{:S(2)}, u32[]{:S(2)}) collective-permute-start(bf16[3,88,128]{2,1,0:T(8,128)(2,1)S(1)} %bitcast.19), channel_id=1, source_target_pairs={{0,1},{1,2},{2,3},{4,5},{5,6},{6,7},{8,9},{9,10},{10,11},{12,13},{... | collective-permute-start | bytes 202760 | tf_op jit(solution)/shard_map/ppermute | solution.py:301
  153.1 1.3 collective-permute-start.3
  154.7 3.2 %coef.1 = (f32[23,32,128]{2,1,0:T(8,128)S(1)}, f32[22,32,128]{2,1,0:T(8,128)S(1)}, f32[22,32,128]{2,1,0:T(8,128)S(1)}, f32[22,2,32,128]{3,2,1,0:T(8,128)S(1)}, f32[22,2,32,128]{3,2,1,0:T(8,128)S(1)}) custom-call(f32[2]{0:T(128)S(1)} %convert_multiply_fusion.omega_ref, f32[4]{0:T(128)S(1)} %copy-done.4, f32[4]{0:T(128)S(1)} %copy-done.5, ...), custom_call_target="tpu_custom_call" | custom-call | tf_op jit(solution)/shard_map/coef/pallas_call | solution.py:261
  157.9 1.4 collective-permute-done.3.yhi_ref
  159.3 7.0 %solve.1 = f32[2,2,16,16,128]{4,3,2,1,0:T(8,128)} custom-call(bf16[16,64,128]{2,1,0:T(8,128)(2,1)S(1)} %all-to-all-done.2.mid_ref, bf16[3,64,128]{2,1,0:T(8,128)(2,1)S(1)} %collective-permute-done.xlo_ref, bf16[3,64,128]{2,1,0:T(8,128)(2,1)S(1)} %collective-permute-done.1.xhi_ref, bf16[3,88,128]{2,1,0:T(8,128)(2,1)S(1)} %collective-permute-done.2.ylo_ref, ...), custom_call_target="tpu_custom_call" | custom-call | tf_op jit(solution)/shard_map/solve/pallas_call | solution.py:303
  (38 shorter events, 2.1 us)
Async XLA Ops:
  0.0 1.2 copy-start.1
  1.2 0.7 copy-start.2
  1.9 0.7 copy-start.3
  6.7 1.4 copy-start
  8.1 62.6 %all-to-all-start = ((bf16[32,272,128]{2,1,0:T(8,128)(2,1)}), bf16[32,272,128]{2,1,0:T(8,128)(2,1)S(1)}, u32[]{:S(2)}, u32[]{:S(2)}) async-start(bf16[32,272,128]{2,1,0:T(8,128)(2,1)} %copy-done), calls=%async_computation | async-start | bytes 4456448 | tf_op jit(solution)/shard_map/all_to_all | solution.py:251
  72.1 45.5 %all-to-all-start.1 = ((bf16[16,64,128]{2,1,0:T(8,128)(2,1)}), bf16[16,64,128]{2,1,0:T(8,128)(2,1)S(1)}, u32[]{:S(2)}, u32[]{:S(2)}) async-start(bf16[16,64,128]{2,1,0:T(8,128)(2,1)} %cell_sum.1), calls=%async_computation.1 | async-start | bytes 524288 | tf_op jit(solution)/shard_map/all_to_all | solution.py:286
  117.6 8.8 %copy-start.6 = (s32[16,16,128]{2,1,0:T(8,128)S(1)}, s32[16,16,128]{2,1,0:T(8,128)}, u32[]{:S(2)}) copy-start(s32[16,16,128]{2,1,0:T(8,128)} %param.9) | copy-start | bytes 393220
  119.1 35.6 %copy-start.4 = (f32[4]{0:T(128)S(1)}, f32[4]{0:T(128)}, u32[]{:S(2)}) copy-start(f32[4]{0:T(128)} %conductivity_ref.1) | copy-start | bytes 52
  119.1 35.6 %copy-start.5 = (f32[4]{0:T(128)S(1)}, f32[4]{0:T(128)}, u32[]{:S(2)}) copy-start(f32[4]{0:T(128)} %capacity_ref.1) | copy-start | bytes 52
  119.1 18.5 %all-to-all-start.2 = ((bf16[16,64,128]{2,1,0:T(8,128)(2,1)}), bf16[16,64,128]{2,1,0:T(8,128)(2,1)S(1)}, u32[]{:S(2)}, u32[]{:S(2)}) async-start(bf16[16,64,128]{2,1,0:T(8,128)(2,1)} %bitcast.4), calls=%async_computation.2 | async-start | bytes 524288 | tf_op jit(solution)/shard_map/all_to_all | solution.py:292
  126.5 5.9 %collective-permute-start.4 = (bf16[4,16,128]{2,1,0:T(8,128)(2,1)S(1)}, bf16[4,16,128]{2,1,0:T(8,128)(2,1)S(1)}, u32[]{:S(2)}, u32[]{:S(2)}) collective-permute-start(bf16[4,16,128]{2,1,0:T(8,128)(2,1)S(1)} %get-tuple-element.23), channel_id=1, source_target_pairs={{0,4},{4,8},{8,12},{12,16},{16,20},{20,24},{24,28},{1,5},{5,9},{9,... | collective-permute-start | bytes 49160 | tf_op jit(solution)/shard_map/ppermute | solution.py:226
  130.3 5.6 %collective-permute-start.5 = (bf16[4,16,128]{2,1,0:T(8,128)(2,1)S(1)}, bf16[4,16,128]{2,1,0:T(8,128)(2,1)S(1)}, u32[]{:S(2)}, u32[]{:S(2)}) collective-permute-start(bf16[4,16,128]{2,1,0:T(8,128)(2,1)S(1)} %get-tuple-element.24), channel_id=1, source_target_pairs={{4,0},{8,4},{12,8},{16,12},{20,16},{24,20},{28,24},{5,1},{9,5},{13... | collective-permute-start | bytes 49160 | tf_op jit(solution)/shard_map/ppermute | solution.py:227
  137.6 10.6 %collective-permute-start = (bf16[3,64,128]{2,1,0:T(8,128)(2,1)S(1)}, bf16[3,64,128]{2,1,0:T(8,128)(2,1)S(1)}, u32[]{:S(2)}, u32[]{:S(2)}) collective-permute-start(bf16[3,64,128]{2,1,0:T(8,128)(2,1)S(1)} %get-tuple-element.18), channel_id=1, source_target_pairs={{0,4},{4,8},{8,12},{12,16},{16,20},{20,24},{24,28},{1,5},{5,9},{9,... | collective-permute-start | bytes 147464 | tf_op jit(solution)/shard_map/ppermute | solution.py:226
  141.5 6.7 %collective-permute-start.1 = (bf16[3,64,128]{2,1,0:T(8,128)(2,1)S(1)}, bf16[3,64,128]{2,1,0:T(8,128)(2,1)S(1)}, u32[]{:S(2)}, u32[]{:S(2)}) collective-permute-start(bf16[3,64,128]{2,1,0:T(8,128)(2,1)S(1)} %get-tuple-element.17), channel_id=1, source_target_pairs={{4,0},{8,4},{12,8},{16,12},{20,16},{24,20},{28,24},{5,1},{9,5},{13... | collective-permute-start | bytes 147464 | tf_op jit(solution)/shard_map/ppermute | solution.py:227
  143.5 11.0 %collective-permute-start.6 = (bf16[24,4,128]{2,1,0:T(4,128)(2,1)S(1)}, bf16[24,4,128]{2,1,0:T(4,128)(2,1)S(1)}, u32[]{:S(2)}, u32[]{:S(2)}) collective-permute-start(bf16[24,4,128]{2,1,0:T(4,128)(2,1)S(1)} %get-tuple-element.22), channel_id=1, source_target_pairs={{0,1},{1,2},{2,3},{4,5},{5,6},{6,7},{8,9},{9,10},{10,11},{12,13},{... | collective-permute-start | bytes 73736 | tf_op jit(solution)/shard_map/ppermute | solution.py:226
  146.9 7.6 %collective-permute-start.7 = (bf16[24,4,128]{2,1,0:T(4,128)(2,1)S(1)}, bf16[24,4,128]{2,1,0:T(4,128)(2,1)S(1)}, u32[]{:S(2)}, u32[]{:S(2)}) collective-permute-start(bf16[24,4,128]{2,1,0:T(4,128)(2,1)S(1)} %get-tuple-element.21), channel_id=1, source_target_pairs={{1,0},{2,1},{3,2},{5,4},{6,5},{7,6},{9,8},{10,9},{11,10},{13,12},{... | collective-permute-start | bytes 73736 | tf_op jit(solution)/shard_map/ppermute | solution.py:227
  148.6 9.3 %collective-permute-start.2 = (bf16[3,88,128]{2,1,0:T(8,128)(2,1)S(1)}, bf16[3,88,128]{2,1,0:T(8,128)(2,1)S(1)}, u32[]{:S(2)}, u32[]{:S(2)}) collective-permute-start(bf16[3,88,128]{2,1,0:T(8,128)(2,1)S(1)} %bitcast.19), channel_id=1, source_target_pairs={{0,1},{1,2},{2,3},{4,5},{5,6},{6,7},{8,9},{9,10},{10,11},{12,13},{... | collective-permute-start | bytes 202760 | tf_op jit(solution)/shard_map/ppermute | solution.py:301
  153.1 6.2 %collective-permute-start.3 = (bf16[3,88,128]{2,1,0:T(8,128)(2,1)S(1)}, bf16[3,88,128]{2,1,0:T(8,128)(2,1)S(1)}, u32[]{:S(2)}, u32[]{:S(2)}) collective-permute-start(bf16[3,88,128]{2,1,0:T(8,128)(2,1)S(1)} %bitcast.18), channel_id=1, source_target_pairs={{1,0},{2,1},{3,2},{5,4},{6,5},{7,6},{9,8},{10,9},{11,10},{13,12},{... | collective-permute-start | bytes 202760 | tf_op jit(solution)/shard_map/ppermute | solution.py:302

commit v2 on v1

--- a/solution.py
+++ b/solution.py
@@ -2,7 +2,6 @@
 
 import jax
 import jax.numpy as jnp
-import numpy as np
 from jax import lax
 from jax.experimental import pallas as pl
 from jax.experimental.pallas import tpu as pltpu
@@ -100,6 +99,26 @@
         )
 
 
+def weight_kernel(table_ref, out_ref):
+    rows, cols = table_ref.shape
+    side = out_ref.shape[0] // rows
+    wide = rows * side
+    spread = (iota((cols, wide), 1) // side == iota((cols, wide), 0)).astype(F32).astype(BF16)
+    lift = (iota((wide, rows), 0) // side == iota((wide, rows), 1)).astype(F32).astype(BF16)
+    wider = jnp.dot(table_ref[...], spread, preferred_element_type=F32).astype(BF16)
+    step = 256
+    for r in range(wide // step):
+        full = jnp.dot(lift[r * step : (r + 1) * step], wider, preferred_element_type=F32)
+        same = (iota((step, wide), 0) - iota((step, wide), 1)) % side == 0
+        out_ref[r * step : (r + 1) * step, :] = jnp.where(same, full, 0.0).astype(BF16)
+
+
+def dft_kernel(weights_ref, rows_ref, out_ref):
+    out_ref[...] = jnp.dot(
+        weights_ref[...], rows_ref[...], preferred_element_type=F32
+    ).astype(BF16)
+
+
 def coef_kernel(omega_ref, conductivity_ref, capacity_ref, ids_ref, fx_ref, fy_ref, fz_ref, a_ref, b_ref, c_ref):
     ext_x, ye, width = ids_ref.shape
     harms = a_ref.shape[1]
@@ -274,6 +293,18 @@
         name="coef",
     )(omega, conductivity, capacity, ids)
 
+    weights = pl.pallas_call(
+        weight_kernel,
+        out_shape=jax.ShapeDtypeStruct((TIME * size_y, TIME * size_y), BF16),
+        in_specs=[vmem],
+        out_specs=vmem,
+        compiler_params=params,
+        name="weights",
+    )(dft_table())
+    received, fx, fy, fz, quot_a, quot_b, weights = lax.optimization_barrier(
+        (received, fx, fy, fz, quot_a, quot_b, weights)
+    )
+
     cells = size_x * size_y
     sums = pl.pallas_call(
         lambda *refs: sum_kernel(*refs, times=times, cells=cells),
@@ -284,10 +315,14 @@
         name="cell_sum",
     )(received)
     gathered = lax.all_to_all(sums, "tm", split_axis=0, concat_axis=0, tiled=True)
-    weights = jnp.kron(dft_table(), jnp.eye(size_y, dtype=BF16))
-    harmonic = jnp.dot(
-        weights, gathered.reshape(TIME * size_y, width), preferred_element_type=F32
-    ).astype(BF16)
+    harmonic = pl.pallas_call(
+        dft_kernel,
+        out_shape=jax.ShapeDtypeStruct((TIME * size_y, width), BF16),
+        in_specs=[vmem] * 2,
+        out_specs=vmem,
+        compiler_params=params,
+        name="dft",
+    )(weights, gathered.reshape(TIME * size_y, width))
     harmonic = harmonic.reshape(steps, comps * size_y, width)
     source = lax.all_to_all(harmonic, "tm", split_axis=0, concat_axis=0, tiled=True)
 

time: 167 us -> 149 us (0.89)
  the two profiles are of different devices: /device:TPU:8 before, /device:TPU:24 now
where the time goes in v2:
time: 149 us; the launch traced here: 148 us
  waiting for transfers between devices  54.6 us (37%)
  blocking collectives  35.8 us (24%)
  starting transfers between devices  32.3 us (22%)
  Pallas kernels  16.8 us (11%)
  local copies, waits for them, and re-layouts  8.05 us (5%)
    ppermute x3, waiting for transfers between devices, swap(): lax.ppermute(lax.slice_in_dim(block, 0, width, axis=dim), axis, backward)  49.1 us
    all_to_all x1, blocking collectives, body(): lax.all_to_all(sums, 'tm', split_axis=0, concat_axis=0, tiled=True)  21.4 us
    all_to_all x1, blocking collectives, body(): lax.all_to_all(harmonic, 'tm', split_axis=0, concat_axis=0, tiled=True)  14.4 us
    ppermute x3, starting transfers between devices, swap(): lax.ppermute(lax.slice_in_dim(block, size - width, size, axis=dim), axis,...  10.4 us
    all_to_all x1, starting transfers between devices, body(): lax.all_to_all(packed, ('sx', 'sy'), split_axis=0, concat_axis=0, tiled=T...  10.1 us
    unnamed x32, local copies, waits for them, and re-layouts  7.74 us
    ppermute x3, starting transfers between devices, swap(): lax.ppermute(lax.slice_in_dim(block, 0, width, axis=dim), axis, backward)  7.11 us
    pallas_call x1, Pallas kernels, body(): pl.pallas_call(solve_kernel, out_shape=jax.ShapeDtypeStruct((harms, 2, si...  6.97 us
  transfers between devices with their start and end apart: 9, of which 6 were waited for; matrix products, arithmetic and copies ran while one was open for 0% of the time, Pallas kernels for 3%

profile of v2, /device:TPU:24, one launch (start us, length us, event | category | flops | bytes accessed | tf_op | source)
XLA Modules:
  0.0 148.2 jit_solution(18421038688103023582)
XLA Ops:
  0.0 1.2 copy-done.3
  2.6 4.1 %pack.1 = bf16[32,272,128]{2,1,0:T(8,128)(2,1)S(1)} custom-call(bf16[4,1024,128]{2,1,0:T(8,128)(2,1)S(1)} %copy-done.3, s32[1,1024]{1,0:T(1,128)S(1)} %bitcast.13, s32[1,1024]{1,0:T(1,128)S(1)} %bitcast.14), custom_call_target="tpu_custom_call" | custom-call | tf_op jit(solution)/shard_map/pack/pallas_call | solution.py:261
  6.7 1.4 copy-done
  8.1 10.1 %all-to-all-start = ((bf16[32,272,128]{2,1,0:T(8,128)(2,1)}), bf16[32,272,128]{2,1,0:T(8,128)(2,1)S(1)}, u32[]{:S(2)}, u32[]{:S(2)}) async-start(bf16[32,272,128]{2,1,0:T(8,128)(2,1)} %copy-done), calls=%async_computation | async-start | bytes 4456448 | tf_op jit(solution)/shard_map/all_to_all | solution.py:270
  18.3 2.5 %collective-permute-start.1 = (bf16[4,16,128]{2,1,0:T(8,128)(2,1)S(1)}, bf16[4,16,128]{2,1,0:T(8,128)(2,1)S(1)}, u32[]{:S(2)}, u32[]{:S(2)}) collective-permute-start(bf16[4,16,128]{2,1,0:T(8,128)(2,1)S(1)} %get-tuple-element.38), channel_id=1, source_target_pairs={{4,0},{8,4},{12,8},{16,12},{20,16},{24,20},{28,24},{5,1},{9,5},{13... | collective-permute-start | bytes 49160 | tf_op jit(solution)/shard_map/ppermute | solution.py:246
  20.7 4.6 %collective-permute-start = (bf16[4,16,128]{2,1,0:T(8,128)(2,1)S(1)}, bf16[4,16,128]{2,1,0:T(8,128)(2,1)S(1)}, u32[]{:S(2)}, u32[]{:S(2)}) collective-permute-start(bf16[4,16,128]{2,1,0:T(8,128)(2,1)S(1)} %get-tuple-element.37), channel_id=1, source_target_pairs={{0,4},{4,8},{8,12},{12,16},{16,20},{20,24},{24,28},{1,5},{5,9},{9,... | collective-permute-start | bytes 49160 | tf_op jit(solution)/shard_map/ppermute | solution.py:245
  25.4 43.7 %collective-permute-done.1 = bf16[4,16,128]{2,1,0:T(8,128)(2,1)S(1)} collective-permute-done((bf16[4,16,128]{2,1,0:T(8,128)(2,1)S(1)}, bf16[4,16,128]{2,1,0:T(8,128)(2,1)S(1)}, u32[]{:S(2)}, u32[]{:S(2)}) %collective-permute-start.1) | collective-permute-done | bytes 16416 | tf_op jit(solution)/shard_map/ppermute | solution.py:246
  69.2 3.4 %collective-permute-start.2 = (bf16[24,4,128]{2,1,0:T(4,128)(2,1)S(1)}, bf16[24,4,128]{2,1,0:T(4,128)(2,1)S(1)}, u32[]{:S(2)}, u32[]{:S(2)}) collective-permute-start(bf16[24,4,128]{2,1,0:T(4,128)(2,1)S(1)} %get-tuple-element.36), channel_id=1, source_target_pairs={{0,1},{1,2},{2,3},{4,5},{5,6},{6,7},{8,9},{9,10},{10,11},{12,13},{... | collective-permute-start | bytes 73736 | tf_op jit(solution)/shard_map/ppermute | solution.py:245
  72.6 1.3 collective-permute-start.3
  74.0 1.2 weights.1.weights_ref
  75.1 1.3 copy-done.1
  76.5 1.9 %collective-permute-done.3 = bf16[24,4,128]{2,1,0:T(4,128)(2,1)S(1)} collective-permute-done((bf16[24,4,128]{2,1,0:T(4,128)(2,1)S(1)}, bf16[24,4,128]{2,1,0:T(4,128)(2,1)S(1)}, u32[]{:S(2)}, u32[]{:S(2)}) %collective-permute-start.3) | collective-permute-done | bytes 24608 | tf_op jit(solution)/shard_map/ppermute | solution.py:246
  78.6 3.2 %coef.1 = (f32[23,32,128]{2,1,0:T(8,128)S(1)}, f32[22,32,128]{2,1,0:T(8,128)S(1)}, f32[22,32,128]{2,1,0:T(8,128)S(1)}, f32[22,2,32,128]{3,2,1,0:T(8,128)S(1)}, f32[22,2,32,128]{3,2,1,0:T(8,128)S(1)}) custom-call(f32[2]{0:T(128)S(1)} %convert_multiply_fusion.omega_ref, f32[4]{0:T(128)S(1)} %copy-done.12, f32[4]{0:T(128)S(1)} %copy-done.13, ...), custom_call_target="tpu_custom_call" | custom-call | tf_op jit(solution)/shard_map/coef/pallas_call | solution.py:280
  81.8 0.9 copy-done.4
  83.4 0.7 copy-done.8
  84.8 21.4 %all_to_all.15 = bf16[16,64,128]{2,1,0:T(8,128)(2,1)S(1)} all-to-all(bf16[16,64,128]{2,1,0:T(8,128)(2,1)S(1)} %cell_sum.1), channel_id=1, replica_groups=mesh['tm'=16,'sx'=8,'sy'=4] {'tm'}, dimensions={0} | all-to-all | bytes 524288 | tf_op jit(solution)/shard_map/all_to_all | solution.py:317
  106.9 14.4 %all_to_all.16.mid_ref = bf16[16,64,128]{2,1,0:T(8,128)(2,1)S(1)} all-to-all(bf16[16,64,128]{2,1,0:T(8,128)(2,1)S(1)} %bitcast.11), channel_id=1, replica_groups=mesh['tm'=16,'sx'=8,'sy'=4] {'tm'}, dimensions={0} | all-to-all | bytes 524288 | tf_op jit(solution)/shard_map/all_to_all | solution.py:327
  121.3 2.5 %collective-permute-start.4 = (bf16[3,64,128]{2,1,0:T(8,128)(2,1)S(1)}, bf16[3,64,128]{2,1,0:T(8,128)(2,1)S(1)}, u32[]{:S(2)}, u32[]{:S(2)}) collective-permute-start(bf16[3,64,128]{2,1,0:T(8,128)(2,1)S(1)} %get-tuple-element.32), channel_id=1, source_target_pairs={{0,4},{4,8},{8,12},{12,16},{16,20},{20,24},{24,28},{1,5},{5,9},{9,... | collective-permute-start | bytes 147464 | tf_op jit(solution)/shard_map/ppermute | solution.py:245
  123.8 3.4 %collective-permute-start.5 = (bf16[3,64,128]{2,1,0:T(8,128)(2,1)S(1)}, bf16[3,64,128]{2,1,0:T(8,128)(2,1)S(1)}, u32[]{:S(2)}, u32[]{:S(2)}) collective-permute-start(bf16[3,64,128]{2,1,0:T(8,128)(2,1)S(1)} %get-tuple-element.31), channel_id=1, source_target_pairs={{4,0},{8,4},{12,8},{16,12},{20,16},{24,20},{28,24},{5,1},{9,5},{13... | collective-permute-start | bytes 147464 | tf_op jit(solution)/shard_map/ppermute | solution.py:246
  127.8 3.4 %collective-permute-done.5.xhi_ref = bf16[3,64,128]{2,1,0:T(8,128)(2,1)S(1)} collective-permute-done((bf16[3,64,128]{2,1,0:T(8,128)(2,1)S(1)}, bf16[3,64,128]{2,1,0:T(8,128)(2,1)S(1)}, u32[]{:S(2)}, u32[]{:S(2)}) %collective-permute-start.5) | collective-permute-done | bytes 49184 | tf_op jit(solution)/shard_map/ppermute | solution.py:246
  131.6 3.4 %collective-permute-start.6 = (bf16[3,88,128]{2,1,0:T(8,128)(2,1)S(1)}, bf16[3,88,128]{2,1,0:T(8,128)(2,1)S(1)}, u32[]{:S(2)}, u32[]{:S(2)}) collective-permute-start(bf16[3,88,128]{2,1,0:T(8,128)(2,1)S(1)} %bitcast.17), channel_id=1, source_target_pairs={{0,1},{1,2},{2,3},{4,5},{5,6},{6,7},{8,9},{9,10},{10,11},{12,13},{... | collective-permute-start | bytes 202760 | tf_op jit(solution)/shard_map/ppermute | solution.py:336
  135.0 1.3 collective-permute-start.7
  136.9 4.3 %collective-permute-done.7.yhi_ref = bf16[3,88,128]{2,1,0:T(8,128)(2,1)S(1)} collective-permute-done((bf16[3,88,128]{2,1,0:T(8,128)(2,1)S(1)}, bf16[3,88,128]{2,1,0:T(8,128)(2,1)S(1)}, u32[]{:S(2)}, u32[]{:S(2)}) %collective-permute-start.7) | collective-permute-done | bytes 67616 | tf_op jit(solution)/shard_map/ppermute | solution.py:337
  141.2 7.0 %solve.1 = f32[2,2,16,16,128]{4,3,2,1,0:T(8,128)} custom-call(bf16[16,64,128]{2,1,0:T(8,128)(2,1)S(1)} %all_to_all.16.mid_ref, bf16[3,64,128]{2,1,0:T(8,128)(2,1)S(1)} %collective-permute-done.4.xlo_ref, bf16[3,64,128]{2,1,0:T(8,128)(2,1)S(1)} %collective-permute-done.5.xhi_ref, bf16[3,88,128]{2,1,0:T(8,128)(2,1)S(1)} %collective-permute-done.6.ylo_ref, ...), custom_call_target="tpu_custom_call" | custom-call | tf_op jit(solution)/shard_map/solve/pallas_call | solution.py:338
  (50 shorter events, 5.5 us)
Async XLA Ops:
  0.0 1.2 copy-start.3
  1.2 0.7 copy-start.10
  1.9 0.7 copy-start.11
  6.7 1.4 copy-start
  8.1 10.1 %copy-start.14 = (s32[16,16,128]{2,1,0:T(8,128)S(1)}, s32[16,16,128]{2,1,0:T(8,128)}, u32[]{:S(2)}) copy-start(s32[16,16,128]{2,1,0:T(8,128)} %param.9) | copy-start | bytes 393220
  8.1 76.0 %all-to-all-start = ((bf16[32,272,128]{2,1,0:T(8,128)(2,1)}), bf16[32,272,128]{2,1,0:T(8,128)(2,1)S(1)}, u32[]{:S(2)}, u32[]{:S(2)}) async-start(bf16[32,272,128]{2,1,0:T(8,128)(2,1)} %copy-done), calls=%async_computation | async-start | bytes 4456448 | tf_op jit(solution)/shard_map/all_to_all | solution.py:270
  18.2 60.3 %copy-start.12 = (f32[4]{0:T(128)S(1)}, f32[4]{0:T(128)}, u32[]{:S(2)}) copy-start(f32[4]{0:T(128)} %conductivity_ref.1) | copy-start | bytes 52
  18.2 60.3 %copy-start.13 = (f32[4]{0:T(128)S(1)}, f32[4]{0:T(128)}, u32[]{:S(2)}) copy-start(f32[4]{0:T(128)} %capacity_ref.1) | copy-start | bytes 52
  18.3 50.9 %collective-permute-start.1 = (bf16[4,16,128]{2,1,0:T(8,128)(2,1)S(1)}, bf16[4,16,128]{2,1,0:T(8,128)(2,1)S(1)}, u32[]{:S(2)}, u32[]{:S(2)}) collective-permute-start(bf16[4,16,128]{2,1,0:T(8,128)(2,1)S(1)} %get-tuple-element.38), channel_id=1, source_target_pairs={{4,0},{8,4},{12,8},{16,12},{20,16},{24,20},{28,24},{5,1},{9,5},{13... | collective-permute-start | bytes 49160 | tf_op jit(solution)/shard_map/ppermute | solution.py:246
  20.7 48.4 %collective-permute-start = (bf16[4,16,128]{2,1,0:T(8,128)(2,1)S(1)}, bf16[4,16,128]{2,1,0:T(8,128)(2,1)S(1)}, u32[]{:S(2)}, u32[]{:S(2)}) collective-permute-start(bf16[4,16,128]{2,1,0:T(8,128)(2,1)S(1)} %get-tuple-element.37), channel_id=1, source_target_pairs={{0,4},{4,8},{8,12},{12,16},{16,20},{20,24},{24,28},{1,5},{5,9},{9,... | collective-permute-start | bytes 49160 | tf_op jit(solution)/shard_map/ppermute | solution.py:245
  69.2 7.2 %collective-permute-start.2 = (bf16[24,4,128]{2,1,0:T(4,128)(2,1)S(1)}, bf16[24,4,128]{2,1,0:T(4,128)(2,1)S(1)}, u32[]{:S(2)}, u32[]{:S(2)}) collective-permute-start(bf16[24,4,128]{2,1,0:T(4,128)(2,1)S(1)} %get-tuple-element.36), channel_id=1, source_target_pairs={{0,1},{1,2},{2,3},{4,5},{5,6},{6,7},{8,9},{9,10},{10,11},{12,13},{... | collective-permute-start | bytes 73736 | tf_op jit(solution)/shard_map/ppermute | solution.py:245
  72.6 5.7 %collective-permute-start.3 = (bf16[24,4,128]{2,1,0:T(4,128)(2,1)S(1)}, bf16[24,4,128]{2,1,0:T(4,128)(2,1)S(1)}, u32[]{:S(2)}, u32[]{:S(2)}) collective-permute-start(bf16[24,4,128]{2,1,0:T(4,128)(2,1)S(1)} %get-tuple-element.35), channel_id=1, source_target_pairs={{1,0},{2,1},{3,2},{5,4},{6,5},{7,6},{9,8},{10,9},{11,10},{13,12},{... | collective-permute-start | bytes 73736 | tf_op jit(solution)/shard_map/ppermute | solution.py:246
  75.1 1.3 copy-start.1
  81.7 0.9 copy-start.4
  82.6 0.7 copy-start.6
  83.4 0.7 copy-start.8
  84.1 22.1 %copy-start.2 = (bf16[1024,1024]{1,0:T(8,128)(2,1)S(1)}, bf16[1024,1024]{1,0:T(8,128)(2,1)}, u32[]{:S(2)}) copy-start(bf16[1024,1024]{1,0:T(8,128)(2,1)} %copy-done.1) | copy-start | bytes 6291460
  106.2 35.0 %copy-start.5 = (f32[22,2,32,128]{3,2,1,0:T(8,128)S(1)}, f32[22,2,32,128]{3,2,1,0:T(8,128)}, u32[]{:S(2)}) copy-start(f32[22,2,32,128]{3,2,1,0:T(8,128)} %copy-done.4) | copy-start | bytes 2162692
  106.2 35.0 %copy-start.7 = (f32[22,32,128]{2,1,0:T(8,128)S(1)}, f32[22,32,128]{2,1,0:T(8,128)}, u32[]{:S(2)}) copy-start(f32[22,32,128]{2,1,0:T(8,128)} %copy-done.6) | copy-start | bytes 1081348
  106.2 35.0 %copy-start.9 = (f32[22,32,128]{2,1,0:T(8,128)S(1)}, f32[22,32,128]{2,1,0:T(8,128)}, u32[]{:S(2)}) copy-start(f32[22,32,128]{2,1,0:T(8,128)} %copy-done.8) | copy-start | bytes 1081348
  121.3 6.5 %collective-permute-start.4 = (bf16[3,64,128]{2,1,0:T(8,128)(2,1)S(1)}, bf16[3,64,128]{2,1,0:T(8,128)(2,1)S(1)}, u32[]{:S(2)}, u32[]{:S(2)}) collective-permute-start(bf16[3,64,128]{2,1,0:T(8,128)(2,1)S(1)} %get-tuple-element.32), channel_id=1, source_target_pairs={{0,4},{4,8},{8,12},{12,16},{16,20},{20,24},{24,28},{1,5},{5,9},{9,... | collective-permute-start | bytes 147464 | tf_op jit(solution)/shard_map/ppermute | solution.py:245
  123.8 7.4 %collective-permute-start.5 = (bf16[3,64,128]{2,1,0:T(8,128)(2,1)S(1)}, bf16[3,64,128]{2,1,0:T(8,128)(2,1)S(1)}, u32[]{:S(2)}, u32[]{:S(2)}) collective-permute-start(bf16[3,64,128]{2,1,0:T(8,128)(2,1)S(1)} %get-tuple-element.31), channel_id=1, source_target_pairs={{4,0},{8,4},{12,8},{16,12},{20,16},{24,20},{28,24},{5,1},{9,5},{13... | collective-permute-start | bytes 147464 | tf_op jit(solution)/shard_map/ppermute | solution.py:246
  131.6 5.3 %collective-permute-start.6 = (bf16[3,88,128]{2,1,0:T(8,128)(2,1)S(1)}, bf16[3,88,128]{2,1,0:T(8,128)(2,1)S(1)}, u32[]{:S(2)}, u32[]{:S(2)}) collective-permute-start(bf16[3,88,128]{2,1,0:T(8,128)(2,1)S(1)} %bitcast.17), channel_id=1, source_target_pairs={{0,1},{1,2},{2,3},{4,5},{5,6},{6,7},{8,9},{9,10},{10,11},{12,13},{... | collective-permute-start | bytes 202760 | tf_op jit(solution)/shard_map/ppermute | solution.py:336
  135.0 6.2 %collective-permute-start.7 = (bf16[3,88,128]{2,1,0:T(8,128)(2,1)S(1)}, bf16[3,88,128]{2,1,0:T(8,128)(2,1)S(1)}, u32[]{:S(2)}, u32[]{:S(2)}) collective-permute-start(bf16[3,88,128]{2,1,0:T(8,128)(2,1)S(1)} %bitcast.16), channel_id=1, source_target_pairs={{1,0},{2,1},{3,2},{5,4},{6,5},{7,6},{9,8},{10,9},{11,10},{13,12},{... | collective-permute-start | bytes 202760 | tf_op jit(solution)/shard_map/ppermute | solution.py:337

commit v3 on v2

--- a/solution.py
+++ b/solution.py
@@ -13,8 +13,8 @@
 CAP = 64
 OWNERS = 32
 WIDE = 3
-Y0 = 8
-YE = 32
+Y0 = 4
+YE = 24
 
 omega_step = 0.1
 
@@ -36,36 +36,53 @@
     return lax.broadcasted_iota(jnp.int32, shape, dim)
 
 
-def pack_kernel(wall_ref, owner_ref, column_ref, out_ref, slot_ref):
+def pack_kernel(
+    wall_hbm, owner_hbm, column_hbm, out_hbm, wall_ref, owner_ref, column_ref, stage_ref, slot_ref, in_sem, out_sem
+):
     times, count, width = wall_ref.shape
+    pulls = [
+        pltpu.make_async_copy(source, target, in_sem.at[k])
+        for k, (source, target) in enumerate(
+            ((owner_hbm, owner_ref), (column_hbm, column_ref), (wall_hbm, wall_ref))
+        )
+    ]
+    for pull in pulls:
+        pull.start()
+    before = (iota((count, count), 0) < iota((count, count), 1)).astype(F32).astype(BF16)
+    pulls[0].wait()
     owner = owner_ref[...]
     hit = owner == iota((OWNERS, count), 0)
     hit_b = hit.astype(F32).astype(BF16)
-    before = (iota((count, count), 0) < iota((count, count), 1)).astype(F32).astype(BF16)
     earlier = jnp.dot(hit_b, before, preferred_element_type=F32)
     rank = jnp.sum(jnp.where(hit, earlier, 0.0), axis=0, keepdims=True).astype(jnp.int32)
     slot_ref[...] = owner * CAP + rank
+    pulls[1].wait()
     at_rank = (rank == iota((2 * CAP, count), 0) % CAP).astype(F32).astype(BF16)
     marks = jnp.where(hit, (column_ref[...] + 1).astype(F32), 0.0).astype(BF16)
     columns = lax.dot_general(
         marks, at_rank, (((1,), (1,)), ((), ())), preferred_element_type=F32
     )
-    out_ref[:, times * CAP :, :] = jnp.broadcast_to(
-        columns[:, None, :], (OWNERS, out_ref.shape[1] - times * CAP, width)
+    stage_ref[:, times * CAP :, :] = jnp.broadcast_to(
+        columns[:, None, :], (OWNERS, stage_ref.shape[1] - times * CAP, width)
     ).astype(BF16)
-    group = 4
-
-    def step(g, _):
+    pulls[2].wait()
+    group = OWNERS // out_sem.shape[0]
+    pushes = []
+    for g in range(OWNERS // group):
         place = (slot_ref[...] - g * (group * CAP) == iota((group * CAP, count), 0)).astype(F32).astype(BF16)
         rows = jnp.concatenate([wall_ref[t] for t in range(times)], axis=1)
         moved = jnp.dot(place, rows, preferred_element_type=F32).astype(BF16)
         for t in range(times):
-            out_ref[pl.ds(g * group, group), t * CAP : (t + 1) * CAP, :] = moved[
+            stage_ref[g * group : (g + 1) * group, t * CAP : (t + 1) * CAP, :] = moved[
                 :, t * width : (t + 1) * width
             ].reshape(group, CAP, width)
-        return 0
-
-    lax.fori_loop(0, OWNERS // group, step, 0)
+        push = pltpu.make_async_copy(
+            stage_ref.at[pl.ds(g * group, group)], out_hbm.at[pl.ds(g * group, group)], out_sem.at[g]
+        )
+        push.start()
+        pushes.append(push)
+    for push in pushes:
+        push.wait()
 
 
 def sum_kernel(rows_ref, out_ref, *, times, cells):
@@ -119,66 +136,65 @@
     ).astype(BF16)
 
 
-def coef_kernel(omega_ref, conductivity_ref, capacity_ref, ids_ref, fx_ref, fy_ref, fz_ref, a_ref, b_ref, c_ref):
+def coef_kernel(omega_ref, conductivity_ref, capacity_ref, ids_ref, coef_ref, c_ref):
     ext_x, ye, width = ids_ref.shape
-    harms = a_ref.shape[1]
-
-    def conduct_step(i, _):
-        ids = ids_ref[i]
+    harms = omega_ref.shape[0]
+
+    def table(ids, values):
         value = jnp.zeros((ye, width), F32)
         for m in range(NMAT):
-            value = jnp.where(ids == m + 1, conductivity_ref[m], value)
-        c_ref[i] = value
+            value = jnp.where(ids == m + 1, values[m], value)
+        return value
+
+    def conduct_step(i, _):
+        c_ref[i] = table(ids_ref[i], conductivity_ref)
         return 0
 
     lax.fori_loop(0, ext_x, conduct_step, 0)
 
     def face(a, b):
-        return jnp.where(b > 0, 2.0 * a * b / jnp.where(b > 0, a + b, 1.0), a)
+        b = jnp.where(b > 0, b, a)
+        both = a + b
+        return 2.0 * a * b / jnp.where(both > 0, both, 1.0)
 
     lane = iota((ye, width), 1)
 
-    def fx_step(i, _):
-        fx_ref[i] = face(c_ref[i], c_ref[i + 1])
-        return 0
-
-    lax.fori_loop(0, ext_x - 1, fx_step, 0)
-
-    def step(i, _):
+    def step(i, prev_x):
         c = c_ref[i + 1]
-        next_x = fx_ref[i + 1]
-        prev_x = face(c, c_ref[i])
+        after = c_ref[i + 2]
+        next_x = face(c, after)
         next_y = face(c, pltpu.roll(c, ye - 1, 0))
+        next_z = face(c, jnp.where(lane == width - 1, 0.0, pltpu.roll(c, width - 1, 1)))
         prev_y = face(c, pltpu.roll(c, 1, 0))
-        next_z = face(c, jnp.where(lane == width - 1, 0.0, pltpu.roll(c, width - 1, 1)))
-        prev_z = face(c, jnp.where(lane == 0, 0.0, pltpu.roll(c, 1, 1)))
-        real_den = next_x + prev_x + next_y + prev_y + next_z + prev_z
-        fy_ref[i] = next_y
-        fz_ref[i] = jnp.where(lane == width - 1, 0.0, next_z)
+        prev_z = jnp.where(lane == 0, c, pltpu.roll(next_z, 1, 1))
+        real_den = next_x + jnp.where(c_ref[i] > 0, prev_x, c) + next_y + prev_y + next_z + prev_z
+        coef_ref[i, 0] = next_x
+        coef_ref[i, 1] = next_y
+        coef_ref[i, 2] = jnp.where(lane == width - 1, 0.0, next_z)
         ids = ids_ref[i + 1]
-        heat = jnp.zeros((ye, width), F32)
-        for m in range(NMAT):
-            heat = jnp.where(ids == m + 1, capacity_ref[m], heat)
+        heat = table(ids, capacity_ref)
         inside = ids > 0
         for h in range(harms):
             imag_den = omega_ref[h] * heat
             modulus = real_den * real_den + imag_den * imag_den
-            modulus = jnp.where(inside, modulus, 1.0)
-            a_ref[i, h] = jnp.where(inside, real_den / modulus, 0.0)
-            b_ref[i, h] = jnp.where(inside, imag_den / modulus, 0.0)
-        return 0
-
-    lax.fori_loop(0, ext_x - 2, step, 0)
-
-
-def solve_kernel(mid_ref, xlo_ref, xhi_ref, ylo_ref, yhi_ref, fx_ref, fy_ref, fz_ref, a_ref, b_ref, out_ref, s_ref, f_ref, g_ref):
+            inverse = jnp.where(inside, 1.0 / jnp.where(inside, modulus, 1.0), 0.0)
+            coef_ref[i, 3 + 2 * h] = real_den * inverse
+            coef_ref[i, 4 + 2 * h] = imag_den * inverse
+        return next_x
+
+    lax.fori_loop(0, ext_x - 2, step, face(c_ref[0], c_ref[1]))
+
+
+def solve_kernel(mid_ref, xlo_ref, xhi_ref, ylo_ref, yhi_ref, coef_ref, out_ref, s_ref, f_ref, g_ref):
     size_x = mid_ref.shape[0]
     wide = xlo_ref.shape[0]
     ext_x, comps, ye, width = s_ref.shape
     harms = comps // 2
     side = mid_ref.shape[1] // comps
 
-    s_ref[...] = jnp.zeros(s_ref.shape, F32)
+    edge = jnp.zeros((ext_x, comps, Y0 - wide, width), F32)
+    s_ref[:, :, : Y0 - wide, :] = edge
+    s_ref[:, :, ye - Y0 + wide :, :] = edge
     for ref, start in ((xlo_ref, 0), (mid_ref, wide), (xhi_ref, wide + size_x)):
         for c in range(comps):
             s_ref[start : start + ref.shape[0], c, Y0 : Y0 + side, :] = ref[
@@ -189,52 +205,53 @@
             s_ref[:, :, start, :] = ref[k].astype(F32).reshape(ext_x, comps, width)
 
     def quotient(i, h, real_num, imag_num):
-        a = a_ref[i, h]
-        b = b_ref[i, h]
+        a = coef_ref[i, 3 + 2 * h]
+        b = coef_ref[i, 4 + 2 * h]
         return real_num * a + imag_num * b, imag_num * a - real_num * b
 
-    def first(i, _):
+    def pairs(begin, end, row):
+        def step(k, _):
+            row(begin + 2 * k)
+            row(begin + 2 * k + 1)
+            return 0
+
+        lax.fori_loop(0, (end - begin) // 2, step, 0)
+
+    def first(i):
         for h in range(harms):
-            real_out, imag_out = quotient(i, h, s_ref[i, 2 * h], s_ref[i, 2 * h + 1])
-            f_ref[i, 2 * h] = real_out
-            f_ref[i, 2 * h + 1] = imag_out
-        return 0
-
-    lax.fori_loop(0, ext_x, first, 0)
+            f_ref[i, 2 * h], f_ref[i, 2 * h + 1] = quotient(i, h, s_ref[i, 2 * h], s_ref[i, 2 * h + 1])
+
+    pairs(0, ext_x, first)
 
     def numerator(src, i, c):
         here = src[i, c]
-        fy = fy_ref[i]
-        fz = fz_ref[i]
-        total = s_ref[i, c] + fx_ref[i + 1] * src[i + 1, c] + fx_ref[i] * src[i - 1, c]
+        fy = coef_ref[i, 1]
+        fz = coef_ref[i, 2]
+        total = s_ref[i, c] + coef_ref[i, 0] * src[i + 1, c] + coef_ref[i - 1, 0] * src[i - 1, c]
         total = total + fy * pltpu.roll(here, ye - 1, 0) + pltpu.roll(fy * here, 1, 0)
         return total + fz * pltpu.roll(here, width - 1, 1) + pltpu.roll(fz * here, 1, 1)
 
     def sweep(src, dst, margin):
-        def step(i, _):
+        def row(i):
             for h in range(harms):
-                real_out, imag_out = quotient(
+                dst[i, 2 * h], dst[i, 2 * h + 1] = quotient(
                     i, h, numerator(src, i, 2 * h), numerator(src, i, 2 * h + 1)
                 )
-                dst[i, 2 * h] = real_out
-                dst[i, 2 * h + 1] = imag_out
-            return 0
-
-        lax.fori_loop(margin, ext_x - margin, step, 0)
+
+        pairs(margin, ext_x - margin, row)
 
     sweep(f_ref, g_ref, 1)
     sweep(g_ref, f_ref, 2)
 
-    def last(i, _):
+    def last(i):
         for h in range(harms):
             real_out, imag_out = quotient(
                 i, h, numerator(f_ref, i, 2 * h), numerator(f_ref, i, 2 * h + 1)
             )
             out_ref[h, 0, i - wide] = real_out[Y0 : Y0 + side]
             out_ref[h, 1, i - wide] = imag_out[Y0 : Y0 + side]
-        return 0
-
-    lax.fori_loop(wide, wide + size_x, last, 0)
+
+    pairs(wide, wide + size_x, last)
 
 
 def swap(block, axis, dim, width):
@@ -245,6 +262,16 @@
     low = lax.ppermute(lax.slice_in_dim(block, size - width, size, axis=dim), axis, forward)
     high = lax.ppermute(lax.slice_in_dim(block, 0, width, axis=dim), axis, backward)
     return low, high
+
+
+def diagonal(dx, dy):
+    count_x, count_y = lax.axis_size("sx"), lax.axis_size("sy")
+    return [
+        (x * count_y + y, (x + dx) * count_y + y + dy)
+        for x in range(count_x)
+        for y in range(count_y)
+        if 0 <= x + dx < count_x and 0 <= y + dy < count_y
+    ]
 
 
 def body(wall_temp, owner_map, stencil_column, material, conductivity, capacity):
@@ -258,36 +285,58 @@
     vmem = pl.BlockSpec(memory_space=pltpu.VMEM)
     smem = pl.BlockSpec(memory_space=pltpu.SMEM)
 
+    hbm = pl.BlockSpec(memory_space=pltpu.HBM)
     packed = pl.pallas_call(
         pack_kernel,
-        out_shape=jax.ShapeDtypeStruct((OWNERS, times * CAP + 16, width), BF16),
-        in_specs=[vmem] * 3,
-        out_specs=vmem,
-        scratch_shapes=[pltpu.VMEM((1, count), jnp.int32)],
+        out_shape=pltpu.HBM((OWNERS, times * CAP + 8, width), BF16),
+        in_specs=[hbm] * 3,
+        out_specs=hbm,
+        scratch_shapes=[
+            pltpu.VMEM((times, count, width), BF16),
+            pltpu.VMEM((1, count), jnp.int32),
+            pltpu.VMEM((1, count), jnp.int32),
+            pltpu.VMEM((OWNERS, times * CAP + 8, width), BF16),
+            pltpu.VMEM((1, count), jnp.int32),
+            pltpu.SemaphoreType.DMA((3,)),
+            pltpu.SemaphoreType.DMA((8,)),
+        ],
         compiler_params=params,
         name="pack",
-    )(wall_temp, owner_map.reshape(1, count), stencil_column.reshape(1, count))
+    )(
+        *(
+            pltpu.with_memory_space_constraint(operand, pltpu.HBM)
+            for operand in (wall_temp, owner_map.reshape(1, count), stencil_column.reshape(1, count))
+        )
+    )
     received = lax.all_to_all(packed, ("sx", "sy"), split_axis=0, concat_axis=0, tiled=True)
 
     ids = (material + 1).astype(BF16)
-    low, high = swap(ids, "sx", 0, WIDE + 1)
-    ids = jnp.concatenate([low, ids, high], axis=0)
-    low, high = swap(ids, "sy", 1, WIDE + 1)
-    rim = jnp.zeros((ids.shape[0], Y0 - WIDE - 1, width), BF16)
-    ids = jnp.concatenate([rim, low, ids, high, rim], axis=1).astype(jnp.int32)
+    west, east = swap(ids, "sx", 0, Y0)
+    south, north = swap(ids, "sy", 1, Y0)
+    corner = {}
+    for dx in (1, -1):
+        for dy in (1, -1):
+            part = ids[size_x - Y0 :] if dx > 0 else ids[:Y0]
+            part = part[:, size_y - Y0 :] if dy > 0 else part[:, :Y0]
+            corner[dx, dy] = lax.ppermute(part, ("sx", "sy"), diagonal(dx, dy))
+    received, west, east, south, north, corner = lax.optimization_barrier(
+        (received, west, east, south, north, corner)
+    )
+    ids = jnp.concatenate(
+        [
+            jnp.concatenate([corner[1, 1], west, corner[1, -1]], axis=1),
+            jnp.concatenate([south, ids, north], axis=1),
+            jnp.concatenate([corner[-1, 1], east, corner[-1, -1]], axis=1),
+        ],
+        axis=0,
+    ).astype(jnp.int32)
     harm_index = lax.axis_index("tm") * harms + jnp.arange(harms, dtype=jnp.int32)
     omega = omega_step * harm_index.astype(F32)
-    fx, fy, fz, quot_a, quot_b = pl.pallas_call(
+    coef = pl.pallas_call(
         coef_kernel,
-        out_shape=[
-            jax.ShapeDtypeStruct((ext_x + 1, YE, width), F32),
-            jax.ShapeDtypeStruct((ext_x, YE, width), F32),
-            jax.ShapeDtypeStruct((ext_x, YE, width), F32),
-            jax.ShapeDtypeStruct((ext_x, harms, YE, width), F32),
-            jax.ShapeDtypeStruct((ext_x, harms, YE, width), F32),
-        ],
+        out_shape=jax.ShapeDtypeStruct((ext_x, 3 + 2 * harms, YE, width), F32),
         in_specs=[smem, smem, smem, vmem],
-        out_specs=[vmem] * 5,
+        out_specs=vmem,
         scratch_shapes=[pltpu.VMEM((ext_x + 2, YE, width), F32)],
         compiler_params=params,
         name="coef",
@@ -301,9 +350,7 @@
         compiler_params=params,
         name="weights",
     )(dft_table())
-    received, fx, fy, fz, quot_a, quot_b, weights = lax.optimization_barrier(
-        (received, fx, fy, fz, quot_a, quot_b, weights)
-    )
+    received, weights = lax.optimization_barrier((received, weights))
 
     cells = size_x * size_y
     sums = pl.pallas_call(
@@ -315,6 +362,7 @@
         name="cell_sum",
     )(received)
     gathered = lax.all_to_all(sums, "tm", split_axis=0, concat_axis=0, tiled=True)
+    gathered, coef = lax.optimization_barrier((gathered, coef))
     harmonic = pl.pallas_call(
         dft_kernel,
         out_shape=jax.ShapeDtypeStruct((TIME * size_y, width), BF16),
@@ -338,12 +386,12 @@
     field = pl.pallas_call(
         solve_kernel,
         out_shape=jax.ShapeDtypeStruct((harms, 2, size_x, size_y, width), F32),
-        in_specs=[vmem] * 10,
+        in_specs=[vmem] * 6,
         out_specs=vmem,
         scratch_shapes=[pltpu.VMEM((ext_x, comps, YE, width), F32)] * 3,
         compiler_params=params,
         name="solve",
-    )(source, xlo, xhi, ylo, yhi, fx, fy, fz, quot_a, quot_b)
+    )(source, xlo, xhi, ylo, yhi, coef)
     return field
 
 

time: 149 us -> 142 us (0.953)
  starting transfers between devices: 32.3 us -> 55.3 us
  blocking collectives: 35.8 us -> 14.4 us
  local copies, waits for them, and re-layouts: 8.05 us -> 2.83 us
  waiting for transfers between devices: 54.6 us -> 51.5 us
    ppermute x3, waiting for transfers between devices: 49.1 us -> 3.14 us  [swap(): lax.ppermute(lax.slice_in_dim(block, 0, width, axis=dim), axis, backward)]
    ppermute x0 -> x4, waiting for transfers between devices: none -> 37.4 us  [body(): corner[dx, dy] = lax.ppermute(part, ('sx', 'sy'), diagonal(dx, dy))]
    all_to_all x1 -> x0, blocking collectives: 21.4 us -> none  [body(): lax.all_to_all(sums, 'tm', split_axis=0, concat_axis=0, tiled=True)]
    ppermute x0 -> x4, starting transfers between devices: none -> 11 us  [body(): corner[dx, dy] = lax.ppermute(part, ('sx', 'sy'), diagonal(dx, dy))]
    all_to_all x0 -> x1, starting transfers between devices: none -> 10.5 us  [body(): lax.all_to_all(sums, 'tm', split_axis=0, concat_axis=0, tiled=True)]
    all_to_all x0 -> x1, waiting for transfers between devices: none -> 5.45 us  [body(): lax.all_to_all(sums, 'tm', split_axis=0, concat_axis=0, tiled=True)]
    unnamed x32 -> x16, local copies, waits for them, and re-layouts: 7.74 us -> 2.65 us
    pallas_call x1, Pallas kernels: 6.97 us -> 4.66 us  [body(): pl.pallas_call(solve_kernel, out_shape=jax.ShapeDtypeStruct((harms, 2, si...]
  transfers between devices with their start and end apart: 9 -> 14, of which waited for: 6 -> 6; matrix products, arithmetic and copies ran while one was open for 0% -> 0% of each run, Pallas kernels for 3% -> 4%
where the time goes in v3:
time: 142 us
  starting transfers between devices  55.3 us (39%)
  waiting for transfers between devices  51.5 us (36%)
  Pallas kernels  16.8 us (12%)
  blocking collectives  14.4 us (10%)
  local copies, waits for them, and re-layouts  2.83 us (2%)
    ppermute x4, waiting for transfers between devices, body(): corner[dx, dy] = lax.ppermute(part, ('sx', 'sy'), diagonal(dx, dy))  37.4 us
    all_to_all x1, blocking collectives, body(): lax.all_to_all(harmonic, 'tm', split_axis=0, concat_axis=0, tiled=True)  14.4 us
    ppermute x4, starting transfers between devices, body(): corner[dx, dy] = lax.ppermute(part, ('sx', 'sy'), diagonal(dx, dy))  11 us
    all_to_all x1, starting transfers between devices, body(): lax.all_to_all(sums, 'tm', split_axis=0, concat_axis=0, tiled=True)  10.5 us
    all_to_all x1, starting transfers between devices, body(): lax.all_to_all(packed, ('sx', 'sy'), split_axis=0, concat_axis=0, tiled=T...  10.1 us
    ppermute x3, starting transfers between devices, swap(): lax.ppermute(lax.slice_in_dim(block, size - width, size, axis=dim), axis,...  9.86 us
    ppermute x3, starting transfers between devices, swap(): lax.ppermute(lax.slice_in_dim(block, 0, width, axis=dim), axis, backward)  7.13 us
    all_to_all x1, waiting for transfers between devices, body(): lax.all_to_all(sums, 'tm', split_axis=0, concat_axis=0, tiled=True)  5.45 us
  transfers between devices with their start and end apart: 14, of which 6 were waited for; matrix products, arithmetic and copies ran while one was open for 0% of the time, Pallas kernels for 4%

profile of v3, /device:TPU:24, one launch (start us, length us, event | category | flops | bytes accessed | tf_op | source)
XLA Modules:
  0.0 141.5 jit_solution(11550211914786369846)
XLA Ops:
  0.0 4.5 %pack.1 = bf16[32,264,128]{2,1,0:T(8,128)(2,1)} custom-call(bf16[4,1024,128]{2,1,0:T(8,128)(2,1)} %wall_hbm.1, s32[1,1024]{1,0:T(1,128)} %bitcast.16, s32[1,1024]{1,0:T(1,128)} %bitcast.17), custom_call_target="tpu_custom_call" | custom-call | tf_op jit(solution)/shard_map/pack/pallas_call | solution.py:289
  4.5 10.1 %all-to-all-start = ((bf16[32,264,128]{2,1,0:T(8,128)(2,1)}), bf16[32,264,128]{2,1,0:T(8,128)(2,1)S(1)}, u32[]{:S(2)}, u32[]{:S(2)}) async-start(bf16[32,264,128]{2,1,0:T(8,128)(2,1)} %pack.1), calls=%async_computation | async-start | bytes 4325376 | tf_op jit(solution)/shard_map/all_to_all | solution.py:311
  14.7 4.6 %collective-permute-start = (bf16[4,16,128]{2,1,0:T(8,128)(2,1)S(1)}, bf16[4,16,128]{2,1,0:T(8,128)(2,1)S(1)}, u32[]{:S(2)}, u32[]{:S(2)}) collective-permute-start(bf16[4,16,128]{2,1,0:T(8,128)(2,1)S(1)} %get-tuple-element.44), channel_id=1, source_target_pairs={{0,4},{4,8},{8,12},{12,16},{16,20},{20,24},{24,28},{1,5},{5,9},{9,... | collective-permute-start | bytes 49160 | tf_op jit(solution)/shard_map/ppermute | solution.py:262
  19.3 1.9 %collective-permute-start.1 = (bf16[4,16,128]{2,1,0:T(8,128)(2,1)S(1)}, bf16[4,16,128]{2,1,0:T(8,128)(2,1)S(1)}, u32[]{:S(2)}, u32[]{:S(2)}) collective-permute-start(bf16[4,16,128]{2,1,0:T(8,128)(2,1)S(1)} %get-tuple-element.43), channel_id=1, source_target_pairs={{4,0},{8,4},{12,8},{16,12},{20,16},{24,20},{28,24},{5,1},{9,5},{13... | collective-permute-start | bytes 49160 | tf_op jit(solution)/shard_map/ppermute | solution.py:263
  21.2 1.3 collective-permute-start.4
  22.5 3.9 %collective-permute-start.5 = (bf16[4,4,128]{2,1,0:T(4,128)(2,1)S(1)}, bf16[4,4,128]{2,1,0:T(4,128)(2,1)S(1)}, u32[]{:S(2)}, u32[]{:S(2)}) collective-permute-start(bf16[4,4,128]{2,1,0:T(4,128)(2,1)S(1)} %get-tuple-element.39), channel_id=1, source_target_pairs={{4,1},{5,2},{6,3},{8,5},{9,6},{10,7},{12,9},{13,10},{14,11},{16,13... | collective-permute-start | bytes 12296 | tf_op jit(solution)/shard_map/ppermute | solution.py:321
  26.4 1.3 collective-permute-start.6
  27.8 37.4 %collective-permute-done.4 = bf16[4,4,128]{2,1,0:T(4,128)(2,1)S(1)} collective-permute-done((bf16[4,4,128]{2,1,0:T(4,128)(2,1)S(1)}, bf16[4,4,128]{2,1,0:T(4,128)(2,1)S(1)}, u32[]{:S(2)}, u32[]{:S(2)}) %collective-permute-start.4) | collective-permute-done | bytes 4128 | tf_op jit(solution)/shard_map/ppermute | solution.py:321
  65.3 3.4 %collective-permute-start.2 = (bf16[16,4,128]{2,1,0:T(4,128)(2,1)S(1)}, bf16[16,4,128]{2,1,0:T(4,128)(2,1)S(1)}, u32[]{:S(2)}, u32[]{:S(2)}) collective-permute-start(bf16[16,4,128]{2,1,0:T(4,128)(2,1)S(1)} %get-tuple-element.42), channel_id=1, source_target_pairs={{0,1},{1,2},{2,3},{4,5},{5,6},{6,7},{8,9},{9,10},{10,11},{12,13},{... | collective-permute-start | bytes 49160 | tf_op jit(solution)/shard_map/ppermute | solution.py:262
  68.6 1.3 collective-permute-start.3
  69.9 4.6 %collective-permute-start.7 = (bf16[4,4,128]{2,1,0:T(4,128)(2,1)S(1)}, bf16[4,4,128]{2,1,0:T(4,128)(2,1)S(1)}, u32[]{:S(2)}, u32[]{:S(2)}) collective-permute-start(bf16[4,4,128]{2,1,0:T(4,128)(2,1)S(1)} %get-tuple-element.37), channel_id=1, source_target_pairs={{0,5},{1,6},{2,7},{4,9},{5,10},{6,11},{8,13},{9,14},{10,15},{12,17... | collective-permute-start | bytes 12296 | tf_op jit(solution)/shard_map/ppermute | solution.py:321
  75.7 1.3 copy-done
  77.1 1.4 cell_sum.1
  78.5 10.5 %all-to-all-start.1 = ((bf16[16,64,128]{2,1,0:T(8,128)(2,1)}), bf16[16,64,128]{2,1,0:T(8,128)(2,1)S(1)}, u32[]{:S(2)}, u32[]{:S(2)}) async-start(bf16[16,64,128]{2,1,0:T(8,128)(2,1)} %cell_sum.1), calls=%async_computation.1 | async-start | bytes 524288 | tf_op jit(solution)/shard_map/all_to_all | solution.py:364
  89.2 4.3 %coef.1.coef_ref = f32[22,7,24,128]{3,2,1,0:T(8,128)S(1)} custom-call(f32[2]{0:T(128)S(1)} %convert_multiply_fusion.omega_ref, f32[4]{0:T(128)S(1)} %copy-done.4, f32[4]{0:T(128)S(1)} %copy-done.5, s32[24,24,128]{2,1,0:T(8,128)S(1)} %maximum_convert_fusion.ids_ref), custom_call_target="tpu_custom_call" | custom-call | tf_op jit(solution)/shard_map/coef/pallas_call | solution.py:335
  94.8 5.4 %all-to-all-done.1 = bf16[16,64,128]{2,1,0:T(8,128)(2,1)S(1)} async-done(((bf16[16,64,128]{2,1,0:T(8,128)(2,1)}), bf16[16,64,128]{2,1,0:T(8,128)(2,1)S(1)}, u32[]{:S(2)}, u32[]{:S(2)}) %all-to-all-start.1) | async-done | bytes 262176 | tf_op jit(solution)/shard_map/all_to_all | solution.py:364
  101.0 14.4 %all_to_all.15.mid_ref = bf16[16,64,128]{2,1,0:T(8,128)(2,1)S(1)} all-to-all(bf16[16,64,128]{2,1,0:T(8,128)(2,1)S(1)} %bitcast.11), channel_id=1, replica_groups=mesh['tm'=16,'sx'=8,'sy'=4] {'tm'}, dimensions={0} | all-to-all | bytes 524288 | tf_op jit(solution)/shard_map/all_to_all | solution.py:375
  115.4 1.9 %collective-permute-start.8 = (bf16[3,64,128]{2,1,0:T(8,128)(2,1)S(1)}, bf16[3,64,128]{2,1,0:T(8,128)(2,1)S(1)}, u32[]{:S(2)}, u32[]{:S(2)}) collective-permute-start(bf16[3,64,128]{2,1,0:T(8,128)(2,1)S(1)} %get-tuple-element.34), channel_id=1, source_target_pairs={{0,4},{4,8},{8,12},{12,16},{16,20},{20,24},{24,28},{1,5},{5,9},{9,... | collective-permute-start | bytes 147464 | tf_op jit(solution)/shard_map/ppermute | solution.py:262
  117.3 3.9 %collective-permute-start.9 = (bf16[3,64,128]{2,1,0:T(8,128)(2,1)S(1)}, bf16[3,64,128]{2,1,0:T(8,128)(2,1)S(1)}, u32[]{:S(2)}, u32[]{:S(2)}) collective-permute-start(bf16[3,64,128]{2,1,0:T(8,128)(2,1)S(1)} %get-tuple-element.33), channel_id=1, source_target_pairs={{4,0},{8,4},{12,8},{16,12},{20,16},{24,20},{28,24},{5,1},{9,5},{13... | collective-permute-start | bytes 147464 | tf_op jit(solution)/shard_map/ppermute | solution.py:263
  121.9 3.1 %collective-permute-done.9.xhi_ref = bf16[3,64,128]{2,1,0:T(8,128)(2,1)S(1)} collective-permute-done((bf16[3,64,128]{2,1,0:T(8,128)(2,1)S(1)}, bf16[3,64,128]{2,1,0:T(8,128)(2,1)S(1)}, u32[]{:S(2)}, u32[]{:S(2)}) %collective-permute-start.9) | collective-permute-done | bytes 49184 | tf_op jit(solution)/shard_map/ppermute | solution.py:263
  125.4 5.3 %collective-permute-start.10 = (bf16[3,88,128]{2,1,0:T(8,128)(2,1)S(1)}, bf16[3,88,128]{2,1,0:T(8,128)(2,1)S(1)}, u32[]{:S(2)}, u32[]{:S(2)}) collective-permute-start(bf16[3,88,128]{2,1,0:T(8,128)(2,1)S(1)} %bitcast.15), channel_id=1, source_target_pairs={{0,1},{1,2},{2,3},{4,5},{5,6},{6,7},{8,9},{9,10},{10,11},{12,13},{... | collective-permute-start | bytes 202760 | tf_op jit(solution)/shard_map/ppermute | solution.py:384
  130.7 1.3 collective-permute-start.11
  132.6 4.3 %collective-permute-done.11.yhi_ref = bf16[3,88,128]{2,1,0:T(8,128)(2,1)S(1)} collective-permute-done((bf16[3,88,128]{2,1,0:T(8,128)(2,1)S(1)}, bf16[3,88,128]{2,1,0:T(8,128)(2,1)S(1)}, u32[]{:S(2)}, u32[]{:S(2)}) %collective-permute-start.11) | collective-permute-done | bytes 67616 | tf_op jit(solution)/shard_map/ppermute | solution.py:385
  136.9 4.7 %solve.1 = f32[2,2,16,16,128]{4,3,2,1,0:T(8,128)} custom-call(bf16[16,64,128]{2,1,0:T(8,128)(2,1)S(1)} %all_to_all.15.mid_ref, bf16[3,64,128]{2,1,0:T(8,128)(2,1)S(1)} %collective-permute-done.8.xlo_ref, bf16[3,64,128]{2,1,0:T(8,128)(2,1)S(1)} %collective-permute-done.9.xhi_ref, bf16[3,88,128]{2,1,0:T(8,128)(2,1)S(1)} %collective-permute-done.10.ylo_ref, ...), custom_call_target="tpu_custom_call" | custom-call | tf_op jit(solution)/shard_map/solve/pallas_call | solution.py:386
  (41 shorter events, 5.0 us)
Async XLA Ops:
  4.5 10.1 %copy-start.6 = (s32[16,16,128]{2,1,0:T(8,128)S(1)}, s32[16,16,128]{2,1,0:T(8,128)}, u32[]{:S(2)}) copy-start(s32[16,16,128]{2,1,0:T(8,128)} %param.9) | copy-start | bytes 393220
  4.5 72.6 %all-to-all-start = ((bf16[32,264,128]{2,1,0:T(8,128)(2,1)}), bf16[32,264,128]{2,1,0:T(8,128)(2,1)S(1)}, u32[]{:S(2)}, u32[]{:S(2)}) async-start(bf16[32,264,128]{2,1,0:T(8,128)(2,1)} %pack.1), calls=%async_computation | async-start | bytes 4325376 | tf_op jit(solution)/shard_map/all_to_all | solution.py:311
  14.7 62.4 %collective-permute-start = (bf16[4,16,128]{2,1,0:T(8,128)(2,1)S(1)}, bf16[4,16,128]{2,1,0:T(8,128)(2,1)S(1)}, u32[]{:S(2)}, u32[]{:S(2)}) collective-permute-start(bf16[4,16,128]{2,1,0:T(8,128)(2,1)S(1)} %get-tuple-element.44), channel_id=1, source_target_pairs={{0,4},{4,8},{8,12},{12,16},{16,20},{20,24},{24,28},{1,5},{5,9},{9,... | collective-permute-start | bytes 49160 | tf_op jit(solution)/shard_map/ppermute | solution.py:262
  19.3 57.8 %collective-permute-start.1 = (bf16[4,16,128]{2,1,0:T(8,128)(2,1)S(1)}, bf16[4,16,128]{2,1,0:T(8,128)(2,1)S(1)}, u32[]{:S(2)}, u32[]{:S(2)}) collective-permute-start(bf16[4,16,128]{2,1,0:T(8,128)(2,1)S(1)} %get-tuple-element.43), channel_id=1, source_target_pairs={{4,0},{8,4},{12,8},{16,12},{20,16},{24,20},{28,24},{5,1},{9,5},{13... | collective-permute-start | bytes 49160 | tf_op jit(solution)/shard_map/ppermute | solution.py:263
  21.2 44.0 %collective-permute-start.4 = (bf16[4,4,128]{2,1,0:T(4,128)(2,1)S(1)}, bf16[4,4,128]{2,1,0:T(4,128)(2,1)S(1)}, u32[]{:S(2)}, u32[]{:S(2)}) collective-permute-start(bf16[4,4,128]{2,1,0:T(4,128)(2,1)S(1)} %get-tuple-element.40), channel_id=1, source_target_pairs={{5,0},{6,1},{7,2},{9,4},{10,5},{11,6},{13,8},{14,9},{15,10},{17,12... | collective-permute-start | bytes 12296 | tf_op jit(solution)/shard_map/ppermute | solution.py:321
  22.5 46.1 %collective-permute-start.5 = (bf16[4,4,128]{2,1,0:T(4,128)(2,1)S(1)}, bf16[4,4,128]{2,1,0:T(4,128)(2,1)S(1)}, u32[]{:S(2)}, u32[]{:S(2)}) collective-permute-start(bf16[4,4,128]{2,1,0:T(4,128)(2,1)S(1)} %get-tuple-element.39), channel_id=1, source_target_pairs={{4,1},{5,2},{6,3},{8,5},{9,6},{10,7},{12,9},{13,10},{14,11},{16,13... | collective-permute-start | bytes 12296 | tf_op jit(solution)/shard_map/ppermute | solution.py:321
  26.4 43.5 %collective-permute-start.6 = (bf16[4,4,128]{2,1,0:T(4,128)(2,1)S(1)}, bf16[4,4,128]{2,1,0:T(4,128)(2,1)S(1)}, u32[]{:S(2)}, u32[]{:S(2)}) collective-permute-start(bf16[4,4,128]{2,1,0:T(4,128)(2,1)S(1)} %get-tuple-element.38), channel_id=1, source_target_pairs={{1,4},{2,5},{3,6},{5,8},{6,9},{7,10},{9,12},{10,13},{11,14},{13,16... | collective-permute-start | bytes 12296 | tf_op jit(solution)/shard_map/ppermute | solution.py:321
  65.3 11.8 %collective-permute-start.2 = (bf16[16,4,128]{2,1,0:T(4,128)(2,1)S(1)}, bf16[16,4,128]{2,1,0:T(4,128)(2,1)S(1)}, u32[]{:S(2)}, u32[]{:S(2)}) collective-permute-start(bf16[16,4,128]{2,1,0:T(4,128)(2,1)S(1)} %get-tuple-element.42), channel_id=1, source_target_pairs={{0,1},{1,2},{2,3},{4,5},{5,6},{6,7},{8,9},{9,10},{10,11},{12,13},{... | collective-permute-start | bytes 49160 | tf_op jit(solution)/shard_map/ppermute | solution.py:262
  68.6 8.5 %collective-permute-start.3 = (bf16[16,4,128]{2,1,0:T(4,128)(2,1)S(1)}, bf16[16,4,128]{2,1,0:T(4,128)(2,1)S(1)}, u32[]{:S(2)}, u32[]{:S(2)}) collective-permute-start(bf16[16,4,128]{2,1,0:T(4,128)(2,1)S(1)} %get-tuple-element.41), channel_id=1, source_target_pairs={{1,0},{2,1},{3,2},{5,4},{6,5},{7,6},{9,8},{10,9},{11,10},{13,12},{... | collective-permute-start | bytes 49160 | tf_op jit(solution)/shard_map/ppermute | solution.py:263
  69.9 7.1 %collective-permute-start.7 = (bf16[4,4,128]{2,1,0:T(4,128)(2,1)S(1)}, bf16[4,4,128]{2,1,0:T(4,128)(2,1)S(1)}, u32[]{:S(2)}, u32[]{:S(2)}) collective-permute-start(bf16[4,4,128]{2,1,0:T(4,128)(2,1)S(1)} %get-tuple-element.37), channel_id=1, source_target_pairs={{0,5},{1,6},{2,7},{4,9},{5,10},{6,11},{8,13},{9,14},{10,15},{12,17... | collective-permute-start | bytes 12296 | tf_op jit(solution)/shard_map/ppermute | solution.py:321
  75.7 1.3 copy-start
  77.0 12.1 %copy-start.4 = (f32[4]{0:T(128)S(1)}, f32[4]{0:T(128)}, u32[]{:S(2)}) copy-start(f32[4]{0:T(128)} %conductivity_ref.1) | copy-start | bytes 52
  77.0 12.1 %copy-start.5 = (f32[4]{0:T(128)S(1)}, f32[4]{0:T(128)}, u32[]{:S(2)}) copy-start(f32[4]{0:T(128)} %capacity_ref.1) | copy-start | bytes 52
  78.5 21.7 %copy-start.1 = (bf16[1024,1024]{1,0:T(8,128)(2,1)S(1)}, bf16[1024,1024]{1,0:T(8,128)(2,1)}, u32[]{:S(2)}) copy-start(bf16[1024,1024]{1,0:T(8,128)(2,1)} %copy-done) | copy-start | bytes 6291460
  78.5 21.7 %all-to-all-start.1 = ((bf16[16,64,128]{2,1,0:T(8,128)(2,1)}), bf16[16,64,128]{2,1,0:T(8,128)(2,1)S(1)}, u32[]{:S(2)}, u32[]{:S(2)}) async-start(bf16[16,64,128]{2,1,0:T(8,128)(2,1)} %cell_sum.1), calls=%async_computation.1 | async-start | bytes 524288 | tf_op jit(solution)/shard_map/all_to_all | solution.py:364
  93.5 1.3 copy-start.2
  100.3 36.6 %copy-start.3 = (f32[22,7,24,128]{3,2,1,0:T(8,128)S(1)}, f32[22,7,24,128]{3,2,1,0:T(8,128)}, u32[]{:S(2)}) copy-start(f32[22,7,24,128]{3,2,1,0:T(8,128)} %copy-done.2) | copy-start | bytes 5677060
  115.4 6.5 %collective-permute-start.8 = (bf16[3,64,128]{2,1,0:T(8,128)(2,1)S(1)}, bf16[3,64,128]{2,1,0:T(8,128)(2,1)S(1)}, u32[]{:S(2)}, u32[]{:S(2)}) collective-permute-start(bf16[3,64,128]{2,1,0:T(8,128)(2,1)S(1)} %get-tuple-element.34), channel_id=1, source_target_pairs={{0,4},{4,8},{8,12},{12,16},{16,20},{20,24},{24,28},{1,5},{5,9},{9,... | collective-permute-start | bytes 147464 | tf_op jit(solution)/shard_map/ppermute | solution.py:262
  117.3 7.7 %collective-permute-start.9 = (bf16[3,64,128]{2,1,0:T(8,128)(2,1)S(1)}, bf16[3,64,128]{2,1,0:T(8,128)(2,1)S(1)}, u32[]{:S(2)}, u32[]{:S(2)}) collective-permute-start(bf16[3,64,128]{2,1,0:T(8,128)(2,1)S(1)} %get-tuple-element.33), channel_id=1, source_target_pairs={{4,0},{8,4},{12,8},{16,12},{20,16},{24,20},{28,24},{5,1},{9,5},{13... | collective-permute-start | bytes 147464 | tf_op jit(solution)/shard_map/ppermute | solution.py:263
  125.4 7.2 %collective-permute-start.10 = (bf16[3,88,128]{2,1,0:T(8,128)(2,1)S(1)}, bf16[3,88,128]{2,1,0:T(8,128)(2,1)S(1)}, u32[]{:S(2)}, u32[]{:S(2)}) collective-permute-start(bf16[3,88,128]{2,1,0:T(8,128)(2,1)S(1)} %bitcast.15), channel_id=1, source_target_pairs={{0,1},{1,2},{2,3},{4,5},{5,6},{6,7},{8,9},{9,10},{10,11},{12,13},{... | collective-permute-start | bytes 202760 | tf_op jit(solution)/shard_map/ppermute | solution.py:384
  130.7 6.2 %collective-permute-start.11 = (bf16[3,88,128]{2,1,0:T(8,128)(2,1)S(1)}, bf16[3,88,128]{2,1,0:T(8,128)(2,1)S(1)}, u32[]{:S(2)}, u32[]{:S(2)}) collective-permute-start(bf16[3,88,128]{2,1,0:T(8,128)(2,1)S(1)} %bitcast.14), channel_id=1, source_target_pairs={{1,0},{2,1},{3,2},{5,4},{6,5},{7,6},{9,8},{10,9},{11,10},{13,12},{... | collective-permute-start | bytes 202760 | tf_op jit(solution)/shard_map/ppermute | solution.py:385

commit v4 on v3

--- a/solution.py
+++ b/solution.py
@@ -264,16 +264,6 @@
     return low, high
 
 
-def diagonal(dx, dy):
-    count_x, count_y = lax.axis_size("sx"), lax.axis_size("sy")
-    return [
-        (x * count_y + y, (x + dx) * count_y + y + dy)
-        for x in range(count_x)
-        for y in range(count_y)
-        if 0 <= x + dx < count_x and 0 <= y + dy < count_y
-    ]
-
-
 def body(wall_temp, owner_map, stencil_column, material, conductivity, capacity):
     times, count, width = wall_temp.shape
     size_x, size_y, _ = material.shape
@@ -310,26 +300,33 @@
     )
     received = lax.all_to_all(packed, ("sx", "sy"), split_axis=0, concat_axis=0, tiled=True)
 
+    table, material = lax.optimization_barrier((dft_table(), material))
+    weights = pl.pallas_call(
+        weight_kernel,
+        out_shape=jax.ShapeDtypeStruct((TIME * size_y, TIME * size_y), BF16),
+        in_specs=[vmem],
+        out_specs=vmem,
+        compiler_params=params,
+        name="weights",
+    )(table)
+    material, weights = lax.optimization_barrier((material, weights))
     ids = (material + 1).astype(BF16)
     west, east = swap(ids, "sx", 0, Y0)
+    received, west, east = lax.optimization_barrier((received, west, east))
+    ids = jnp.concatenate([west, ids, east], axis=0)
     south, north = swap(ids, "sy", 1, Y0)
-    corner = {}
-    for dx in (1, -1):
-        for dy in (1, -1):
-            part = ids[size_x - Y0 :] if dx > 0 else ids[:Y0]
-            part = part[:, size_y - Y0 :] if dy > 0 else part[:, :Y0]
-            corner[dx, dy] = lax.ppermute(part, ("sx", "sy"), diagonal(dx, dy))
-    received, west, east, south, north, corner = lax.optimization_barrier(
-        (received, west, east, south, north, corner)
-    )
-    ids = jnp.concatenate(
-        [
-            jnp.concatenate([corner[1, 1], west, corner[1, -1]], axis=1),
-            jnp.concatenate([south, ids, north], axis=1),
-            jnp.concatenate([corner[-1, 1], east, corner[-1, -1]], axis=1),
-        ],
-        axis=0,
-    ).astype(jnp.int32)
+    cells = size_x * size_y
+    sums = pl.pallas_call(
+        lambda *refs: sum_kernel(*refs, times=times, cells=cells),
+        out_shape=jax.ShapeDtypeStruct((size_x, times * size_y, width), BF16),
+        in_specs=[vmem],
+        out_specs=vmem,
+        compiler_params=params,
+        name="cell_sum",
+    )(received)
+    gathered = lax.all_to_all(sums, "tm", split_axis=0, concat_axis=0, tiled=True)
+    gathered, ids, south, north = lax.optimization_barrier((gathered, ids, south, north))
+    ids = jnp.concatenate([south, ids, north], axis=1).astype(jnp.int32)
     harm_index = lax.axis_index("tm") * harms + jnp.arange(harms, dtype=jnp.int32)
     omega = omega_step * harm_index.astype(F32)
     coef = pl.pallas_call(
@@ -341,28 +338,6 @@
         compiler_params=params,
         name="coef",
     )(omega, conductivity, capacity, ids)
-
-    weights = pl.pallas_call(
-        weight_kernel,
-        out_shape=jax.ShapeDtypeStruct((TIME * size_y, TIME * size_y), BF16),
-        in_specs=[vmem],
-        out_specs=vmem,
-        compiler_params=params,
-        name="weights",
-    )(dft_table())
-    received, weights = lax.optimization_barrier((received, weights))
-
-    cells = size_x * size_y
-    sums = pl.pallas_call(
-        lambda *refs: sum_kernel(*refs, times=times, cells=cells),
-        out_shape=jax.ShapeDtypeStruct((size_x, times * size_y, width), BF16),
-        in_specs=[vmem],
-        out_specs=vmem,
-        compiler_params=params,
-        name="cell_sum",
-    )(received)
-    gathered = lax.all_to_all(sums, "tm", split_axis=0, concat_axis=0, tiled=True)
-    gathered, coef = lax.optimization_barrier((gathered, coef))
     harmonic = pl.pallas_call(
         dft_kernel,
         out_shape=jax.ShapeDtypeStruct((TIME * size_y, width), BF16),
@@ -373,6 +348,7 @@
     )(weights, gathered.reshape(TIME * size_y, width))
     harmonic = harmonic.reshape(steps, comps * size_y, width)
     source = lax.all_to_all(harmonic, "tm", split_axis=0, concat_axis=0, tiled=True)
+    source, coef = lax.optimization_barrier((source, coef))
 
     xlo, xhi = swap(source, "sx", 0, WIDE)
     rows = jnp.concatenate([xlo, source, xhi], axis=0).reshape(ext_x, comps, size_y, width)

time: 142 us -> 133 us (0.937)
  the two profiles are of different devices: /device:TPU:24 before, /device:TPU:2 now
where the time goes in v4:
time: 133 us; the launch traced here: 132 us
  waiting for transfers between devices  65.1 us (49%)
  starting transfers between devices  46.2 us (35%)
  Pallas kernels  17.5 us (13%)
  local copies, waits for them, and re-layouts  3.14 us (2%)
    ppermute x3, waiting for transfers between devices, swap(): lax.ppermute(lax.slice_in_dim(block, size - width, size, axis=dim), axis,...  38.7 us
    all_to_all x1, starting transfers between devices, body(): lax.all_to_all(sums, 'tm', split_axis=0, concat_axis=0, tiled=True)  10.5 us
    all_to_all x1, starting transfers between devices, body(): lax.all_to_all(packed, ('sx', 'sy'), split_axis=0, concat_axis=0, tiled=T...  10.3 us
    ppermute x3, waiting for transfers between devices, swap(): lax.ppermute(lax.slice_in_dim(block, 0, width, axis=dim), axis, backward)  9.64 us
    ppermute x3, starting transfers between devices, swap(): lax.ppermute(lax.slice_in_dim(block, size - width, size, axis=dim), axis,...  9.29 us
    all_to_all x1, waiting for transfers between devices, body(): lax.all_to_all(harmonic, 'tm', split_axis=0, concat_axis=0, tiled=True)  6.72 us
    ppermute x3, starting transfers between devices, swap(): lax.ppermute(lax.slice_in_dim(block, 0, width, axis=dim), axis, backward)  5.93 us
    pallas_call x1, Pallas kernels, body(): pl.pallas_call(solve_kernel, out_shape=jax.ShapeDtypeStruct((harms, 2, si...  4.66 us
  transfers between devices with their start and end apart: 11, of which 10 were waited for; matrix products, arithmetic and copies ran while one was open for 0% of the time, Pallas kernels for 4%

profile of v4, /device:TPU:2, one launch (start us, length us, event | category | flops | bytes accessed | tf_op | source)
XLA Modules:
  0.0 132.5 jit_solution(16971074003922887708)
XLA Ops:
  0.0 4.5 %pack.1 = bf16[32,264,128]{2,1,0:T(8,128)(2,1)} custom-call(bf16[4,1024,128]{2,1,0:T(8,128)(2,1)} %wall_hbm.1, s32[1,1024]{1,0:T(1,128)} %bitcast.15, s32[1,1024]{1,0:T(1,128)} %bitcast.16), custom_call_target="tpu_custom_call" | custom-call | tf_op jit(solution)/shard_map/pack/pallas_call | solution.py:279
  4.5 10.3 %all-to-all-start = ((bf16[32,264,128]{2,1,0:T(8,128)(2,1)}), bf16[32,264,128]{2,1,0:T(8,128)(2,1)S(1)}, u32[]{:S(2)}, u32[]{:S(2)}) async-start(bf16[32,264,128]{2,1,0:T(8,128)(2,1)} %pack.1), calls=%async_computation | async-start | bytes 4325376 | tf_op jit(solution)/shard_map/all_to_all | solution.py:301
  16.1 1.3 copy-done
  17.4 3.4 %collective-permute-start = (bf16[4,16,128]{2,1,0:T(8,128)(2,1)S(1)}, bf16[4,16,128]{2,1,0:T(8,128)(2,1)S(1)}, u32[]{:S(2)}, u32[]{:S(2)}) collective-permute-start(bf16[4,16,128]{2,1,0:T(8,128)(2,1)S(1)} %get-tuple-element.40), channel_id=1, source_target_pairs={{0,4},{4,8},{8,12},{12,16},{16,20},{20,24},{24,28},{1,5},{5,9},{9,... | collective-permute-start | bytes 49160 | tf_op jit(solution)/shard_map/ppermute | solution.py:262
  22.1 37.9 %collective-permute-done = bf16[4,16,128]{2,1,0:T(8,128)(2,1)S(1)} collective-permute-done((bf16[4,16,128]{2,1,0:T(8,128)(2,1)S(1)}, bf16[4,16,128]{2,1,0:T(8,128)(2,1)S(1)}, u32[]{:S(2)}, u32[]{:S(2)}) %collective-permute-start) | collective-permute-done | bytes 16416 | tf_op jit(solution)/shard_map/ppermute | solution.py:262
  60.0 3.2 %collective-permute-done.1 = bf16[4,16,128]{2,1,0:T(8,128)(2,1)S(1)} collective-permute-done((bf16[4,16,128]{2,1,0:T(8,128)(2,1)S(1)}, bf16[4,16,128]{2,1,0:T(8,128)(2,1)S(1)}, u32[]{:S(2)}, u32[]{:S(2)}) %collective-permute-start.1) | collective-permute-done | bytes 16416 | tf_op jit(solution)/shard_map/ppermute | solution.py:263
  63.2 3.7 %all-to-all-done.refs_0_ = bf16[32,264,128]{2,1,0:T(8,128)(2,1)S(1)} async-done(((bf16[32,264,128]{2,1,0:T(8,128)(2,1)}), bf16[32,264,128]{2,1,0:T(8,128)(2,1)S(1)}, u32[]{:S(2)}, u32[]{:S(2)}) %all-to-all-start) | async-done | bytes 2162720 | tf_op jit(solution)/shard_map/all_to_all | solution.py:301
  66.9 1.4 %cell_sum.1 = bf16[16,64,128]{2,1,0:T(8,128)(2,1)} custom-call(bf16[32,264,128]{2,1,0:T(8,128)(2,1)S(1)} %all-to-all-done.refs_0_), custom_call_target="tpu_custom_call" | custom-call | tf_op jit(solution)/shard_map/cell_sum/pallas_call | solution.py:319
  68.3 10.5 %all-to-all-start.1 = ((bf16[16,64,128]{2,1,0:T(8,128)(2,1)}), bf16[16,64,128]{2,1,0:T(8,128)(2,1)S(1)}, u32[]{:S(2)}, u32[]{:S(2)}) async-start(bf16[16,64,128]{2,1,0:T(8,128)(2,1)} %cell_sum.1), calls=%async_computation.1 | async-start | bytes 524288 | tf_op jit(solution)/shard_map/all_to_all | solution.py:327
  78.9 2.5 %collective-permute-start.2 = (bf16[24,4,128]{2,1,0:T(4,128)(2,1)S(1)}, bf16[24,4,128]{2,1,0:T(4,128)(2,1)S(1)}, u32[]{:S(2)}, u32[]{:S(2)}) collective-permute-start(bf16[24,4,128]{2,1,0:T(4,128)(2,1)S(1)} %get-tuple-element.38), channel_id=1, source_target_pairs={{0,1},{1,2},{2,3},{4,5},{5,6},{6,7},{8,9},{9,10},{10,11},{12,13},{... | collective-permute-start | bytes 73736 | tf_op jit(solution)/shard_map/ppermute | solution.py:262
  81.4 3.3 %collective-permute-start.3 = (bf16[24,4,128]{2,1,0:T(4,128)(2,1)S(1)}, bf16[24,4,128]{2,1,0:T(4,128)(2,1)S(1)}, u32[]{:S(2)}, u32[]{:S(2)}) collective-permute-start(bf16[24,4,128]{2,1,0:T(4,128)(2,1)S(1)} %get-tuple-element.37), channel_id=1, source_target_pairs={{1,0},{2,1},{3,2},{5,4},{6,5},{7,6},{9,8},{10,9},{11,10},{13,12},{... | collective-permute-start | bytes 73736 | tf_op jit(solution)/shard_map/ppermute | solution.py:263
  84.8 2.4 %collective-permute-done.3 = bf16[24,4,128]{2,1,0:T(4,128)(2,1)S(1)} collective-permute-done((bf16[24,4,128]{2,1,0:T(4,128)(2,1)S(1)}, bf16[24,4,128]{2,1,0:T(4,128)(2,1)S(1)}, u32[]{:S(2)}, u32[]{:S(2)}) %collective-permute-start.3) | collective-permute-done | bytes 24608 | tf_op jit(solution)/shard_map/ppermute | solution.py:263
  87.1 2.9 %all-to-all-done.1 = bf16[16,64,128]{2,1,0:T(8,128)(2,1)S(1)} async-done(((bf16[16,64,128]{2,1,0:T(8,128)(2,1)}), bf16[16,64,128]{2,1,0:T(8,128)(2,1)S(1)}, u32[]{:S(2)}, u32[]{:S(2)}) %all-to-all-start.1) | async-done | bytes 262176 | tf_op jit(solution)/shard_map/all_to_all | solution.py:327
  90.0 1.6 %copy-done.1 = bf16[1024,1024]{1,0:T(8,128)(2,1)S(1)} copy-done((bf16[1024,1024]{1,0:T(8,128)(2,1)S(1)}, bf16[1024,1024]{1,0:T(8,128)(2,1)}, u32[]{:S(2)}) %copy-start.1) | copy-done | bytes 2097176
  91.6 1.4 %dft.1 = bf16[1024,128]{1,0:T(8,128)(2,1)} custom-call(bf16[1024,1024]{1,0:T(8,128)(2,1)S(1)} %copy-done.1, bf16[1024,128]{1,0:T(8,128)(2,1)S(1)} %bitcast.10), custom_call_target="tpu_custom_call" | custom-call | tf_op jit(solution)/shard_map/dft/pallas_call | solution.py:341
  93.0 4.3 %all-to-all-start.2 = ((bf16[16,64,128]{2,1,0:T(8,128)(2,1)}), bf16[16,64,128]{2,1,0:T(8,128)(2,1)S(1)}, u32[]{:S(2)}, u32[]{:S(2)}) async-start(bf16[16,64,128]{2,1,0:T(8,128)(2,1)} %bitcast.4), calls=%async_computation.2 | async-start | bytes 524288 | tf_op jit(solution)/shard_map/all_to_all | solution.py:350
  97.5 4.3 %coef.1.coef_ref = f32[22,7,24,128]{3,2,1,0:T(8,128)S(1)} custom-call(f32[2]{0:T(128)S(1)} %convert_multiply_fusion.omega_ref, f32[4]{0:T(128)S(1)} %copy-done.2, f32[4]{0:T(128)S(1)} %copy-done.3, s32[24,24,128]{2,1,0:T(8,128)S(1)} %maximum_convert_fusion.ids_ref), custom_call_target="tpu_custom_call" | custom-call | tf_op jit(solution)/shard_map/coef/pallas_call | solution.py:332
  101.8 6.7 %all-to-all-done.2.mid_ref = bf16[16,64,128]{2,1,0:T(8,128)(2,1)S(1)} async-done(((bf16[16,64,128]{2,1,0:T(8,128)(2,1)}), bf16[16,64,128]{2,1,0:T(8,128)(2,1)S(1)}, u32[]{:S(2)}, u32[]{:S(2)}) %all-to-all-start.2) | async-done | bytes 262176 | tf_op jit(solution)/shard_map/all_to_all | solution.py:350
  108.6 3.4 %collective-permute-start.4 = (bf16[3,64,128]{2,1,0:T(8,128)(2,1)S(1)}, bf16[3,64,128]{2,1,0:T(8,128)(2,1)S(1)}, u32[]{:S(2)}, u32[]{:S(2)}) collective-permute-start(bf16[3,64,128]{2,1,0:T(8,128)(2,1)S(1)} %get-tuple-element.34), channel_id=1, source_target_pairs={{0,4},{4,8},{8,12},{12,16},{16,20},{20,24},{24,28},{1,5},{5,9},{9,... | collective-permute-start | bytes 147464 | tf_op jit(solution)/shard_map/ppermute | solution.py:262
  114.1 4.1 %collective-permute-done.5.xhi_ref = bf16[3,64,128]{2,1,0:T(8,128)(2,1)S(1)} collective-permute-done((bf16[3,64,128]{2,1,0:T(8,128)(2,1)S(1)}, bf16[3,64,128]{2,1,0:T(8,128)(2,1)S(1)}, u32[]{:S(2)}, u32[]{:S(2)}) %collective-permute-start.5) | collective-permute-done | bytes 49184 | tf_op jit(solution)/shard_map/ppermute | solution.py:263
  118.6 3.1 %collective-permute-start.6 = (bf16[3,88,128]{2,1,0:T(8,128)(2,1)S(1)}, bf16[3,88,128]{2,1,0:T(8,128)(2,1)S(1)}, u32[]{:S(2)}, u32[]{:S(2)}) collective-permute-start(bf16[3,88,128]{2,1,0:T(8,128)(2,1)S(1)} %bitcast.14), channel_id=1, source_target_pairs={{0,1},{1,2},{2,3},{4,5},{5,6},{6,7},{8,9},{9,10},{10,11},{12,13},{... | collective-permute-start | bytes 202760 | tf_op jit(solution)/shard_map/ppermute | solution.py:360
  121.7 2.8 %collective-permute-start.7 = (bf16[3,88,128]{2,1,0:T(8,128)(2,1)S(1)}, bf16[3,88,128]{2,1,0:T(8,128)(2,1)S(1)}, u32[]{:S(2)}, u32[]{:S(2)}) collective-permute-start(bf16[3,88,128]{2,1,0:T(8,128)(2,1)S(1)} %bitcast.13), channel_id=1, source_target_pairs={{1,0},{2,1},{3,2},{5,4},{6,5},{7,6},{9,8},{10,9},{11,10},{13,12},{... | collective-permute-start | bytes 202760 | tf_op jit(solution)/shard_map/ppermute | solution.py:361
  124.7 3.1 %collective-permute-done.7.yhi_ref = bf16[3,88,128]{2,1,0:T(8,128)(2,1)S(1)} collective-permute-done((bf16[3,88,128]{2,1,0:T(8,128)(2,1)S(1)}, bf16[3,88,128]{2,1,0:T(8,128)(2,1)S(1)}, u32[]{:S(2)}, u32[]{:S(2)}) %collective-permute-start.7) | collective-permute-done | bytes 67616 | tf_op jit(solution)/shard_map/ppermute | solution.py:361
  127.8 4.7 %solve.1 = f32[2,2,16,16,128]{4,3,2,1,0:T(8,128)} custom-call(bf16[16,64,128]{2,1,0:T(8,128)(2,1)S(1)} %all-to-all-done.2.mid_ref, bf16[3,64,128]{2,1,0:T(8,128)(2,1)S(1)} %collective-permute-done.4.xlo_ref, bf16[3,64,128]{2,1,0:T(8,128)(2,1)S(1)} %collective-permute-done.5.xhi_ref, bf16[3,88,128]{2,1,0:T(8,128)(2,1)S(1)} %collective-permute-done.6.ylo_ref, ...), custom_call_target="tpu_custom_call" | custom-call | tf_op jit(solution)/shard_map/solve/pallas_call | solution.py:362
  (30 shorter events, 5.5 us)
Async XLA Ops:
  4.5 62.4 %all-to-all-start = ((bf16[32,264,128]{2,1,0:T(8,128)(2,1)}), bf16[32,264,128]{2,1,0:T(8,128)(2,1)S(1)}, u32[]{:S(2)}, u32[]{:S(2)}) async-start(bf16[32,264,128]{2,1,0:T(8,128)(2,1)} %pack.1), calls=%async_computation | async-start | bytes 4325376 | tf_op jit(solution)/shard_map/all_to_all | solution.py:301
  14.8 2.6 %copy-start.4 = (s32[16,16,128]{2,1,0:T(8,128)S(1)}, s32[16,16,128]{2,1,0:T(8,128)}, u32[]{:S(2)}) copy-start(s32[16,16,128]{2,1,0:T(8,128)} %param.9) | copy-start | bytes 393220
  16.1 1.3 copy-start
  17.4 42.5 %collective-permute-start = (bf16[4,16,128]{2,1,0:T(8,128)(2,1)S(1)}, bf16[4,16,128]{2,1,0:T(8,128)(2,1)S(1)}, u32[]{:S(2)}, u32[]{:S(2)}) collective-permute-start(bf16[4,16,128]{2,1,0:T(8,128)(2,1)S(1)} %get-tuple-element.40), channel_id=1, source_target_pairs={{0,4},{4,8},{8,12},{12,16},{16,20},{20,24},{24,28},{1,5},{5,9},{9,... | collective-permute-start | bytes 49160 | tf_op jit(solution)/shard_map/ppermute | solution.py:262
  20.8 42.4 %collective-permute-start.1 = (bf16[4,16,128]{2,1,0:T(8,128)(2,1)S(1)}, bf16[4,16,128]{2,1,0:T(8,128)(2,1)S(1)}, u32[]{:S(2)}, u32[]{:S(2)}) collective-permute-start(bf16[4,16,128]{2,1,0:T(8,128)(2,1)S(1)} %get-tuple-element.39), channel_id=1, source_target_pairs={{4,0},{8,4},{12,8},{16,12},{20,16},{24,20},{28,24},{5,1},{9,5},{13... | collective-permute-start | bytes 49160 | tf_op jit(solution)/shard_map/ppermute | solution.py:263
  68.3 29.2 %copy-start.2 = (f32[4]{0:T(128)S(1)}, f32[4]{0:T(128)}, u32[]{:S(2)}) copy-start(f32[4]{0:T(128)} %conductivity_ref.1) | copy-start | bytes 52
  68.3 29.2 %copy-start.3 = (f32[4]{0:T(128)S(1)}, f32[4]{0:T(128)}, u32[]{:S(2)}) copy-start(f32[4]{0:T(128)} %capacity_ref.1) | copy-start | bytes 52
  68.3 21.7 %all-to-all-start.1 = ((bf16[16,64,128]{2,1,0:T(8,128)(2,1)}), bf16[16,64,128]{2,1,0:T(8,128)(2,1)S(1)}, u32[]{:S(2)}, u32[]{:S(2)}) async-start(bf16[16,64,128]{2,1,0:T(8,128)(2,1)} %cell_sum.1), calls=%async_computation.1 | async-start | bytes 524288 | tf_op jit(solution)/shard_map/all_to_all | solution.py:327
  78.9 5.9 %collective-permute-start.2 = (bf16[24,4,128]{2,1,0:T(4,128)(2,1)S(1)}, bf16[24,4,128]{2,1,0:T(4,128)(2,1)S(1)}, u32[]{:S(2)}, u32[]{:S(2)}) collective-permute-start(bf16[24,4,128]{2,1,0:T(4,128)(2,1)S(1)} %get-tuple-element.38), channel_id=1, source_target_pairs={{0,1},{1,2},{2,3},{4,5},{5,6},{6,7},{8,9},{9,10},{10,11},{12,13},{... | collective-permute-start | bytes 73736 | tf_op jit(solution)/shard_map/ppermute | solution.py:262
  81.4 5.7 %collective-permute-start.3 = (bf16[24,4,128]{2,1,0:T(4,128)(2,1)S(1)}, bf16[24,4,128]{2,1,0:T(4,128)(2,1)S(1)}, u32[]{:S(2)}, u32[]{:S(2)}) collective-permute-start(bf16[24,4,128]{2,1,0:T(4,128)(2,1)S(1)} %get-tuple-element.37), channel_id=1, source_target_pairs={{1,0},{2,1},{3,2},{5,4},{6,5},{7,6},{9,8},{10,9},{11,10},{13,12},{... | collective-permute-start | bytes 73736 | tf_op jit(solution)/shard_map/ppermute | solution.py:263
  90.0 1.6 %copy-start.1 = (bf16[1024,1024]{1,0:T(8,128)(2,1)S(1)}, bf16[1024,1024]{1,0:T(8,128)(2,1)}, u32[]{:S(2)}) copy-start(bf16[1024,1024]{1,0:T(8,128)(2,1)} %copy-done) | copy-start | bytes 6291460
  93.0 15.5 %all-to-all-start.2 = ((bf16[16,64,128]{2,1,0:T(8,128)(2,1)}), bf16[16,64,128]{2,1,0:T(8,128)(2,1)S(1)}, u32[]{:S(2)}, u32[]{:S(2)}) async-start(bf16[16,64,128]{2,1,0:T(8,128)(2,1)} %bitcast.4), calls=%async_computation.2 | async-start | bytes 524288 | tf_op jit(solution)/shard_map/all_to_all | solution.py:350
  108.6 5.5 %collective-permute-start.4 = (bf16[3,64,128]{2,1,0:T(8,128)(2,1)S(1)}, bf16[3,64,128]{2,1,0:T(8,128)(2,1)S(1)}, u32[]{:S(2)}, u32[]{:S(2)}) collective-permute-start(bf16[3,64,128]{2,1,0:T(8,128)(2,1)S(1)} %get-tuple-element.34), channel_id=1, source_target_pairs={{0,4},{4,8},{8,12},{12,16},{16,20},{20,24},{24,28},{1,5},{5,9},{9,... | collective-permute-start | bytes 147464 | tf_op jit(solution)/shard_map/ppermute | solution.py:262
  112.0 6.2 %collective-permute-start.5 = (bf16[3,64,128]{2,1,0:T(8,128)(2,1)S(1)}, bf16[3,64,128]{2,1,0:T(8,128)(2,1)S(1)}, u32[]{:S(2)}, u32[]{:S(2)}) collective-permute-start(bf16[3,64,128]{2,1,0:T(8,128)(2,1)S(1)} %get-tuple-element.33), channel_id=1, source_target_pairs={{4,0},{8,4},{12,8},{16,12},{20,16},{24,20},{28,24},{5,1},{9,5},{13... | collective-permute-start | bytes 147464 | tf_op jit(solution)/shard_map/ppermute | solution.py:263
  118.6 6.2 %collective-permute-start.6 = (bf16[3,88,128]{2,1,0:T(8,128)(2,1)S(1)}, bf16[3,88,128]{2,1,0:T(8,128)(2,1)S(1)}, u32[]{:S(2)}, u32[]{:S(2)}) collective-permute-start(bf16[3,88,128]{2,1,0:T(8,128)(2,1)S(1)} %bitcast.14), channel_id=1, source_target_pairs={{0,1},{1,2},{2,3},{4,5},{5,6},{6,7},{8,9},{9,10},{10,11},{12,13},{... | collective-permute-start | bytes 202760 | tf_op jit(solution)/shard_map/ppermute | solution.py:360
  121.7 6.2 %collective-permute-start.7 = (bf16[3,88,128]{2,1,0:T(8,128)(2,1)S(1)}, bf16[3,88,128]{2,1,0:T(8,128)(2,1)S(1)}, u32[]{:S(2)}, u32[]{:S(2)}) collective-permute-start(bf16[3,88,128]{2,1,0:T(8,128)(2,1)S(1)} %bitcast.13), channel_id=1, source_target_pairs={{1,0},{2,1},{3,2},{5,4},{6,5},{7,6},{9,8},{10,9},{11,10},{13,12},{... | collective-permute-start | bytes 202760 | tf_op jit(solution)/shard_map/ppermute | solution.py:361

commit v5 on v4

--- a/solution.py
+++ b/solution.py
@@ -37,7 +37,7 @@
 
 
 def pack_kernel(
-    wall_hbm, owner_hbm, column_hbm, out_hbm, wall_ref, owner_ref, column_ref, stage_ref, slot_ref, in_sem, out_sem
+    wall_hbm, owner_hbm, column_hbm, out_hbm, wall_ref, owner_ref, column_ref, stage_ref, in_sem, out_sem
 ):
     times, count, width = wall_ref.shape
     pulls = [
@@ -55,9 +55,9 @@
     hit_b = hit.astype(F32).astype(BF16)
     earlier = jnp.dot(hit_b, before, preferred_element_type=F32)
     rank = jnp.sum(jnp.where(hit, earlier, 0.0), axis=0, keepdims=True).astype(jnp.int32)
-    slot_ref[...] = owner * CAP + rank
     pulls[1].wait()
-    at_rank = (rank == iota((2 * CAP, count), 0) % CAP).astype(F32).astype(BF16)
+    half = (rank == iota((CAP, count), 0)).astype(F32).astype(BF16)
+    at_rank = jnp.concatenate([half, half], axis=0)
     marks = jnp.where(hit, (column_ref[...] + 1).astype(F32), 0.0).astype(BF16)
     columns = lax.dot_general(
         marks, at_rank, (((1,), (1,)), ((), ())), preferred_element_type=F32
@@ -69,7 +69,9 @@
     group = OWNERS // out_sem.shape[0]
     pushes = []
     for g in range(OWNERS // group):
-        place = (slot_ref[...] - g * (group * CAP) == iota((group * CAP, count), 0)).astype(F32).astype(BF16)
+        place = jnp.concatenate(
+            [half * hit_b[o : o + 1, :] for o in range(g * group, (g + 1) * group)], axis=0
+        )
         rows = jnp.concatenate([wall_ref[t] for t in range(times)], axis=1)
         moved = jnp.dot(place, rows, preferred_element_type=F32).astype(BF16)
         for t in range(times):
@@ -131,9 +133,17 @@
 
 
 def dft_kernel(weights_ref, rows_ref, out_ref):
-    out_ref[...] = jnp.dot(
-        weights_ref[...], rows_ref[...], preferred_element_type=F32
+    times, side, width = rows_ref.shape
+    half = side // 2
+    rows = rows_ref[...].astype(F32)
+    rows = jnp.concatenate(
+        [rows[:, :half].reshape(times * half, width), rows[:, half:].reshape(times * half, width)], axis=1
     ).astype(BF16)
+    made = jnp.dot(weights_ref[...], rows, preferred_element_type=F32)
+    made = jnp.concatenate(
+        [made[:, :width].reshape(times, half, width), made[:, width:].reshape(times, half, width)], axis=1
+    )
+    out_ref[...] = made.astype(BF16)
 
 
 def coef_kernel(omega_ref, conductivity_ref, capacity_ref, ids_ref, coef_ref, c_ref):
@@ -271,7 +281,7 @@
     comps = 2 * HARM // steps
     harms = comps // 2
     ext_x = size_x + 2 * WIDE
-    params = pltpu.CompilerParams(vmem_limit_bytes=48 * 1024 * 1024)
+    params = pltpu.CompilerParams(vmem_limit_bytes=16 * 1024 * 1024)
     vmem = pl.BlockSpec(memory_space=pltpu.VMEM)
     smem = pl.BlockSpec(memory_space=pltpu.SMEM)
 
@@ -286,7 +296,6 @@
             pltpu.VMEM((1, count), jnp.int32),
             pltpu.VMEM((1, count), jnp.int32),
             pltpu.VMEM((OWNERS, times * CAP + 8, width), BF16),
-            pltpu.VMEM((1, count), jnp.int32),
             pltpu.SemaphoreType.DMA((3,)),
             pltpu.SemaphoreType.DMA((8,)),
         ],
@@ -303,7 +312,7 @@
     table, material = lax.optimization_barrier((dft_table(), material))
     weights = pl.pallas_call(
         weight_kernel,
-        out_shape=jax.ShapeDtypeStruct((TIME * size_y, TIME * size_y), BF16),
+        out_shape=jax.ShapeDtypeStruct((TIME * size_y // 2, TIME * size_y // 2), BF16),
         in_specs=[vmem],
         out_specs=vmem,
         compiler_params=params,
@@ -340,12 +349,12 @@
     )(omega, conductivity, capacity, ids)
     harmonic = pl.pallas_call(
         dft_kernel,
-        out_shape=jax.ShapeDtypeStruct((TIME * size_y, width), BF16),
+        out_shape=jax.ShapeDtypeStruct((TIME, size_y, width), BF16),
         in_specs=[vmem] * 2,
         out_specs=vmem,
         compiler_params=params,
         name="dft",
-    )(weights, gathered.reshape(TIME * size_y, width))
+    )(weights, gathered.reshape(TIME, size_y, width))
     harmonic = harmonic.reshape(steps, comps * size_y, width)
     source = lax.all_to_all(harmonic, "tm", split_axis=0, concat_axis=0, tiled=True)
     source, coef = lax.optimization_barrier((source, coef))

time: 133 us -> 131 us (0.985)
  local copies, waits for them, and re-layouts: 3.14 us -> 0.26 us
  waiting for transfers between devices: 65.1 us -> 67 us
    unnamed x12 -> x8, local copies, waits for them, and re-layouts: 2.97 us -> 0.08 us
    ppermute x3, waiting for transfers between devices: 38.7 us -> 40.6 us  [swap(): lax.ppermute(lax.slice_in_dim(block, size - width, size, axis=dim), axis,...]
where the time goes in v5:
time: 131 us
  waiting for transfers between devices  67 us (51%)
  starting transfers between devices  46.2 us (35%)
  Pallas kernels  16.4 us (13%)
    ppermute x3, waiting for transfers between devices, swap(): lax.ppermute(lax.slice_in_dim(block, size - width, size, axis=dim), axis,...  40.6 us
    all_to_all x1, starting transfers between devices, body(): lax.all_to_all(sums, 'tm', split_axis=0, concat_axis=0, tiled=True)  10.4 us
    all_to_all x1, starting transfers between devices, body(): lax.all_to_all(packed, ('sx', 'sy'), split_axis=0, concat_axis=0, tiled=T...  10.4 us
    ppermute x3, waiting for transfers between devices, swap(): lax.ppermute(lax.slice_in_dim(block, 0, width, axis=dim), axis, backward)  9.64 us
    ppermute x3, starting transfers between devices, swap(): lax.ppermute(lax.slice_in_dim(block, size - width, size, axis=dim), axis,...  9.3 us
    all_to_all x1, waiting for transfers between devices, body(): lax.all_to_all(harmonic, 'tm', split_axis=0, concat_axis=0, tiled=True)  6.72 us
    ppermute x3, starting transfers between devices, swap(): lax.ppermute(lax.slice_in_dim(block, 0, width, axis=dim), axis, backward)  5.92 us
    pallas_call x1, Pallas kernels, body(): pl.pallas_call(solve_kernel, out_shape=jax.ShapeDtypeStruct((harms, 2, si...  4.66 us
  transfers between devices with their start and end apart: 11, of which 10 were waited for; matrix products, arithmetic and copies ran while one was open for 0% of the time, Pallas kernels for 4%

profile of v5, /device:TPU:2, one launch (start us, length us, event | category | flops | bytes accessed | tf_op | source)
XLA Modules:
  0.0 130.5 jit_solution(4930476126424792310)
XLA Ops:
  0.0 4.5 %pack.1 = bf16[32,264,128]{2,1,0:T(8,128)(2,1)} custom-call(bf16[4,1024,128]{2,1,0:T(8,128)(2,1)} %wall_hbm.1, s32[1,1024]{1,0:T(1,128)} %bitcast.15, s32[1,1024]{1,0:T(1,128)} %bitcast.16), custom_call_target="tpu_custom_call" | custom-call | tf_op jit(solution)/shard_map/pack/pallas_call | solution.py:289
  4.5 10.4 %all-to-all-start = ((bf16[32,264,128]{2,1,0:T(8,128)(2,1)}), bf16[32,264,128]{2,1,0:T(8,128)(2,1)S(1)}, u32[]{:S(2)}, u32[]{:S(2)}) async-start(bf16[32,264,128]{2,1,0:T(8,128)(2,1)} %pack.1), calls=%async_computation | async-start | bytes 4325376 | tf_op jit(solution)/shard_map/all_to_all | solution.py:310
  15.6 3.4 %collective-permute-start = (bf16[4,16,128]{2,1,0:T(8,128)(2,1)S(1)}, bf16[4,16,128]{2,1,0:T(8,128)(2,1)S(1)}, u32[]{:S(2)}, u32[]{:S(2)}) collective-permute-start(bf16[4,16,128]{2,1,0:T(8,128)(2,1)S(1)} %get-tuple-element.40), channel_id=1, source_target_pairs={{0,4},{4,8},{8,12},{12,16},{16,20},{20,24},{24,28},{1,5},{5,9},{9,... | collective-permute-start | bytes 49160 | tf_op jit(solution)/shard_map/ppermute | solution.py:272
  19.0 1.3 collective-permute-start.1
  20.3 39.8 %collective-permute-done = bf16[4,16,128]{2,1,0:T(8,128)(2,1)S(1)} collective-permute-done((bf16[4,16,128]{2,1,0:T(8,128)(2,1)S(1)}, bf16[4,16,128]{2,1,0:T(8,128)(2,1)S(1)}, u32[]{:S(2)}, u32[]{:S(2)}) %collective-permute-start) | collective-permute-done | bytes 16416 | tf_op jit(solution)/shard_map/ppermute | solution.py:272
  60.1 3.2 %collective-permute-done.1 = bf16[4,16,128]{2,1,0:T(8,128)(2,1)S(1)} collective-permute-done((bf16[4,16,128]{2,1,0:T(8,128)(2,1)S(1)}, bf16[4,16,128]{2,1,0:T(8,128)(2,1)S(1)}, u32[]{:S(2)}, u32[]{:S(2)}) %collective-permute-start.1) | collective-permute-done | bytes 16416 | tf_op jit(solution)/shard_map/ppermute | solution.py:273
  63.3 3.7 %all-to-all-done.refs_0_ = bf16[32,264,128]{2,1,0:T(8,128)(2,1)S(1)} async-done(((bf16[32,264,128]{2,1,0:T(8,128)(2,1)}), bf16[32,264,128]{2,1,0:T(8,128)(2,1)S(1)}, u32[]{:S(2)}, u32[]{:S(2)}) %all-to-all-start) | async-done | bytes 2162720 | tf_op jit(solution)/shard_map/all_to_all | solution.py:310
  67.0 1.4 %cell_sum.1 = bf16[16,64,128]{2,1,0:T(8,128)(2,1)} custom-call(bf16[32,264,128]{2,1,0:T(8,128)(2,1)S(1)} %all-to-all-done.refs_0_), custom_call_target="tpu_custom_call" | custom-call | tf_op jit(solution)/shard_map/cell_sum/pallas_call | solution.py:328
  68.4 10.4 %all-to-all-start.1 = ((bf16[16,64,128]{2,1,0:T(8,128)(2,1)}), bf16[16,64,128]{2,1,0:T(8,128)(2,1)S(1)}, u32[]{:S(2)}, u32[]{:S(2)}) async-start(bf16[16,64,128]{2,1,0:T(8,128)(2,1)} %cell_sum.1), calls=%async_computation.1 | async-start | bytes 524288 | tf_op jit(solution)/shard_map/all_to_all | solution.py:336
  78.9 2.5 %collective-permute-start.2 = (bf16[24,4,128]{2,1,0:T(4,128)(2,1)S(1)}, bf16[24,4,128]{2,1,0:T(4,128)(2,1)S(1)}, u32[]{:S(2)}, u32[]{:S(2)}) collective-permute-start(bf16[24,4,128]{2,1,0:T(4,128)(2,1)S(1)} %get-tuple-element.38), channel_id=1, source_target_pairs={{0,1},{1,2},{2,3},{4,5},{5,6},{6,7},{8,9},{9,10},{10,11},{12,13},{... | collective-permute-start | bytes 73736 | tf_op jit(solution)/shard_map/ppermute | solution.py:272
  81.4 3.3 %collective-permute-start.3 = (bf16[24,4,128]{2,1,0:T(4,128)(2,1)S(1)}, bf16[24,4,128]{2,1,0:T(4,128)(2,1)S(1)}, u32[]{:S(2)}, u32[]{:S(2)}) collective-permute-start(bf16[24,4,128]{2,1,0:T(4,128)(2,1)S(1)} %get-tuple-element.37), channel_id=1, source_target_pairs={{1,0},{2,1},{3,2},{5,4},{6,5},{7,6},{9,8},{10,9},{11,10},{13,12},{... | collective-permute-start | bytes 73736 | tf_op jit(solution)/shard_map/ppermute | solution.py:273
  84.8 2.4 %collective-permute-done.3 = bf16[24,4,128]{2,1,0:T(4,128)(2,1)S(1)} collective-permute-done((bf16[24,4,128]{2,1,0:T(4,128)(2,1)S(1)}, bf16[24,4,128]{2,1,0:T(4,128)(2,1)S(1)}, u32[]{:S(2)}, u32[]{:S(2)}) %collective-permute-start.3) | collective-permute-done | bytes 24608 | tf_op jit(solution)/shard_map/ppermute | solution.py:273
  87.2 2.9 %all-to-all-done.1 = bf16[16,64,128]{2,1,0:T(8,128)(2,1)S(1)} async-done(((bf16[16,64,128]{2,1,0:T(8,128)(2,1)}), bf16[16,64,128]{2,1,0:T(8,128)(2,1)S(1)}, u32[]{:S(2)}, u32[]{:S(2)}) %all-to-all-start.1) | async-done | bytes 262176 | tf_op jit(solution)/shard_map/all_to_all | solution.py:336
  90.1 1.0 dft.1
  91.1 4.3 %all-to-all-start.2 = ((bf16[16,64,128]{2,1,0:T(8,128)(2,1)}), bf16[16,64,128]{2,1,0:T(8,128)(2,1)S(1)}, u32[]{:S(2)}, u32[]{:S(2)}) async-start(bf16[16,64,128]{2,1,0:T(8,128)(2,1)} %bitcast.4), calls=%async_computation.2 | async-start | bytes 524288 | tf_op jit(solution)/shard_map/all_to_all | solution.py:359
  95.5 4.3 %coef.1.coef_ref = f32[22,7,24,128]{3,2,1,0:T(8,128)S(1)} custom-call(f32[2]{0:T(128)S(1)} %convert_multiply_fusion.omega_ref, f32[4]{0:T(128)S(1)} %copy-done, f32[4]{0:T(128)S(1)} %copy-done.1, s32[24,24,128]{2,1,0:T(8,128)S(1)} %maximum_convert_fusion.ids_ref), custom_call_target="tpu_custom_call" | custom-call | tf_op jit(solution)/shard_map/coef/pallas_call | solution.py:341
  99.8 6.7 %all-to-all-done.2.mid_ref = bf16[16,64,128]{2,1,0:T(8,128)(2,1)S(1)} async-done(((bf16[16,64,128]{2,1,0:T(8,128)(2,1)}), bf16[16,64,128]{2,1,0:T(8,128)(2,1)S(1)}, u32[]{:S(2)}, u32[]{:S(2)}) %all-to-all-start.2) | async-done | bytes 262176 | tf_op jit(solution)/shard_map/all_to_all | solution.py:359
  106.6 3.4 %collective-permute-start.4 = (bf16[3,64,128]{2,1,0:T(8,128)(2,1)S(1)}, bf16[3,64,128]{2,1,0:T(8,128)(2,1)S(1)}, u32[]{:S(2)}, u32[]{:S(2)}) collective-permute-start(bf16[3,64,128]{2,1,0:T(8,128)(2,1)S(1)} %get-tuple-element.34), channel_id=1, source_target_pairs={{0,4},{4,8},{8,12},{12,16},{16,20},{20,24},{24,28},{1,5},{5,9},{9,... | collective-permute-start | bytes 147464 | tf_op jit(solution)/shard_map/ppermute | solution.py:272
  110.0 1.3 collective-permute-start.5
  112.1 4.1 %collective-permute-done.5.xhi_ref = bf16[3,64,128]{2,1,0:T(8,128)(2,1)S(1)} collective-permute-done((bf16[3,64,128]{2,1,0:T(8,128)(2,1)S(1)}, bf16[3,64,128]{2,1,0:T(8,128)(2,1)S(1)}, u32[]{:S(2)}, u32[]{:S(2)}) %collective-permute-start.5) | collective-permute-done | bytes 49184 | tf_op jit(solution)/shard_map/ppermute | solution.py:273
  116.6 3.1 %collective-permute-start.6 = (bf16[3,88,128]{2,1,0:T(8,128)(2,1)S(1)}, bf16[3,88,128]{2,1,0:T(8,128)(2,1)S(1)}, u32[]{:S(2)}, u32[]{:S(2)}) collective-permute-start(bf16[3,88,128]{2,1,0:T(8,128)(2,1)S(1)} %bitcast.14), channel_id=1, source_target_pairs={{0,1},{1,2},{2,3},{4,5},{5,6},{6,7},{8,9},{9,10},{10,11},{12,13},{... | collective-permute-start | bytes 202760 | tf_op jit(solution)/shard_map/ppermute | solution.py:369
  119.7 2.8 %collective-permute-start.7 = (bf16[3,88,128]{2,1,0:T(8,128)(2,1)S(1)}, bf16[3,88,128]{2,1,0:T(8,128)(2,1)S(1)}, u32[]{:S(2)}, u32[]{:S(2)}) collective-permute-start(bf16[3,88,128]{2,1,0:T(8,128)(2,1)S(1)} %bitcast.13), channel_id=1, source_target_pairs={{1,0},{2,1},{3,2},{5,4},{6,5},{7,6},{9,8},{10,9},{11,10},{13,12},{... | collective-permute-start | bytes 202760 | tf_op jit(solution)/shard_map/ppermute | solution.py:370
  122.8 3.1 %collective-permute-done.7.yhi_ref = bf16[3,88,128]{2,1,0:T(8,128)(2,1)S(1)} collective-permute-done((bf16[3,88,128]{2,1,0:T(8,128)(2,1)S(1)}, bf16[3,88,128]{2,1,0:T(8,128)(2,1)S(1)}, u32[]{:S(2)}, u32[]{:S(2)}) %collective-permute-start.7) | collective-permute-done | bytes 67616 | tf_op jit(solution)/shard_map/ppermute | solution.py:370
  125.8 4.7 %solve.1 = f32[2,2,16,16,128]{4,3,2,1,0:T(8,128)} custom-call(bf16[16,64,128]{2,1,0:T(8,128)(2,1)S(1)} %all-to-all-done.2.mid_ref, bf16[3,64,128]{2,1,0:T(8,128)(2,1)S(1)} %collective-permute-done.4.xlo_ref, bf16[3,64,128]{2,1,0:T(8,128)(2,1)S(1)} %collective-permute-done.5.xhi_ref, bf16[3,88,128]{2,1,0:T(8,128)(2,1)S(1)} %collective-permute-done.6.ylo_ref, ...), custom_call_target="tpu_custom_call" | custom-call | tf_op jit(solution)/shard_map/solve/pallas_call | solution.py:371
  (26 shorter events, 2.2 us)
Async XLA Ops:
  4.5 11.0 %copy-start.2 = (s32[16,16,128]{2,1,0:T(8,128)S(1)}, s32[16,16,128]{2,1,0:T(8,128)}, u32[]{:S(2)}) copy-start(s32[16,16,128]{2,1,0:T(8,128)} %param.9) | copy-start | bytes 393220
  4.5 62.5 %all-to-all-start = ((bf16[32,264,128]{2,1,0:T(8,128)(2,1)}), bf16[32,264,128]{2,1,0:T(8,128)(2,1)S(1)}, u32[]{:S(2)}, u32[]{:S(2)}) async-start(bf16[32,264,128]{2,1,0:T(8,128)(2,1)} %pack.1), calls=%async_computation | async-start | bytes 4325376 | tf_op jit(solution)/shard_map/all_to_all | solution.py:310
  15.6 44.5 %collective-permute-start = (bf16[4,16,128]{2,1,0:T(8,128)(2,1)S(1)}, bf16[4,16,128]{2,1,0:T(8,128)(2,1)S(1)}, u32[]{:S(2)}, u32[]{:S(2)}) collective-permute-start(bf16[4,16,128]{2,1,0:T(8,128)(2,1)S(1)} %get-tuple-element.40), channel_id=1, source_target_pairs={{0,4},{4,8},{8,12},{12,16},{16,20},{20,24},{24,28},{1,5},{5,9},{9,... | collective-permute-start | bytes 49160 | tf_op jit(solution)/shard_map/ppermute | solution.py:272
  19.0 76.5 %copy-start = (f32[4]{0:T(128)S(1)}, f32[4]{0:T(128)}, u32[]{:S(2)}) copy-start(f32[4]{0:T(128)} %conductivity_ref.1) | copy-start | bytes 52
  19.0 76.5 %copy-start.1 = (f32[4]{0:T(128)S(1)}, f32[4]{0:T(128)}, u32[]{:S(2)}) copy-start(f32[4]{0:T(128)} %capacity_ref.1) | copy-start | bytes 52
  19.0 44.3 %collective-permute-start.1 = (bf16[4,16,128]{2,1,0:T(8,128)(2,1)S(1)}, bf16[4,16,128]{2,1,0:T(8,128)(2,1)S(1)}, u32[]{:S(2)}, u32[]{:S(2)}) collective-permute-start(bf16[4,16,128]{2,1,0:T(8,128)(2,1)S(1)} %get-tuple-element.39), channel_id=1, source_target_pairs={{4,0},{8,4},{12,8},{16,12},{20,16},{24,20},{28,24},{5,1},{9,5},{13... | collective-permute-start | bytes 49160 | tf_op jit(solution)/shard_map/ppermute | solution.py:273
  68.4 21.6 %all-to-all-start.1 = ((bf16[16,64,128]{2,1,0:T(8,128)(2,1)}), bf16[16,64,128]{2,1,0:T(8,128)(2,1)S(1)}, u32[]{:S(2)}, u32[]{:S(2)}) async-start(bf16[16,64,128]{2,1,0:T(8,128)(2,1)} %cell_sum.1), calls=%async_computation.1 | async-start | bytes 524288 | tf_op jit(solution)/shard_map/all_to_all | solution.py:336
  78.9 5.9 %collective-permute-start.2 = (bf16[24,4,128]{2,1,0:T(4,128)(2,1)S(1)}, bf16[24,4,128]{2,1,0:T(4,128)(2,1)S(1)}, u32[]{:S(2)}, u32[]{:S(2)}) collective-permute-start(bf16[24,4,128]{2,1,0:T(4,128)(2,1)S(1)} %get-tuple-element.38), channel_id=1, source_target_pairs={{0,1},{1,2},{2,3},{4,5},{5,6},{6,7},{8,9},{9,10},{10,11},{12,13},{... | collective-permute-start | bytes 73736 | tf_op jit(solution)/shard_map/ppermute | solution.py:272
  81.4 5.7 %collective-permute-start.3 = (bf16[24,4,128]{2,1,0:T(4,128)(2,1)S(1)}, bf16[24,4,128]{2,1,0:T(4,128)(2,1)S(1)}, u32[]{:S(2)}, u32[]{:S(2)}) collective-permute-start(bf16[24,4,128]{2,1,0:T(4,128)(2,1)S(1)} %get-tuple-element.37), channel_id=1, source_target_pairs={{1,0},{2,1},{3,2},{5,4},{6,5},{7,6},{9,8},{10,9},{11,10},{13,12},{... | collective-permute-start | bytes 73736 | tf_op jit(solution)/shard_map/ppermute | solution.py:273
  91.1 15.5 %all-to-all-start.2 = ((bf16[16,64,128]{2,1,0:T(8,128)(2,1)}), bf16[16,64,128]{2,1,0:T(8,128)(2,1)S(1)}, u32[]{:S(2)}, u32[]{:S(2)}) async-start(bf16[16,64,128]{2,1,0:T(8,128)(2,1)} %bitcast.4), calls=%async_computation.2 | async-start | bytes 524288 | tf_op jit(solution)/shard_map/all_to_all | solution.py:359
  106.6 5.5 %collective-permute-start.4 = (bf16[3,64,128]{2,1,0:T(8,128)(2,1)S(1)}, bf16[3,64,128]{2,1,0:T(8,128)(2,1)S(1)}, u32[]{:S(2)}, u32[]{:S(2)}) collective-permute-start(bf16[3,64,128]{2,1,0:T(8,128)(2,1)S(1)} %get-tuple-element.34), channel_id=1, source_target_pairs={{0,4},{4,8},{8,12},{12,16},{16,20},{20,24},{24,28},{1,5},{5,9},{9,... | collective-permute-start | bytes 147464 | tf_op jit(solution)/shard_map/ppermute | solution.py:272
  110.0 6.2 %collective-permute-start.5 = (bf16[3,64,128]{2,1,0:T(8,128)(2,1)S(1)}, bf16[3,64,128]{2,1,0:T(8,128)(2,1)S(1)}, u32[]{:S(2)}, u32[]{:S(2)}) collective-permute-start(bf16[3,64,128]{2,1,0:T(8,128)(2,1)S(1)} %get-tuple-element.33), channel_id=1, source_target_pairs={{4,0},{8,4},{12,8},{16,12},{20,16},{24,20},{28,24},{5,1},{9,5},{13... | collective-permute-start | bytes 147464 | tf_op jit(solution)/shard_map/ppermute | solution.py:273
  116.6 6.2 %collective-permute-start.6 = (bf16[3,88,128]{2,1,0:T(8,128)(2,1)S(1)}, bf16[3,88,128]{2,1,0:T(8,128)(2,1)S(1)}, u32[]{:S(2)}, u32[]{:S(2)}) collective-permute-start(bf16[3,88,128]{2,1,0:T(8,128)(2,1)S(1)} %bitcast.14), channel_id=1, source_target_pairs={{0,1},{1,2},{2,3},{4,5},{5,6},{6,7},{8,9},{9,10},{10,11},{12,13},{... | collective-permute-start | bytes 202760 | tf_op jit(solution)/shard_map/ppermute | solution.py:369
  119.7 6.2 %collective-permute-start.7 = (bf16[3,88,128]{2,1,0:T(8,128)(2,1)S(1)}, bf16[3,88,128]{2,1,0:T(8,128)(2,1)S(1)}, u32[]{:S(2)}, u32[]{:S(2)}) collective-permute-start(bf16[3,88,128]{2,1,0:T(8,128)(2,1)S(1)} %bitcast.13), channel_id=1, source_target_pairs={{1,0},{2,1},{3,2},{5,4},{6,5},{7,6},{9,8},{10,9},{11,10},{13,12},{... | collective-permute-start | bytes 202760 | tf_op jit(solution)/shard_map/ppermute | solution.py:370

commit v6 on v5

--- a/solution.py
+++ b/solution.py
@@ -48,13 +48,21 @@
     ]
     for pull in pulls:
         pull.start()
-    before = (iota((count, count), 0) < iota((count, count), 1)).astype(F32).astype(BF16)
+    before = (iota((width, width), 0) < iota((width, width), 1)).astype(F32).astype(BF16)
     pulls[0].wait()
     owner = owner_ref[...]
     hit = owner == iota((OWNERS, count), 0)
     hit_b = hit.astype(F32).astype(BF16)
-    earlier = jnp.dot(hit_b, before, preferred_element_type=F32)
-    rank = jnp.sum(jnp.where(hit, earlier, 0.0), axis=0, keepdims=True).astype(jnp.int32)
+    blocks = [hit_b[:, k * width : (k + 1) * width] for k in range(count // width)]
+    earlier = jnp.dot(jnp.concatenate(blocks, axis=0), before, preferred_element_type=F32)
+    carry = jnp.zeros((OWNERS, 1), F32)
+    ranks = []
+    for k, block in enumerate(blocks):
+        inside = block.astype(F32)
+        prefix = earlier[k * OWNERS : (k + 1) * OWNERS] + carry
+        ranks.append(jnp.sum(inside * prefix, axis=0, keepdims=True))
+        carry = carry + jnp.sum(inside, axis=1, keepdims=True)
+    rank = jnp.concatenate(ranks, axis=1).astype(jnp.int32)
     pulls[1].wait()
     half = (rank == iota((CAP, count), 0)).astype(F32).astype(BF16)
     at_rank = jnp.concatenate([half, half], axis=0)
@@ -195,29 +203,48 @@
     lax.fori_loop(0, ext_x - 2, step, face(c_ref[0], c_ref[1]))
 
 
-def solve_kernel(mid_ref, xlo_ref, xhi_ref, ylo_ref, yhi_ref, coef_ref, out_ref, s_ref, f_ref, g_ref):
-    size_x = mid_ref.shape[0]
-    wide = xlo_ref.shape[0]
-    ext_x, comps, ye, width = s_ref.shape
-    harms = comps // 2
+def widen_kernel(mid_ref, ylo_ref, yhi_ref, s_ref, first_ref, last_ref):
+    size_x, comps, ye, width = s_ref.shape
+    wide = ylo_ref.shape[0]
     side = mid_ref.shape[1] // comps
-
-    edge = jnp.zeros((ext_x, comps, Y0 - wide, width), F32)
+    edge = jnp.zeros((size_x, comps, Y0 - wide, width), F32)
     s_ref[:, :, : Y0 - wide, :] = edge
     s_ref[:, :, ye - Y0 + wide :, :] = edge
-    for ref, start in ((xlo_ref, 0), (mid_ref, wide), (xhi_ref, wide + size_x)):
-        for c in range(comps):
-            s_ref[start : start + ref.shape[0], c, Y0 : Y0 + side, :] = ref[
-                :, c * side : (c + 1) * side, :
-            ].astype(F32)
+    for c in range(comps):
+        s_ref[:, c, Y0 : Y0 + side, :] = mid_ref[:, c * side : (c + 1) * side, :].astype(F32)
     for k in range(wide):
         for ref, start in ((ylo_ref, Y0 - wide + k), (yhi_ref, Y0 + side + k)):
-            s_ref[:, :, start, :] = ref[k].astype(F32).reshape(ext_x, comps, width)
-
-    def quotient(i, h, real_num, imag_num):
-        a = coef_ref[i, 3 + 2 * h]
-        b = coef_ref[i, 4 + 2 * h]
-        return real_num * a + imag_num * b, imag_num * a - real_num * b
+            s_ref[:, :, start, :] = ref[k].astype(F32).reshape(size_x, comps, width)
+    first_ref[...] = s_ref[:wide].reshape(wide, comps * ye, width).astype(BF16)
+    last_ref[...] = s_ref[size_x - wide :].reshape(wide, comps * ye, width).astype(BF16)
+
+
+def quotient(coef_ref, i, h, real_num, imag_num):
+    a = coef_ref[i, 3 + 2 * h]
+    b = coef_ref[i, 4 + 2 * h]
+    return real_num * a + imag_num * b, imag_num * a - real_num * b
+
+
+def sweep_row(coef_ref, source, field, i):
+    ye, width = coef_ref.shape[2:]
+
+    def numerator(c):
+        here = field(i, c)
+        fy = coef_ref[i, 1]
+        fz = coef_ref[i, 2]
+        total = source(c) + coef_ref[i, 0] * field(i + 1, c) + coef_ref[i - 1, 0] * field(i - 1, c)
+        total = total + fy * pltpu.roll(here, ye - 1, 0) + pltpu.roll(fy * here, 1, 0)
+        return total + fz * pltpu.roll(here, width - 1, 1) + pltpu.roll(fz * here, 1, 1)
+
+    made = []
+    for h in range((coef_ref.shape[1] - 3) // 2):
+        made.extend(quotient(coef_ref, i, h, numerator(2 * h), numerator(2 * h + 1)))
+    return made
+
+
+def inner_kernel(s_ref, coef_ref, f1_ref, f2_ref, f3_ref, out_ref, *, wide):
+    size_x, comps, ye, width = s_ref.shape
+    side = out_ref.shape[3]
 
     def pairs(begin, end, row):
         def step(k, _):
@@ -227,41 +254,105 @@
 
         lax.fori_loop(0, (end - begin) // 2, step, 0)
 
-    def first(i):
-        for h in range(harms):
-            f_ref[i, 2 * h], f_ref[i, 2 * h + 1] = quotient(i, h, s_ref[i, 2 * h], s_ref[i, 2 * h + 1])
-
-    pairs(0, ext_x, first)
-
-    def numerator(src, i, c):
-        here = src[i, c]
-        fy = coef_ref[i, 1]
-        fz = coef_ref[i, 2]
-        total = s_ref[i, c] + coef_ref[i, 0] * src[i + 1, c] + coef_ref[i - 1, 0] * src[i - 1, c]
-        total = total + fy * pltpu.roll(here, ye - 1, 0) + pltpu.roll(fy * here, 1, 0)
-        return total + fz * pltpu.roll(here, width - 1, 1) + pltpu.roll(fz * here, 1, 1)
+    def first(x):
+        for h in range(comps // 2):
+            f1_ref[x, 2 * h], f1_ref[x, 2 * h + 1] = quotient(
+                coef_ref, x + wide, h, s_ref[x, 2 * h], s_ref[x, 2 * h + 1]
+            )
+
+    pairs(0, size_x, first)
+
+    def made(src, x):
+        return sweep_row(
+            coef_ref, lambda c: s_ref[x, c], lambda i, c: src[i - wide, c], x + wide
+        )
 
     def sweep(src, dst, margin):
-        def row(i):
-            for h in range(harms):
-                dst[i, 2 * h], dst[i, 2 * h + 1] = quotient(
-                    i, h, numerator(src, i, 2 * h), numerator(src, i, 2 * h + 1)
+        def row(x):
+            for c, value in enumerate(made(src, x)):
+                dst[x, c] = value
+
+        pairs(margin, size_x - margin, row)
+
+    sweep(f1_ref, f2_ref, 1)
+    sweep(f2_ref, f3_ref, 2)
+
+    def last(x):
+        for c, value in enumerate(made(f3_ref, x)):
+            out_ref[c // 2, c % 2, x - wide] = value[Y0 : Y0 + side]
+
+    pairs(wide, size_x - wide, last)
+
+
+def outer_kernel(
+    xlo_ref, xhi_ref, s_ref, f1_ref, f2_ref, f3_ref, inner_ref, coef_ref, out_hbm, s_rim, g1_ref, g2_ref, g3_ref, rim_ref, sem
+):
+    size_x, comps, ye, width = s_ref.shape
+    wide = xlo_ref.shape[0]
+    side = rim_ref.shape[4]
+    ext_x = size_x + 2 * wide
+    inner = pltpu.make_async_copy(
+        inner_ref, out_hbm.at[:, :, pl.ds(wide, size_x - 2 * wide)], sem.at[0]
+    )
+    inner.start()
+    span = 2 * wide + 1
+
+    base = (0, ext_x - span)
+    s_rim[0, :wide] = xlo_ref[...].astype(F32).reshape(wide, comps, ye, width)
+    s_rim[0, wide : 2 * wide] = s_ref[:wide]
+    s_rim[1, wide + 1 :] = xhi_ref[...].astype(F32).reshape(wide, comps, ye, width)
+    s_rim[1, 1 : wide + 1] = s_ref[size_x - wide :]
+    g1_ref[0, wide : wide + 2] = f1_ref[:2]
+    g1_ref[1, wide - 1 : wide + 1] = f1_ref[size_x - 2 :]
+    g2_ref[0, wide + 1 : wide + 3] = f2_ref[1:3]
+    g2_ref[1, wide - 2 : wide] = f2_ref[size_x - 3 : size_x - 1]
+    g3_ref[0, wide + 2 : wide + 4] = f3_ref[2:4]
+    g3_ref[1, wide - 3 : wide - 1] = f3_ref[size_x - 4 : size_x - 2]
+
+    def first(k, _):
+        for part, j in ((0, k), (1, wide + 1 + k)):
+            for h in range(comps // 2):
+                g1_ref[part, j, 2 * h], g1_ref[part, j, 2 * h + 1] = quotient(
+                    coef_ref, base[part] + j, h, s_rim[part, j, 2 * h], s_rim[part, j, 2 * h + 1]
                 )
-
-        pairs(margin, ext_x - margin, row)
-
-    sweep(f_ref, g_ref, 1)
-    sweep(g_ref, f_ref, 2)
-
-    def last(i):
-        for h in range(harms):
-            real_out, imag_out = quotient(
-                i, h, numerator(f_ref, i, 2 * h), numerator(f_ref, i, 2 * h + 1)
-            )
-            out_ref[h, 0, i - wide] = real_out[Y0 : Y0 + side]
-            out_ref[h, 1, i - wide] = imag_out[Y0 : Y0 + side]
-
-    pairs(wide, wide + size_x, last)
+        return 0
+
+    lax.fori_loop(0, wide, first, 0)
+
+    def made(src, part, j):
+        return sweep_row(
+            coef_ref,
+            lambda c: s_rim[part, j, c],
+            lambda i, c: src[part, i - base[part], c],
+            base[part] + j,
+        )
+
+    def sweep(src, dst, margin):
+        def step(k, _):
+            for part, j in ((0, margin + k), (1, wide + 1 - margin + k)):
+                for c, value in enumerate(made(src, part, j)):
+                    dst[part, j, c] = value
+            return 0
+
+        lax.fori_loop(0, wide, step, 0)
+
+    sweep(g1_ref, g2_ref, 1)
+    sweep(g2_ref, g3_ref, 2)
+
+    def last(k, _):
+        for part, j in ((0, wide + k), (1, 1 + k)):
+            for c, value in enumerate(made(g3_ref, part, j)):
+                rim_ref[part, c // 2, c % 2, k] = value[Y0 : Y0 + side]
+        return 0
+
+    lax.fori_loop(0, wide, last, 0)
+    low = pltpu.make_async_copy(rim_ref.at[0], out_hbm.at[:, :, pl.ds(0, wide)], sem.at[1])
+    high = pltpu.make_async_copy(rim_ref.at[1], out_hbm.at[:, :, pl.ds(size_x - wide, wide)], sem.at[2])
+    low.start()
+    high.start()
+    inner.wait()
+    low.wait()
+    high.wait()
 
 
 def swap(block, axis, dim, width):
@@ -336,6 +427,22 @@
     gathered = lax.all_to_all(sums, "tm", split_axis=0, concat_axis=0, tiled=True)
     gathered, ids, south, north = lax.optimization_barrier((gathered, ids, south, north))
     ids = jnp.concatenate([south, ids, north], axis=1).astype(jnp.int32)
+    harmonic = pl.pallas_call(
+        dft_kernel,
+        out_shape=jax.ShapeDtypeStruct((TIME, size_y, width), BF16),
+        in_specs=[vmem] * 2,
+        out_specs=vmem,
+        compiler_params=params,
+        name="dft",
+    )(weights, gathered.reshape(TIME, size_y, width))
+    harmonic = harmonic.reshape(steps, comps * size_y, width)
+    source = lax.all_to_all(harmonic, "tm", split_axis=0, concat_axis=0, tiled=True)
+    source, ids = lax.optimization_barrier((source, ids))
+
+    rows = source.reshape(size_x, comps, size_y, width)
+    rows = jnp.concatenate([rows[:, :, :WIDE], rows[:, :, size_y - WIDE :]], axis=2)
+    rows = jnp.transpose(rows, (2, 0, 1, 3)).reshape(2 * WIDE, size_x * comps, width)
+    ylo, yhi = swap(rows, "sy", 0, WIDE)
     harm_index = lax.axis_index("tm") * harms + jnp.arange(harms, dtype=jnp.int32)
     omega = omega_step * harm_index.astype(F32)
     coef = pl.pallas_call(
@@ -347,37 +454,45 @@
         compiler_params=params,
         name="coef",
     )(omega, conductivity, capacity, ids)
-    harmonic = pl.pallas_call(
-        dft_kernel,
-        out_shape=jax.ShapeDtypeStruct((TIME, size_y, width), BF16),
+    ylo, yhi, coef = lax.optimization_barrier((ylo, yhi, coef))
+    widened = jax.ShapeDtypeStruct((size_x, comps, YE, width), F32)
+    strip = jax.ShapeDtypeStruct((WIDE, comps * YE, width), BF16)
+    source, first_rows, last_rows = pl.pallas_call(
+        widen_kernel,
+        out_shape=[widened, strip, strip],
+        in_specs=[vmem] * 3,
+        out_specs=[vmem] * 3,
+        compiler_params=params,
+        name="widen",
+    )(source, ylo, yhi)
+    count_x = lax.axis_size("sx")
+    forward = [(i, i + 1) for i in range(count_x - 1)]
+    backward = [(target, start) for start, target in forward]
+    xlo = lax.ppermute(last_rows, "sx", forward)
+    xhi = lax.ppermute(first_rows, "sx", backward)
+    field1, field2, field3, inner = pl.pallas_call(
+        lambda *refs: inner_kernel(*refs, wide=WIDE),
+        out_shape=[widened] * 3
+        + [jax.ShapeDtypeStruct((harms, 2, size_x - 2 * WIDE, size_y, width), F32)],
         in_specs=[vmem] * 2,
-        out_specs=vmem,
-        compiler_params=params,
-        name="dft",
-    )(weights, gathered.reshape(TIME, size_y, width))
-    harmonic = harmonic.reshape(steps, comps * size_y, width)
-    source = lax.all_to_all(harmonic, "tm", split_axis=0, concat_axis=0, tiled=True)
-    source, coef = lax.optimization_barrier((source, coef))
-
-    xlo, xhi = swap(source, "sx", 0, WIDE)
-    rows = jnp.concatenate([xlo, source, xhi], axis=0).reshape(ext_x, comps, size_y, width)
-    rows = jnp.concatenate([rows[:, :, :WIDE], rows[:, :, size_y - WIDE :]], axis=2)
-    rows = jnp.transpose(rows, (2, 0, 1, 3)).reshape(2 * WIDE, ext_x * comps, width)
-    count_y = lax.axis_size("sy")
-    forward = [(i, i + 1) for i in range(count_y - 1)]
-    backward = [(target, start) for start, target in forward]
-    ylo = lax.ppermute(rows[WIDE:], "sy", forward)
-    yhi = lax.ppermute(rows[:WIDE], "sy", backward)
-    field = pl.pallas_call(
-        solve_kernel,
-        out_shape=jax.ShapeDtypeStruct((harms, 2, size_x, size_y, width), F32),
-        in_specs=[vmem] * 6,
-        out_specs=vmem,
-        scratch_shapes=[pltpu.VMEM((ext_x, comps, YE, width), F32)] * 3,
-        compiler_params=params,
-        name="solve",
-    )(source, xlo, xhi, ylo, yhi, coef)
-    return field
+        out_specs=[vmem] * 4,
+        compiler_params=params,
+        name="inner",
+    )(source, coef)
+    rim = pltpu.VMEM((2, 2 * WIDE + 1, comps, YE, width), F32)
+    return pl.pallas_call(
+        outer_kernel,
+        out_shape=pltpu.HBM((harms, 2, size_x, size_y, width), F32),
+        in_specs=[vmem] * 8,
+        out_specs=hbm,
+        scratch_shapes=[rim] * 4
+        + [
+            pltpu.VMEM((2, harms, 2, WIDE, size_y, width), F32),
+            pltpu.SemaphoreType.DMA((3,)),
+        ],
+        compiler_params=params,
+        name="outer",
+    )(xlo, xhi, source, field1, field2, field3, inner, coef)
 
 
 def solution(mesh):

time: 131 us -> 129 us (0.985)
  the two profiles are of different devices: /device:TPU:2 before, /device:TPU:10 now
where the time goes in v6:
time: 129 us
  waiting for transfers between devices  63 us (49%)
  starting transfers between devices  48.5 us (38%)
  Pallas kernels  16.3 us (13%)
    ppermute x3, waiting for transfers between devices, swap(): lax.ppermute(lax.slice_in_dim(block, 0, width, axis=dim), axis, backward)  40.1 us
    all_to_all x1, waiting for transfers between devices, body(): lax.all_to_all(harmonic, 'tm', split_axis=0, concat_axis=0, tiled=True)  11.1 us
    all_to_all x1, starting transfers between devices, body(): lax.all_to_all(sums, 'tm', split_axis=0, concat_axis=0, tiled=True)  10.6 us
    all_to_all x1, starting transfers between devices, body(): lax.all_to_all(packed, ('sx', 'sy'), split_axis=0, concat_axis=0, tiled=T...  10.3 us
    ppermute x3, starting transfers between devices, swap(): lax.ppermute(lax.slice_in_dim(block, size - width, size, axis=dim), axis,...  10.1 us
    ppermute x3, starting transfers between devices, swap(): lax.ppermute(lax.slice_in_dim(block, 0, width, axis=dim), axis, backward)  7.39 us
    all_to_all x1, waiting for transfers between devices, body(): lax.all_to_all(packed, ('sx', 'sy'), split_axis=0, concat_axis=0, tiled=T...  4.68 us
    pallas_call x1, Pallas kernels, body(): pl.pallas_call(pack_kernel, out_shape=pltpu.HBM((OWNERS, times * CAP + 8,...  4.45 us
  transfers between devices with their start and end apart: 11, of which 6 were waited for; matrix products, arithmetic and copies ran while one was open for 0% of the time, Pallas kernels for 6%

profile of v6, /device:TPU:10, one launch (start us, length us, event | category | flops | bytes accessed | tf_op | source)
XLA Modules:
  0.0 128.6 jit_solution(5766731827819465590)
XLA Ops:
  0.0 4.4 %pack.1 = bf16[32,264,128]{2,1,0:T(8,128)(2,1)} custom-call(bf16[4,1024,128]{2,1,0:T(8,128)(2,1)} %wall_hbm.1, s32[1,1024]{1,0:T(1,128)} %bitcast.15, s32[1,1024]{1,0:T(1,128)} %bitcast.16), custom_call_target="tpu_custom_call" | custom-call | tf_op jit(solution)/shard_map/pack/pallas_call | solution.py:380
  4.5 10.3 %all-to-all-start = ((bf16[32,264,128]{2,1,0:T(8,128)(2,1)}), bf16[32,264,128]{2,1,0:T(8,128)(2,1)S(1)}, u32[]{:S(2)}, u32[]{:S(2)}) async-start(bf16[32,264,128]{2,1,0:T(8,128)(2,1)} %pack.1), calls=%async_computation | async-start | bytes 4325376 | tf_op jit(solution)/shard_map/all_to_all | solution.py:401
  14.9 0.5 weights.1.weights_ref
  15.4 2.5 %collective-permute-start.1 = (bf16[4,16,128]{2,1,0:T(8,128)(2,1)S(1)}, bf16[4,16,128]{2,1,0:T(8,128)(2,1)S(1)}, u32[]{:S(2)}, u32[]{:S(2)}) collective-permute-start(bf16[4,16,128]{2,1,0:T(8,128)(2,1)S(1)} %get-tuple-element.57), channel_id=1, source_target_pairs={{4,0},{8,4},{12,8},{16,12},{20,16},{24,20},{28,24},{5,1},{9,5},{13... | collective-permute-start | bytes 49160 | tf_op jit(solution)/shard_map/ppermute | solution.py:364
  17.9 3.4 %collective-permute-start = (bf16[4,16,128]{2,1,0:T(8,128)(2,1)S(1)}, bf16[4,16,128]{2,1,0:T(8,128)(2,1)S(1)}, u32[]{:S(2)}, u32[]{:S(2)}) collective-permute-start(bf16[4,16,128]{2,1,0:T(8,128)(2,1)S(1)} %get-tuple-element.58), channel_id=1, source_target_pairs={{0,4},{4,8},{8,12},{12,16},{16,20},{20,24},{24,28},{1,5},{5,9},{9,... | collective-permute-start | bytes 49160 | tf_op jit(solution)/shard_map/ppermute | solution.py:363
  21.3 40.1 %collective-permute-done.1 = bf16[4,16,128]{2,1,0:T(8,128)(2,1)S(1)} collective-permute-done((bf16[4,16,128]{2,1,0:T(8,128)(2,1)S(1)}, bf16[4,16,128]{2,1,0:T(8,128)(2,1)S(1)}, u32[]{:S(2)}, u32[]{:S(2)}) %collective-permute-start.1) | collective-permute-done | bytes 16416 | tf_op jit(solution)/shard_map/ppermute | solution.py:364
  61.4 4.7 %all-to-all-done.refs_0_ = bf16[32,264,128]{2,1,0:T(8,128)(2,1)S(1)} async-done(((bf16[32,264,128]{2,1,0:T(8,128)(2,1)}), bf16[32,264,128]{2,1,0:T(8,128)(2,1)S(1)}, u32[]{:S(2)}, u32[]{:S(2)}) %all-to-all-start) | async-done | bytes 2162720 | tf_op jit(solution)/shard_map/all_to_all | solution.py:401
  66.0 1.4 %cell_sum.1 = bf16[16,64,128]{2,1,0:T(8,128)(2,1)} custom-call(bf16[32,264,128]{2,1,0:T(8,128)(2,1)S(1)} %all-to-all-done.refs_0_), custom_call_target="tpu_custom_call" | custom-call | tf_op jit(solution)/shard_map/cell_sum/pallas_call | solution.py:419
  67.5 10.6 %all-to-all-start.1 = ((bf16[16,64,128]{2,1,0:T(8,128)(2,1)}), bf16[16,64,128]{2,1,0:T(8,128)(2,1)S(1)}, u32[]{:S(2)}, u32[]{:S(2)}) async-start(bf16[16,64,128]{2,1,0:T(8,128)(2,1)} %cell_sum.1), calls=%async_computation.1 | async-start | bytes 524288 | tf_op jit(solution)/shard_map/all_to_all | solution.py:427
  78.1 2.5 %collective-permute-start.3 = (bf16[24,4,128]{2,1,0:T(4,128)(2,1)S(1)}, bf16[24,4,128]{2,1,0:T(4,128)(2,1)S(1)}, u32[]{:S(2)}, u32[]{:S(2)}) collective-permute-start(bf16[24,4,128]{2,1,0:T(4,128)(2,1)S(1)} %get-tuple-element.55), channel_id=1, source_target_pairs={{1,0},{2,1},{3,2},{5,4},{6,5},{7,6},{9,8},{10,9},{11,10},{13,12},{... | collective-permute-start | bytes 73736 | tf_op jit(solution)/shard_map/ppermute | solution.py:364
  80.5 3.4 %collective-permute-start.2 = (bf16[24,4,128]{2,1,0:T(4,128)(2,1)S(1)}, bf16[24,4,128]{2,1,0:T(4,128)(2,1)S(1)}, u32[]{:S(2)}, u32[]{:S(2)}) collective-permute-start(bf16[24,4,128]{2,1,0:T(4,128)(2,1)S(1)} %get-tuple-element.56), channel_id=1, source_target_pairs={{0,1},{1,2},{2,3},{4,5},{5,6},{6,7},{8,9},{9,10},{10,11},{12,13},{... | collective-permute-start | bytes 73736 | tf_op jit(solution)/shard_map/ppermute | solution.py:363
  83.9 2.3 %collective-permute-done.2 = bf16[24,4,128]{2,1,0:T(4,128)(2,1)S(1)} collective-permute-done((bf16[24,4,128]{2,1,0:T(4,128)(2,1)S(1)}, bf16[24,4,128]{2,1,0:T(4,128)(2,1)S(1)}, u32[]{:S(2)}, u32[]{:S(2)}) %collective-permute-start.2) | collective-permute-done | bytes 24608 | tf_op jit(solution)/shard_map/ppermute | solution.py:363
  86.3 2.9 %all-to-all-done.1 = bf16[16,64,128]{2,1,0:T(8,128)(2,1)S(1)} async-done(((bf16[16,64,128]{2,1,0:T(8,128)(2,1)}), bf16[16,64,128]{2,1,0:T(8,128)(2,1)S(1)}, u32[]{:S(2)}, u32[]{:S(2)}) %all-to-all-start.1) | async-done | bytes 262176 | tf_op jit(solution)/shard_map/all_to_all | solution.py:427
  89.2 1.0 dft.1
  90.2 4.3 %all-to-all-start.2 = ((bf16[16,64,128]{2,1,0:T(8,128)(2,1)}), bf16[16,64,128]{2,1,0:T(8,128)(2,1)S(1)}, u32[]{:S(2)}, u32[]{:S(2)}) async-start(bf16[16,64,128]{2,1,0:T(8,128)(2,1)} %bitcast.4), calls=%async_computation.2 | async-start | bytes 524288 | tf_op jit(solution)/shard_map/all_to_all | solution.py:439
  94.6 11.1 %all-to-all-done.2.mid_ref = bf16[16,64,128]{2,1,0:T(8,128)(2,1)S(1)} async-done(((bf16[16,64,128]{2,1,0:T(8,128)(2,1)}), bf16[16,64,128]{2,1,0:T(8,128)(2,1)S(1)}, u32[]{:S(2)}, u32[]{:S(2)}) %all-to-all-start.2) | async-done | bytes 262176 | tf_op jit(solution)/shard_map/all_to_all | solution.py:439
  105.9 3.4 %collective-permute-start.4 = (bf16[3,64,128]{2,1,0:T(8,128)(2,1)S(1)}, bf16[3,64,128]{2,1,0:T(8,128)(2,1)S(1)}, u32[]{:S(2)}, u32[]{:S(2)}) collective-permute-start(bf16[3,64,128]{2,1,0:T(8,128)(2,1)S(1)} %bitcast.14), channel_id=1, source_target_pairs={{0,1},{1,2},{2,3},{4,5},{5,6},{6,7},{8,9},{9,10},{10,11},{12,13},{... | collective-permute-start | bytes 147464 | tf_op jit(solution)/shard_map/ppermute | solution.py:363
  109.3 2.5 %collective-permute-start.5 = (bf16[3,64,128]{2,1,0:T(8,128)(2,1)S(1)}, bf16[3,64,128]{2,1,0:T(8,128)(2,1)S(1)}, u32[]{:S(2)}, u32[]{:S(2)}) collective-permute-start(bf16[3,64,128]{2,1,0:T(8,128)(2,1)S(1)} %bitcast.13), channel_id=1, source_target_pairs={{1,0},{2,1},{3,2},{5,4},{6,5},{7,6},{9,8},{10,9},{11,10},{13,12},{... | collective-permute-start | bytes 147464 | tf_op jit(solution)/shard_map/ppermute | solution.py:364
  111.8 4.3 %coef.1.refs_1_.coef_ref = f32[22,7,24,128]{3,2,1,0:T(8,128)S(1)} custom-call(f32[2]{0:T(128)S(1)} %convert_multiply_fusion.omega_ref, f32[4]{0:T(128)S(1)} %copy-done, f32[4]{0:T(128)S(1)} %copy-done.1, s32[24,24,128]{2,1,0:T(8,128)S(1)} %maximum_convert_fusion.ids_ref), custom_call_target="tpu_custom_call" | custom-call | tf_op jit(solution)/shard_map/coef/pallas_call | solution.py:448
  116.4 4.0 %collective-permute-start.6 = (bf16[3,96,128]{2,1,0:T(8,128)(2,1)S(1)}, bf16[3,96,128]{2,1,0:T(8,128)(2,1)S(1)}, u32[]{:S(2)}, u32[]{:S(2)}) collective-permute-start(bf16[3,96,128]{2,1,0:T(8,128)(2,1)S(1)} %get-tuple-element.43), channel_id=1, source_target_pairs={{0,4},{4,8},{8,12},{12,16},{16,20},{20,24},{24,28},{1,5},{5,9},{9,... | collective-permute-start | bytes 221192 | tf_op jit(solution)/shard_map/ppermute | solution.py:471
  120.3 1.9 %collective-permute-start.7 = (bf16[3,96,128]{2,1,0:T(8,128)(2,1)S(1)}, bf16[3,96,128]{2,1,0:T(8,128)(2,1)S(1)}, u32[]{:S(2)}, u32[]{:S(2)}) collective-permute-start(bf16[3,96,128]{2,1,0:T(8,128)(2,1)S(1)} %get-tuple-element.44), channel_id=1, source_target_pairs={{4,0},{8,4},{12,8},{16,12},{20,16},{24,20},{28,24},{5,1},{9,5},{13... | collective-permute-start | bytes 221192 | tf_op jit(solution)/shard_map/ppermute | solution.py:472
  122.3 2.4 %inner.1 = (f32[16,4,24,128]{3,2,1,0:T(8,128)S(1)}, f32[16,4,24,128]{3,2,1,0:T(8,128)S(1)}, f32[16,4,24,128]{3,2,1,0:T(8,128)S(1)}, f32[2,2,10,16,128]{4,3,2,1,0:T(8,128)S(1)}) custom-call(f32[16,4,24,128]{3,2,1,0:T(8,128)S(1)} %get-tuple-element.45.refs_0_.s_ref, f32[22,7,24,128]{3,2,1,0:T(8,128)S(1)} %coef.1.refs_1_.coef_ref), custom_call_target="tpu_custom_call" | custom-call | tf_op jit(solution)/shard_map/inner/pallas_call | solution.py:473
  124.7 1.9 %collective-permute-done.7.xhi_ref = bf16[3,96,128]{2,1,0:T(8,128)(2,1)S(1)} collective-permute-done((bf16[3,96,128]{2,1,0:T(8,128)(2,1)S(1)}, bf16[3,96,128]{2,1,0:T(8,128)(2,1)S(1)}, u32[]{:S(2)}, u32[]{:S(2)}) %collective-permute-start.7) | collective-permute-done | bytes 73760 | tf_op jit(solution)/shard_map/ppermute | solution.py:472
  126.6 2.0 %outer.1 = f32[2,2,16,16,128]{4,3,2,1,0:T(8,128)} custom-call(bf16[3,96,128]{2,1,0:T(8,128)(2,1)S(1)} %collective-permute-done.6.xlo_ref, bf16[3,96,128]{2,1,0:T(8,128)(2,1)S(1)} %collective-permute-done.7.xhi_ref, f32[16,4,24,128]{3,2,1,0:T(8,128)S(1)} %get-tuple-element.45.refs_0_.s_ref, f32[16,4,24,128]{3,2,1,0:T(8,128)S(1)} %get-tuple-element.47.f1_ref, ...), custom_call_target="tpu_custom_call" | custom-call | tf_op jit(solution)/shard_map/outer/pallas_call | solution.py:483
  (26 shorter events, 0.7 us)
Async XLA Ops:
  4.5 10.9 %copy-start.2 = (s32[16,16,128]{2,1,0:T(8,128)S(1)}, s32[16,16,128]{2,1,0:T(8,128)}, u32[]{:S(2)}) copy-start(s32[16,16,128]{2,1,0:T(8,128)} %param.9) | copy-start | bytes 393220
  4.5 61.6 %all-to-all-start = ((bf16[32,264,128]{2,1,0:T(8,128)(2,1)}), bf16[32,264,128]{2,1,0:T(8,128)(2,1)S(1)}, u32[]{:S(2)}, u32[]{:S(2)}) async-start(bf16[32,264,128]{2,1,0:T(8,128)(2,1)} %pack.1), calls=%async_computation | async-start | bytes 4325376 | tf_op jit(solution)/shard_map/all_to_all | solution.py:401
  15.4 45.9 %collective-permute-start.1 = (bf16[4,16,128]{2,1,0:T(8,128)(2,1)S(1)}, bf16[4,16,128]{2,1,0:T(8,128)(2,1)S(1)}, u32[]{:S(2)}, u32[]{:S(2)}) collective-permute-start(bf16[4,16,128]{2,1,0:T(8,128)(2,1)S(1)} %get-tuple-element.57), channel_id=1, source_target_pairs={{4,0},{8,4},{12,8},{16,12},{20,16},{24,20},{28,24},{5,1},{9,5},{13... | collective-permute-start | bytes 49160 | tf_op jit(solution)/shard_map/ppermute | solution.py:364
  17.9 43.5 %collective-permute-start = (bf16[4,16,128]{2,1,0:T(8,128)(2,1)S(1)}, bf16[4,16,128]{2,1,0:T(8,128)(2,1)S(1)}, u32[]{:S(2)}, u32[]{:S(2)}) collective-permute-start(bf16[4,16,128]{2,1,0:T(8,128)(2,1)S(1)} %get-tuple-element.58), channel_id=1, source_target_pairs={{0,4},{4,8},{8,12},{12,16},{16,20},{20,24},{24,28},{1,5},{5,9},{9,... | collective-permute-start | bytes 49160 | tf_op jit(solution)/shard_map/ppermute | solution.py:363
  67.5 44.3 %copy-start = (f32[4]{0:T(128)S(1)}, f32[4]{0:T(128)}, u32[]{:S(2)}) copy-start(f32[4]{0:T(128)} %conductivity_ref.1) | copy-start | bytes 52
  67.5 44.3 %copy-start.1 = (f32[4]{0:T(128)S(1)}, f32[4]{0:T(128)}, u32[]{:S(2)}) copy-start(f32[4]{0:T(128)} %capacity_ref.1) | copy-start | bytes 52
  67.5 21.7 %all-to-all-start.1 = ((bf16[16,64,128]{2,1,0:T(8,128)(2,1)}), bf16[16,64,128]{2,1,0:T(8,128)(2,1)S(1)}, u32[]{:S(2)}, u32[]{:S(2)}) async-start(bf16[16,64,128]{2,1,0:T(8,128)(2,1)} %cell_sum.1), calls=%async_computation.1 | async-start | bytes 524288 | tf_op jit(solution)/shard_map/all_to_all | solution.py:427
  78.1 5.9 %collective-permute-start.3 = (bf16[24,4,128]{2,1,0:T(4,128)(2,1)S(1)}, bf16[24,4,128]{2,1,0:T(4,128)(2,1)S(1)}, u32[]{:S(2)}, u32[]{:S(2)}) collective-permute-start(bf16[24,4,128]{2,1,0:T(4,128)(2,1)S(1)} %get-tuple-element.55), channel_id=1, source_target_pairs={{1,0},{2,1},{3,2},{5,4},{6,5},{7,6},{9,8},{10,9},{11,10},{13,12},{... | collective-permute-start | bytes 73736 | tf_op jit(solution)/shard_map/ppermute | solution.py:364
  80.5 5.7 %collective-permute-start.2 = (bf16[24,4,128]{2,1,0:T(4,128)(2,1)S(1)}, bf16[24,4,128]{2,1,0:T(4,128)(2,1)S(1)}, u32[]{:S(2)}, u32[]{:S(2)}) collective-permute-start(bf16[24,4,128]{2,1,0:T(4,128)(2,1)S(1)} %get-tuple-element.56), channel_id=1, source_target_pairs={{0,1},{1,2},{2,3},{4,5},{5,6},{6,7},{8,9},{9,10},{10,11},{12,13},{... | collective-permute-start | bytes 73736 | tf_op jit(solution)/shard_map/ppermute | solution.py:363
  90.2 15.5 %all-to-all-start.2 = ((bf16[16,64,128]{2,1,0:T(8,128)(2,1)}), bf16[16,64,128]{2,1,0:T(8,128)(2,1)S(1)}, u32[]{:S(2)}, u32[]{:S(2)}) async-start(bf16[16,64,128]{2,1,0:T(8,128)(2,1)} %bitcast.4), calls=%async_computation.2 | async-start | bytes 524288 | tf_op jit(solution)/shard_map/all_to_all | solution.py:439
  105.9 10.2 %collective-permute-start.4 = (bf16[3,64,128]{2,1,0:T(8,128)(2,1)S(1)}, bf16[3,64,128]{2,1,0:T(8,128)(2,1)S(1)}, u32[]{:S(2)}, u32[]{:S(2)}) collective-permute-start(bf16[3,64,128]{2,1,0:T(8,128)(2,1)S(1)} %bitcast.14), channel_id=1, source_target_pairs={{0,1},{1,2},{2,3},{4,5},{5,6},{6,7},{8,9},{9,10},{10,11},{12,13},{... | collective-permute-start | bytes 147464 | tf_op jit(solution)/shard_map/ppermute | solution.py:363
  109.3 6.8 %collective-permute-start.5 = (bf16[3,64,128]{2,1,0:T(8,128)(2,1)S(1)}, bf16[3,64,128]{2,1,0:T(8,128)(2,1)S(1)}, u32[]{:S(2)}, u32[]{:S(2)}) collective-permute-start(bf16[3,64,128]{2,1,0:T(8,128)(2,1)S(1)} %bitcast.13), channel_id=1, source_target_pairs={{1,0},{2,1},{3,2},{5,4},{6,5},{7,6},{9,8},{10,9},{11,10},{13,12},{... | collective-permute-start | bytes 147464 | tf_op jit(solution)/shard_map/ppermute | solution.py:364
  116.4 8.4 %collective-permute-start.6 = (bf16[3,96,128]{2,1,0:T(8,128)(2,1)S(1)}, bf16[3,96,128]{2,1,0:T(8,128)(2,1)S(1)}, u32[]{:S(2)}, u32[]{:S(2)}) collective-permute-start(bf16[3,96,128]{2,1,0:T(8,128)(2,1)S(1)} %get-tuple-element.43), channel_id=1, source_target_pairs={{0,4},{4,8},{8,12},{12,16},{16,20},{20,24},{24,28},{1,5},{5,9},{9,... | collective-permute-start | bytes 221192 | tf_op jit(solution)/shard_map/ppermute | solution.py:471
  120.3 6.2 %collective-permute-start.7 = (bf16[3,96,128]{2,1,0:T(8,128)(2,1)S(1)}, bf16[3,96,128]{2,1,0:T(8,128)(2,1)S(1)}, u32[]{:S(2)}, u32[]{:S(2)}) collective-permute-start(bf16[3,96,128]{2,1,0:T(8,128)(2,1)S(1)} %get-tuple-element.44), channel_id=1, source_target_pairs={{4,0},{8,4},{12,8},{16,12},{20,16},{24,20},{28,24},{5,1},{9,5},{13... | collective-permute-start | bytes 221192 | tf_op jit(solution)/shard_map/ppermute | solution.py:472

commit v7 on v6

--- a/solution.py
+++ b/solution.py
@@ -154,8 +154,12 @@
     out_ref[...] = made.astype(BF16)
 
 
-def coef_kernel(omega_ref, conductivity_ref, capacity_ref, ids_ref, coef_ref, c_ref):
-    ext_x, ye, width = ids_ref.shape
+def coef_kernel(
+    omega_ref, conductivity_ref, capacity_ref, south_ref, ids_ref, north_ref, coef_ref, mark_ref, c_ref
+):
+    ext_x, side, width = ids_ref.shape
+    edge = south_ref.shape[1]
+    ye = side + 2 * edge
     harms = omega_ref.shape[0]
 
     def table(ids, values):
@@ -164,11 +168,16 @@
             value = jnp.where(ids == m + 1, values[m], value)
         return value
 
-    def conduct_step(i, _):
-        c_ref[i] = table(ids_ref[i], conductivity_ref)
+    mark_ref[:, :edge] = south_ref[...].astype(F32)
+    mark_ref[:, edge : edge + side] = ids_ref[...].astype(F32)
+    mark_ref[:, edge + side :] = north_ref[...].astype(F32)
+
+    def conduct_step(k, _):
+        for i in (4 * k, 4 * k + 1, 4 * k + 2, 4 * k + 3):
+            c_ref[i] = table(mark_ref[i], conductivity_ref)
         return 0
 
-    lax.fori_loop(0, ext_x, conduct_step, 0)
+    lax.fori_loop(0, ext_x // 4, conduct_step, 0)
 
     def face(a, b):
         b = jnp.where(b > 0, b, a)
@@ -177,21 +186,20 @@
 
     lane = iota((ye, width), 1)
 
-    def step(i, prev_x):
+    def row(i, prev_x):
         c = c_ref[i + 1]
-        after = c_ref[i + 2]
-        next_x = face(c, after)
+        next_x = face(c, c_ref[i + 2])
         next_y = face(c, pltpu.roll(c, ye - 1, 0))
         next_z = face(c, jnp.where(lane == width - 1, 0.0, pltpu.roll(c, width - 1, 1)))
-        prev_y = face(c, pltpu.roll(c, 1, 0))
+        prev_y = jnp.where(pltpu.roll(c, 1, 0) > 0, pltpu.roll(next_y, 1, 0), c)
         prev_z = jnp.where(lane == 0, c, pltpu.roll(next_z, 1, 1))
         real_den = next_x + jnp.where(c_ref[i] > 0, prev_x, c) + next_y + prev_y + next_z + prev_z
         coef_ref[i, 0] = next_x
         coef_ref[i, 1] = next_y
         coef_ref[i, 2] = jnp.where(lane == width - 1, 0.0, next_z)
-        ids = ids_ref[i + 1]
-        heat = table(ids, capacity_ref)
-        inside = ids > 0
+        mark = mark_ref[i + 1]
+        heat = table(mark, capacity_ref)
+        inside = mark > 0
         for h in range(harms):
             imag_den = omega_ref[h] * heat
             modulus = real_den * real_den + imag_den * imag_den
@@ -200,7 +208,10 @@
             coef_ref[i, 4 + 2 * h] = imag_den * inverse
         return next_x
 
-    lax.fori_loop(0, ext_x - 2, step, face(c_ref[0], c_ref[1]))
+    def step(k, prev_x):
+        return row(2 * k + 1, row(2 * k, prev_x))
+
+    lax.fori_loop(0, (ext_x - 2) // 2, step, face(c_ref[0], c_ref[1]))
 
 
 def widen_kernel(mid_ref, ylo_ref, yhi_ref, s_ref, first_ref, last_ref):
@@ -426,7 +437,6 @@
     )(received)
     gathered = lax.all_to_all(sums, "tm", split_axis=0, concat_axis=0, tiled=True)
     gathered, ids, south, north = lax.optimization_barrier((gathered, ids, south, north))
-    ids = jnp.concatenate([south, ids, north], axis=1).astype(jnp.int32)
     harmonic = pl.pallas_call(
         dft_kernel,
         out_shape=jax.ShapeDtypeStruct((TIME, size_y, width), BF16),
@@ -437,7 +447,7 @@
     )(weights, gathered.reshape(TIME, size_y, width))
     harmonic = harmonic.reshape(steps, comps * size_y, width)
     source = lax.all_to_all(harmonic, "tm", split_axis=0, concat_axis=0, tiled=True)
-    source, ids = lax.optimization_barrier((source, ids))
+    source, south, ids, north = lax.optimization_barrier((source, south, ids, north))
 
     rows = source.reshape(size_x, comps, size_y, width)
     rows = jnp.concatenate([rows[:, :, :WIDE], rows[:, :, size_y - WIDE :]], axis=2)
@@ -448,12 +458,12 @@
     coef = pl.pallas_call(
         coef_kernel,
         out_shape=jax.ShapeDtypeStruct((ext_x, 3 + 2 * harms, YE, width), F32),
-        in_specs=[smem, smem, smem, vmem],
+        in_specs=[smem] * 3 + [vmem] * 3,
         out_specs=vmem,
-        scratch_shapes=[pltpu.VMEM((ext_x + 2, YE, width), F32)],
+        scratch_shapes=[pltpu.VMEM((ext_x + 2, YE, width), F32)] * 2,
         compiler_params=params,
         name="coef",
-    )(omega, conductivity, capacity, ids)
+    )(omega, conductivity, capacity, south, ids, north)
     ylo, yhi, coef = lax.optimization_barrier((ylo, yhi, coef))
     widened = jax.ShapeDtypeStruct((size_x, comps, YE, width), F32)
     strip = jax.ShapeDtypeStruct((WIDE, comps * YE, width), BF16)

time: 129 us -> 129 us (level)
  the two profiles are of different devices: /device:TPU:10 before, /device:TPU:8 now
where the time goes in v7:
time: 129 us; the launch traced here: 128 us
  waiting for transfers between devices  65.5 us (51%)
  starting transfers between devices  47.2 us (37%)
  Pallas kernels  14.5 us (11%)
    ppermute x3, waiting for transfers between devices, swap(): lax.ppermute(lax.slice_in_dim(block, 0, width, axis=dim), axis, backward)  42.5 us
    ppermute x3, starting transfers between devices, swap(): lax.ppermute(lax.slice_in_dim(block, size - width, size, axis=dim), axis,...  12.2 us
    all_to_all x1, waiting for transfers between devices, body(): lax.all_to_all(harmonic, 'tm', split_axis=0, concat_axis=0, tiled=True)  11.3 us
    all_to_all x1, starting transfers between devices, body(): lax.all_to_all(sums, 'tm', split_axis=0, concat_axis=0, tiled=True)  10.6 us
    all_to_all x1, starting transfers between devices, body(): lax.all_to_all(packed, ('sx', 'sy'), split_axis=0, concat_axis=0, tiled=T...  10.3 us
    ppermute x3, starting transfers between devices, swap(): lax.ppermute(lax.slice_in_dim(block, 0, width, axis=dim), axis, backward)  4.72 us
    all_to_all x1, waiting for transfers between devices, body(): lax.all_to_all(packed, ('sx', 'sy'), split_axis=0, concat_axis=0, tiled=T...  4.61 us
    pallas_call x1, Pallas kernels, body(): pl.pallas_call(pack_kernel, out_shape=pltpu.HBM((OWNERS, times * CAP + 8,...  4.45 us
  transfers between devices with their start and end apart: 11, of which 7 were waited for; matrix products, arithmetic and copies ran while one was open for 0% of the time, Pallas kernels for 4%

profile of v7, /device:TPU:8, one launch (start us, length us, event | category | flops | bytes accessed | tf_op | source)
XLA Modules:
  0.0 127.9 jit_solution(6868035681944807636)
XLA Ops:
  0.0 4.4 %pack.1 = bf16[32,264,128]{2,1,0:T(8,128)(2,1)} custom-call(bf16[4,1024,128]{2,1,0:T(8,128)(2,1)} %wall_hbm.1, s32[1,1024]{1,0:T(1,128)} %bitcast.15, s32[1,1024]{1,0:T(1,128)} %bitcast.16), custom_call_target="tpu_custom_call" | custom-call | tf_op jit(solution)/shard_map/pack/pallas_call | solution.py:391
  4.5 10.3 %all-to-all-start = ((bf16[32,264,128]{2,1,0:T(8,128)(2,1)}), bf16[32,264,128]{2,1,0:T(8,128)(2,1)S(1)}, u32[]{:S(2)}, u32[]{:S(2)}) async-start(bf16[32,264,128]{2,1,0:T(8,128)(2,1)} %pack.1), calls=%async_computation | async-start | bytes 4325376 | tf_op jit(solution)/shard_map/all_to_all | solution.py:412
  15.5 2.1 %collective-permute-start.1 = (bf16[4,16,128]{2,1,0:T(8,128)(2,1)S(1)}, bf16[4,16,128]{2,1,0:T(8,128)(2,1)S(1)}, u32[]{:S(2)}, u32[]{:S(2)}) collective-permute-start(bf16[4,16,128]{2,1,0:T(8,128)(2,1)S(1)} %get-tuple-element.61), channel_id=1, source_target_pairs={{4,0},{8,4},{12,8},{16,12},{20,16},{24,20},{28,24},{5,1},{9,5},{13... | collective-permute-start | bytes 49160 | tf_op jit(solution)/shard_map/ppermute | solution.py:375
  17.6 3.7 %collective-permute-start = (bf16[4,16,128]{2,1,0:T(8,128)(2,1)S(1)}, bf16[4,16,128]{2,1,0:T(8,128)(2,1)S(1)}, u32[]{:S(2)}, u32[]{:S(2)}) collective-permute-start(bf16[4,16,128]{2,1,0:T(8,128)(2,1)S(1)} %get-tuple-element.62), channel_id=1, source_target_pairs={{0,4},{4,8},{8,12},{12,16},{16,20},{20,24},{24,28},{1,5},{5,9},{9,... | collective-permute-start | bytes 49160 | tf_op jit(solution)/shard_map/ppermute | solution.py:374
  21.3 40.1 %collective-permute-done.1 = bf16[4,16,128]{2,1,0:T(8,128)(2,1)S(1)} collective-permute-done((bf16[4,16,128]{2,1,0:T(8,128)(2,1)S(1)}, bf16[4,16,128]{2,1,0:T(8,128)(2,1)S(1)}, u32[]{:S(2)}, u32[]{:S(2)}) %collective-permute-start.1) | collective-permute-done | bytes 16416 | tf_op jit(solution)/shard_map/ppermute | solution.py:375
  61.5 4.6 %all-to-all-done.refs_0_ = bf16[32,264,128]{2,1,0:T(8,128)(2,1)S(1)} async-done(((bf16[32,264,128]{2,1,0:T(8,128)(2,1)}), bf16[32,264,128]{2,1,0:T(8,128)(2,1)S(1)}, u32[]{:S(2)}, u32[]{:S(2)}) %all-to-all-start) | async-done | bytes 2162720 | tf_op jit(solution)/shard_map/all_to_all | solution.py:412
  66.1 1.4 %cell_sum.1 = bf16[16,64,128]{2,1,0:T(8,128)(2,1)} custom-call(bf16[32,264,128]{2,1,0:T(8,128)(2,1)S(1)} %all-to-all-done.refs_0_), custom_call_target="tpu_custom_call" | custom-call | tf_op jit(solution)/shard_map/cell_sum/pallas_call | solution.py:430
  67.5 10.6 %all-to-all-start.1 = ((bf16[16,64,128]{2,1,0:T(8,128)(2,1)}), bf16[16,64,128]{2,1,0:T(8,128)(2,1)S(1)}, u32[]{:S(2)}, u32[]{:S(2)}) async-start(bf16[16,64,128]{2,1,0:T(8,128)(2,1)} %cell_sum.1), calls=%async_computation.1 | async-start | bytes 524288 | tf_op jit(solution)/shard_map/all_to_all | solution.py:438
  78.1 1.3 %collective-permute-start.3 = (bf16[24,4,128]{2,1,0:T(4,128)(2,1)S(1)}, bf16[24,4,128]{2,1,0:T(4,128)(2,1)S(1)}, u32[]{:S(2)}, u32[]{:S(2)}) collective-permute-start(bf16[24,4,128]{2,1,0:T(4,128)(2,1)S(1)} %get-tuple-element.59), channel_id=1, source_target_pairs={{1,0},{2,1},{3,2},{5,4},{6,5},{7,6},{9,8},{10,9},{11,10},{13,12},{... | collective-permute-start | bytes 73736 | tf_op jit(solution)/shard_map/ppermute | solution.py:375
  79.4 4.5 %collective-permute-start.2 = (bf16[24,4,128]{2,1,0:T(4,128)(2,1)S(1)}, bf16[24,4,128]{2,1,0:T(4,128)(2,1)S(1)}, u32[]{:S(2)}, u32[]{:S(2)}) collective-permute-start(bf16[24,4,128]{2,1,0:T(4,128)(2,1)S(1)} %get-tuple-element.60), channel_id=1, source_target_pairs={{0,1},{1,2},{2,3},{4,5},{5,6},{6,7},{8,9},{9,10},{10,11},{12,13},{... | collective-permute-start | bytes 73736 | tf_op jit(solution)/shard_map/ppermute | solution.py:374
  84.0 1.5 %collective-permute-done.2.south_ref = bf16[24,4,128]{2,1,0:T(4,128)(2,1)S(1)} collective-permute-done((bf16[24,4,128]{2,1,0:T(4,128)(2,1)S(1)}, bf16[24,4,128]{2,1,0:T(4,128)(2,1)S(1)}, u32[]{:S(2)}, u32[]{:S(2)}) %collective-permute-start.2) | collective-permute-done | bytes 24608 | tf_op jit(solution)/shard_map/ppermute | solution.py:374
  85.5 3.8 %all-to-all-done.1 = bf16[16,64,128]{2,1,0:T(8,128)(2,1)S(1)} async-done(((bf16[16,64,128]{2,1,0:T(8,128)(2,1)}), bf16[16,64,128]{2,1,0:T(8,128)(2,1)S(1)}, u32[]{:S(2)}, u32[]{:S(2)}) %all-to-all-start.1) | async-done | bytes 262176 | tf_op jit(solution)/shard_map/all_to_all | solution.py:438
  89.2 1.0 dft.1
  90.2 3.5 %all-to-all-start.2 = ((bf16[16,64,128]{2,1,0:T(8,128)(2,1)}), bf16[16,64,128]{2,1,0:T(8,128)(2,1)S(1)}, u32[]{:S(2)}, u32[]{:S(2)}) async-start(bf16[16,64,128]{2,1,0:T(8,128)(2,1)} %bitcast.4), calls=%async_computation.2 | async-start | bytes 524288 | tf_op jit(solution)/shard_map/all_to_all | solution.py:449
  93.8 11.3 %all-to-all-done.2.mid_ref = bf16[16,64,128]{2,1,0:T(8,128)(2,1)S(1)} async-done(((bf16[16,64,128]{2,1,0:T(8,128)(2,1)}), bf16[16,64,128]{2,1,0:T(8,128)(2,1)S(1)}, u32[]{:S(2)}, u32[]{:S(2)}) %all-to-all-start.2) | async-done | bytes 262176 | tf_op jit(solution)/shard_map/all_to_all | solution.py:449
  105.4 4.0 %collective-permute-start.4 = (bf16[3,64,128]{2,1,0:T(8,128)(2,1)S(1)}, bf16[3,64,128]{2,1,0:T(8,128)(2,1)S(1)}, u32[]{:S(2)}, u32[]{:S(2)}) collective-permute-start(bf16[3,64,128]{2,1,0:T(8,128)(2,1)S(1)} %bitcast.14), channel_id=1, source_target_pairs={{0,1},{1,2},{2,3},{4,5},{5,6},{6,7},{8,9},{9,10},{10,11},{12,13},{... | collective-permute-start | bytes 147464 | tf_op jit(solution)/shard_map/ppermute | solution.py:374
  109.3 1.3 %collective-permute-start.5 = (bf16[3,64,128]{2,1,0:T(8,128)(2,1)S(1)}, bf16[3,64,128]{2,1,0:T(8,128)(2,1)S(1)}, u32[]{:S(2)}, u32[]{:S(2)}) collective-permute-start(bf16[3,64,128]{2,1,0:T(8,128)(2,1)S(1)} %bitcast.13), channel_id=1, source_target_pairs={{1,0},{2,1},{3,2},{5,4},{6,5},{7,6},{9,8},{10,9},{11,10},{13,12},{... | collective-permute-start | bytes 147464 | tf_op jit(solution)/shard_map/ppermute | solution.py:375
  110.6 2.5 %coef.1.refs_1_.coef_ref = f32[22,7,24,128]{3,2,1,0:T(8,128)S(1)} custom-call(f32[2]{0:T(128)S(1)} %convert_multiply_fusion.omega_ref, f32[4]{0:T(128)S(1)} %copy-done, f32[4]{0:T(128)S(1)} %copy-done.1, bf16[24,4,128]{2,1,0:T(4,128)(2,1)S(1)} %collective-permute-done.2.south_ref, bf16[24,16,128]{2,1,0:T(8,128)(2,1)S(1)} %pad_maximum_fusion.ids_ref, ...), custom_call_target="tpu_custom_call" | custom-call | tf_op jit(solution)/shard_map/coef/pallas_call | solution.py:458
  113.2 2.3 %collective-permute-done.5.yhi_ref = bf16[3,64,128]{2,1,0:T(8,128)(2,1)S(1)} collective-permute-done((bf16[3,64,128]{2,1,0:T(8,128)(2,1)S(1)}, bf16[3,64,128]{2,1,0:T(8,128)(2,1)S(1)}, u32[]{:S(2)}, u32[]{:S(2)}) %collective-permute-start.5) | collective-permute-done | bytes 49184 | tf_op jit(solution)/shard_map/ppermute | solution.py:375
  115.7 4.0 %collective-permute-start.6 = (bf16[3,96,128]{2,1,0:T(8,128)(2,1)S(1)}, bf16[3,96,128]{2,1,0:T(8,128)(2,1)S(1)}, u32[]{:S(2)}, u32[]{:S(2)}) collective-permute-start(bf16[3,96,128]{2,1,0:T(8,128)(2,1)S(1)} %get-tuple-element.47), channel_id=1, source_target_pairs={{0,4},{4,8},{8,12},{12,16},{16,20},{20,24},{24,28},{1,5},{5,9},{9,... | collective-permute-start | bytes 221192 | tf_op jit(solution)/shard_map/ppermute | solution.py:481
  119.7 1.9 %collective-permute-start.7 = (bf16[3,96,128]{2,1,0:T(8,128)(2,1)S(1)}, bf16[3,96,128]{2,1,0:T(8,128)(2,1)S(1)}, u32[]{:S(2)}, u32[]{:S(2)}) collective-permute-start(bf16[3,96,128]{2,1,0:T(8,128)(2,1)S(1)} %get-tuple-element.48), channel_id=1, source_target_pairs={{4,0},{8,4},{12,8},{16,12},{20,16},{24,20},{28,24},{5,1},{9,5},{13... | collective-permute-start | bytes 221192 | tf_op jit(solution)/shard_map/ppermute | solution.py:482
  121.6 2.4 %inner.1 = (f32[16,4,24,128]{3,2,1,0:T(8,128)S(1)}, f32[16,4,24,128]{3,2,1,0:T(8,128)S(1)}, f32[16,4,24,128]{3,2,1,0:T(8,128)S(1)}, f32[2,2,10,16,128]{4,3,2,1,0:T(8,128)S(1)}) custom-call(f32[16,4,24,128]{3,2,1,0:T(8,128)S(1)} %get-tuple-element.49.refs_0_.s_ref, f32[22,7,24,128]{3,2,1,0:T(8,128)S(1)} %coef.1.refs_1_.coef_ref), custom_call_target="tpu_custom_call" | custom-call | tf_op jit(solution)/shard_map/inner/pallas_call | solution.py:483
  124.1 1.9 %collective-permute-done.7.xhi_ref = bf16[3,96,128]{2,1,0:T(8,128)(2,1)S(1)} collective-permute-done((bf16[3,96,128]{2,1,0:T(8,128)(2,1)S(1)}, bf16[3,96,128]{2,1,0:T(8,128)(2,1)S(1)}, u32[]{:S(2)}, u32[]{:S(2)}) %collective-permute-start.7) | collective-permute-done | bytes 73760 | tf_op jit(solution)/shard_map/ppermute | solution.py:482
  125.9 2.0 %outer.1 = f32[2,2,16,16,128]{4,3,2,1,0:T(8,128)} custom-call(bf16[3,96,128]{2,1,0:T(8,128)(2,1)S(1)} %collective-permute-done.6.xlo_ref, bf16[3,96,128]{2,1,0:T(8,128)(2,1)S(1)} %collective-permute-done.7.xhi_ref, f32[16,4,24,128]{3,2,1,0:T(8,128)S(1)} %get-tuple-element.49.refs_0_.s_ref, f32[16,4,24,128]{3,2,1,0:T(8,128)S(1)} %get-tuple-element.51.f1_ref, ...), custom_call_target="tpu_custom_call" | custom-call | tf_op jit(solution)/shard_map/outer/pallas_call | solution.py:493
  (25 shorter events, 1.1 us)
Async XLA Ops:
  4.5 11.0 %copy-start.2 = (s32[16,16,128]{2,1,0:T(8,128)S(1)}, s32[16,16,128]{2,1,0:T(8,128)}, u32[]{:S(2)}) copy-start(s32[16,16,128]{2,1,0:T(8,128)} %param.9) | copy-start | bytes 393220
  4.5 61.6 %all-to-all-start = ((bf16[32,264,128]{2,1,0:T(8,128)(2,1)}), bf16[32,264,128]{2,1,0:T(8,128)(2,1)S(1)}, u32[]{:S(2)}, u32[]{:S(2)}) async-start(bf16[32,264,128]{2,1,0:T(8,128)(2,1)} %pack.1), calls=%async_computation | async-start | bytes 4325376 | tf_op jit(solution)/shard_map/all_to_all | solution.py:412
  15.5 46.0 %collective-permute-start.1 = (bf16[4,16,128]{2,1,0:T(8,128)(2,1)S(1)}, bf16[4,16,128]{2,1,0:T(8,128)(2,1)S(1)}, u32[]{:S(2)}, u32[]{:S(2)}) collective-permute-start(bf16[4,16,128]{2,1,0:T(8,128)(2,1)S(1)} %get-tuple-element.61), channel_id=1, source_target_pairs={{4,0},{8,4},{12,8},{16,12},{20,16},{24,20},{28,24},{5,1},{9,5},{13... | collective-permute-start | bytes 49160 | tf_op jit(solution)/shard_map/ppermute | solution.py:375
  17.6 43.9 %collective-permute-start = (bf16[4,16,128]{2,1,0:T(8,128)(2,1)S(1)}, bf16[4,16,128]{2,1,0:T(8,128)(2,1)S(1)}, u32[]{:S(2)}, u32[]{:S(2)}) collective-permute-start(bf16[4,16,128]{2,1,0:T(8,128)(2,1)S(1)} %get-tuple-element.62), channel_id=1, source_target_pairs={{0,4},{4,8},{8,12},{12,16},{16,20},{20,24},{24,28},{1,5},{5,9},{9,... | collective-permute-start | bytes 49160 | tf_op jit(solution)/shard_map/ppermute | solution.py:374
  67.5 43.2 %copy-start = (f32[4]{0:T(128)S(1)}, f32[4]{0:T(128)}, u32[]{:S(2)}) copy-start(f32[4]{0:T(128)} %conductivity_ref.1) | copy-start | bytes 52
  67.5 43.2 %copy-start.1 = (f32[4]{0:T(128)S(1)}, f32[4]{0:T(128)}, u32[]{:S(2)}) copy-start(f32[4]{0:T(128)} %capacity_ref.1) | copy-start | bytes 52
  67.5 21.7 %all-to-all-start.1 = ((bf16[16,64,128]{2,1,0:T(8,128)(2,1)}), bf16[16,64,128]{2,1,0:T(8,128)(2,1)S(1)}, u32[]{:S(2)}, u32[]{:S(2)}) async-start(bf16[16,64,128]{2,1,0:T(8,128)(2,1)} %cell_sum.1), calls=%async_computation.1 | async-start | bytes 524288 | tf_op jit(solution)/shard_map/all_to_all | solution.py:438
  78.1 5.9 %collective-permute-start.3 = (bf16[24,4,128]{2,1,0:T(4,128)(2,1)S(1)}, bf16[24,4,128]{2,1,0:T(4,128)(2,1)S(1)}, u32[]{:S(2)}, u32[]{:S(2)}) collective-permute-start(bf16[24,4,128]{2,1,0:T(4,128)(2,1)S(1)} %get-tuple-element.59), channel_id=1, source_target_pairs={{1,0},{2,1},{3,2},{5,4},{6,5},{7,6},{9,8},{10,9},{11,10},{13,12},{... | collective-permute-start | bytes 73736 | tf_op jit(solution)/shard_map/ppermute | solution.py:375
  79.4 6.1 %collective-permute-start.2 = (bf16[24,4,128]{2,1,0:T(4,128)(2,1)S(1)}, bf16[24,4,128]{2,1,0:T(4,128)(2,1)S(1)}, u32[]{:S(2)}, u32[]{:S(2)}) collective-permute-start(bf16[24,4,128]{2,1,0:T(4,128)(2,1)S(1)} %get-tuple-element.60), channel_id=1, source_target_pairs={{0,1},{1,2},{2,3},{4,5},{5,6},{6,7},{8,9},{9,10},{10,11},{12,13},{... | collective-permute-start | bytes 73736 | tf_op jit(solution)/shard_map/ppermute | solution.py:374
  90.2 14.9 %all-to-all-start.2 = ((bf16[16,64,128]{2,1,0:T(8,128)(2,1)}), bf16[16,64,128]{2,1,0:T(8,128)(2,1)S(1)}, u32[]{:S(2)}, u32[]{:S(2)}) async-start(bf16[16,64,128]{2,1,0:T(8,128)(2,1)} %bitcast.4), calls=%async_computation.2 | async-start | bytes 524288 | tf_op jit(solution)/shard_map/all_to_all | solution.py:449
  105.4 7.8 %collective-permute-start.4 = (bf16[3,64,128]{2,1,0:T(8,128)(2,1)S(1)}, bf16[3,64,128]{2,1,0:T(8,128)(2,1)S(1)}, u32[]{:S(2)}, u32[]{:S(2)}) collective-permute-start(bf16[3,64,128]{2,1,0:T(8,128)(2,1)S(1)} %bitcast.14), channel_id=1, source_target_pairs={{0,1},{1,2},{2,3},{4,5},{5,6},{6,7},{8,9},{9,10},{10,11},{12,13},{... | collective-permute-start | bytes 147464 | tf_op jit(solution)/shard_map/ppermute | solution.py:374
  109.3 6.2 %collective-permute-start.5 = (bf16[3,64,128]{2,1,0:T(8,128)(2,1)S(1)}, bf16[3,64,128]{2,1,0:T(8,128)(2,1)S(1)}, u32[]{:S(2)}, u32[]{:S(2)}) collective-permute-start(bf16[3,64,128]{2,1,0:T(8,128)(2,1)S(1)} %bitcast.13), channel_id=1, source_target_pairs={{1,0},{2,1},{3,2},{5,4},{6,5},{7,6},{9,8},{10,9},{11,10},{13,12},{... | collective-permute-start | bytes 147464 | tf_op jit(solution)/shard_map/ppermute | solution.py:375
  115.7 8.4 %collective-permute-start.6 = (bf16[3,96,128]{2,1,0:T(8,128)(2,1)S(1)}, bf16[3,96,128]{2,1,0:T(8,128)(2,1)S(1)}, u32[]{:S(2)}, u32[]{:S(2)}) collective-permute-start(bf16[3,96,128]{2,1,0:T(8,128)(2,1)S(1)} %get-tuple-element.47), channel_id=1, source_target_pairs={{0,4},{4,8},{8,12},{12,16},{16,20},{20,24},{24,28},{1,5},{5,9},{9,... | collective-permute-start | bytes 221192 | tf_op jit(solution)/shard_map/ppermute | solution.py:481
  119.7 6.2 %collective-permute-start.7 = (bf16[3,96,128]{2,1,0:T(8,128)(2,1)S(1)}, bf16[3,96,128]{2,1,0:T(8,128)(2,1)S(1)}, u32[]{:S(2)}, u32[]{:S(2)}) collective-permute-start(bf16[3,96,128]{2,1,0:T(8,128)(2,1)S(1)} %get-tuple-element.48), channel_id=1, source_target_pairs={{4,0},{8,4},{12,8},{16,12},{20,16},{24,20},{28,24},{5,1},{9,5},{13... | collective-permute-start | bytes 221192 | tf_op jit(solution)/shard_map/ppermute | solution.py:482

commit v8 on v7

--- a/solution.py
+++ b/solution.py
@@ -447,12 +447,6 @@
     )(weights, gathered.reshape(TIME, size_y, width))
     harmonic = harmonic.reshape(steps, comps * size_y, width)
     source = lax.all_to_all(harmonic, "tm", split_axis=0, concat_axis=0, tiled=True)
-    source, south, ids, north = lax.optimization_barrier((source, south, ids, north))
-
-    rows = source.reshape(size_x, comps, size_y, width)
-    rows = jnp.concatenate([rows[:, :, :WIDE], rows[:, :, size_y - WIDE :]], axis=2)
-    rows = jnp.transpose(rows, (2, 0, 1, 3)).reshape(2 * WIDE, size_x * comps, width)
-    ylo, yhi = swap(rows, "sy", 0, WIDE)
     harm_index = lax.axis_index("tm") * harms + jnp.arange(harms, dtype=jnp.int32)
     omega = omega_step * harm_index.astype(F32)
     coef = pl.pallas_call(
@@ -464,7 +458,12 @@
         compiler_params=params,
         name="coef",
     )(omega, conductivity, capacity, south, ids, north)
-    ylo, yhi, coef = lax.optimization_barrier((ylo, yhi, coef))
+    source, coef = lax.optimization_barrier((source, coef))
+
+    rows = source.reshape(size_x, comps, size_y, width)
+    rows = jnp.concatenate([rows[:, :, :WIDE], rows[:, :, size_y - WIDE :]], axis=2)
+    rows = jnp.transpose(rows, (2, 0, 1, 3)).reshape(2 * WIDE, size_x * comps, width)
+    ylo, yhi = swap(rows, "sy", 0, WIDE)
     widened = jax.ShapeDtypeStruct((size_x, comps, YE, width), F32)
     strip = jax.ShapeDtypeStruct((WIDE, comps * YE, width), BF16)
     source, first_rows, last_rows = pl.pallas_call(

time: 129 us -> 128 us (level)
    all_to_all x1, waiting for transfers between devices: 11.3 us -> 8.78 us  [body(): lax.all_to_all(harmonic, 'tm', split_axis=0, concat_axis=0, tiled=True)]
    ppermute x3, waiting for transfers between devices: 42.5 us -> 44.2 us  [swap(): lax.ppermute(lax.slice_in_dim(block, 0, width, axis=dim), axis, backward)]
  transfers between devices with their start and end apart: 11 -> 11, of which waited for: 7 -> 8; matrix products, arithmetic and copies ran while one was open for 0% -> 0% of each run, Pallas kernels for 4% -> 4%
where the time goes in v8:
time: 128 us
  waiting for transfers between devices  65.5 us (51%)
  starting transfers between devices  47.1 us (37%)
  Pallas kernels  14.5 us (11%)
    ppermute x3, waiting for transfers between devices, swap(): lax.ppermute(lax.slice_in_dim(block, 0, width, axis=dim), axis, backward)  44.2 us
    ppermute x3, starting transfers between devices, swap(): lax.ppermute(lax.slice_in_dim(block, size - width, size, axis=dim), axis,...  12.2 us
    all_to_all x1, starting transfers between devices, body(): lax.all_to_all(sums, 'tm', split_axis=0, concat_axis=0, tiled=True)  10.4 us
    all_to_all x1, starting transfers between devices, body(): lax.all_to_all(packed, ('sx', 'sy'), split_axis=0, concat_axis=0, tiled=T...  10.3 us
    all_to_all x1, waiting for transfers between devices, body(): lax.all_to_all(harmonic, 'tm', split_axis=0, concat_axis=0, tiled=True)  8.78 us
    ppermute x3, starting transfers between devices, swap(): lax.ppermute(lax.slice_in_dim(block, 0, width, axis=dim), axis, backward)  4.72 us
    all_to_all x1, waiting for transfers between devices, body(): lax.all_to_all(packed, ('sx', 'sy'), split_axis=0, concat_axis=0, tiled=T...  4.61 us
    pallas_call x1, Pallas kernels, body(): pl.pallas_call(pack_kernel, out_shape=pltpu.HBM((OWNERS, times * CAP + 8,...  4.45 us
  transfers between devices with their start and end apart: 11, of which 8 were waited for; matrix products, arithmetic and copies ran while one was open for 0% of the time, Pallas kernels for 4%

profile of v8, /device:TPU:8, one launch (start us, length us, event | category | flops | bytes accessed | tf_op | source)
XLA Modules:
  0.0 127.8 jit_solution(16205509045607599152)
XLA Ops:
  0.0 4.4 %pack.1 = bf16[32,264,128]{2,1,0:T(8,128)(2,1)} custom-call(bf16[4,1024,128]{2,1,0:T(8,128)(2,1)} %wall_hbm.1, s32[1,1024]{1,0:T(1,128)} %bitcast.15, s32[1,1024]{1,0:T(1,128)} %bitcast.16), custom_call_target="tpu_custom_call" | custom-call | tf_op jit(solution)/shard_map/pack/pallas_call | solution.py:391
  4.5 10.3 %all-to-all-start = ((bf16[32,264,128]{2,1,0:T(8,128)(2,1)}), bf16[32,264,128]{2,1,0:T(8,128)(2,1)S(1)}, u32[]{:S(2)}, u32[]{:S(2)}) async-start(bf16[32,264,128]{2,1,0:T(8,128)(2,1)} %pack.1), calls=%async_computation | async-start | bytes 4325376 | tf_op jit(solution)/shard_map/all_to_all | solution.py:412
  15.5 2.1 %collective-permute-start.1 = (bf16[4,16,128]{2,1,0:T(8,128)(2,1)S(1)}, bf16[4,16,128]{2,1,0:T(8,128)(2,1)S(1)}, u32[]{:S(2)}, u32[]{:S(2)}) collective-permute-start(bf16[4,16,128]{2,1,0:T(8,128)(2,1)S(1)} %get-tuple-element.51), channel_id=1, source_target_pairs={{4,0},{8,4},{12,8},{16,12},{20,16},{24,20},{28,24},{5,1},{9,5},{13... | collective-permute-start | bytes 49160 | tf_op jit(solution)/shard_map/ppermute | solution.py:375
  17.6 3.7 %collective-permute-start = (bf16[4,16,128]{2,1,0:T(8,128)(2,1)S(1)}, bf16[4,16,128]{2,1,0:T(8,128)(2,1)S(1)}, u32[]{:S(2)}, u32[]{:S(2)}) collective-permute-start(bf16[4,16,128]{2,1,0:T(8,128)(2,1)S(1)} %get-tuple-element.52), channel_id=1, source_target_pairs={{0,4},{4,8},{8,12},{12,16},{16,20},{20,24},{24,28},{1,5},{5,9},{9,... | collective-permute-start | bytes 49160 | tf_op jit(solution)/shard_map/ppermute | solution.py:374
  21.3 40.1 %collective-permute-done.1 = bf16[4,16,128]{2,1,0:T(8,128)(2,1)S(1)} collective-permute-done((bf16[4,16,128]{2,1,0:T(8,128)(2,1)S(1)}, bf16[4,16,128]{2,1,0:T(8,128)(2,1)S(1)}, u32[]{:S(2)}, u32[]{:S(2)}) %collective-permute-start.1) | collective-permute-done | bytes 16416 | tf_op jit(solution)/shard_map/ppermute | solution.py:375
  61.5 4.6 %all-to-all-done.refs_0_ = bf16[32,264,128]{2,1,0:T(8,128)(2,1)S(1)} async-done(((bf16[32,264,128]{2,1,0:T(8,128)(2,1)}), bf16[32,264,128]{2,1,0:T(8,128)(2,1)S(1)}, u32[]{:S(2)}, u32[]{:S(2)}) %all-to-all-start) | async-done | bytes 2162720 | tf_op jit(solution)/shard_map/all_to_all | solution.py:412
  66.1 1.4 %cell_sum.1 = bf16[16,64,128]{2,1,0:T(8,128)(2,1)} custom-call(bf16[32,264,128]{2,1,0:T(8,128)(2,1)S(1)} %all-to-all-done.refs_0_), custom_call_target="tpu_custom_call" | custom-call | tf_op jit(solution)/shard_map/cell_sum/pallas_call | solution.py:430
  67.5 10.4 %all-to-all-start.1 = ((bf16[16,64,128]{2,1,0:T(8,128)(2,1)}), bf16[16,64,128]{2,1,0:T(8,128)(2,1)S(1)}, u32[]{:S(2)}, u32[]{:S(2)}) async-start(bf16[16,64,128]{2,1,0:T(8,128)(2,1)} %cell_sum.1), calls=%async_computation.1 | async-start | bytes 524288 | tf_op jit(solution)/shard_map/all_to_all | solution.py:438
  78.0 1.3 %collective-permute-start.3 = (bf16[24,4,128]{2,1,0:T(4,128)(2,1)S(1)}, bf16[24,4,128]{2,1,0:T(4,128)(2,1)S(1)}, u32[]{:S(2)}, u32[]{:S(2)}) collective-permute-start(bf16[24,4,128]{2,1,0:T(4,128)(2,1)S(1)} %get-tuple-element.49), channel_id=1, source_target_pairs={{1,0},{2,1},{3,2},{5,4},{6,5},{7,6},{9,8},{10,9},{11,10},{13,12},{... | collective-permute-start | bytes 73736 | tf_op jit(solution)/shard_map/ppermute | solution.py:375
  79.3 4.5 %collective-permute-start.2 = (bf16[24,4,128]{2,1,0:T(4,128)(2,1)S(1)}, bf16[24,4,128]{2,1,0:T(4,128)(2,1)S(1)}, u32[]{:S(2)}, u32[]{:S(2)}) collective-permute-start(bf16[24,4,128]{2,1,0:T(4,128)(2,1)S(1)} %get-tuple-element.50), channel_id=1, source_target_pairs={{0,1},{1,2},{2,3},{4,5},{5,6},{6,7},{8,9},{9,10},{10,11},{12,13},{... | collective-permute-start | bytes 73736 | tf_op jit(solution)/shard_map/ppermute | solution.py:374
  83.8 1.5 %collective-permute-done.2.south_ref = bf16[24,4,128]{2,1,0:T(4,128)(2,1)S(1)} collective-permute-done((bf16[24,4,128]{2,1,0:T(4,128)(2,1)S(1)}, bf16[24,4,128]{2,1,0:T(4,128)(2,1)S(1)}, u32[]{:S(2)}, u32[]{:S(2)}) %collective-permute-start.2) | collective-permute-done | bytes 24608 | tf_op jit(solution)/shard_map/ppermute | solution.py:374
  85.3 3.8 %all-to-all-done.1 = bf16[16,64,128]{2,1,0:T(8,128)(2,1)S(1)} async-done(((bf16[16,64,128]{2,1,0:T(8,128)(2,1)}), bf16[16,64,128]{2,1,0:T(8,128)(2,1)S(1)}, u32[]{:S(2)}, u32[]{:S(2)}) %all-to-all-start.1) | async-done | bytes 262176 | tf_op jit(solution)/shard_map/all_to_all | solution.py:438
  89.1 1.0 dft.1
  90.1 3.5 %all-to-all-start.2 = ((bf16[16,64,128]{2,1,0:T(8,128)(2,1)}), bf16[16,64,128]{2,1,0:T(8,128)(2,1)S(1)}, u32[]{:S(2)}, u32[]{:S(2)}) async-start(bf16[16,64,128]{2,1,0:T(8,128)(2,1)} %bitcast.4), calls=%async_computation.2 | async-start | bytes 524288 | tf_op jit(solution)/shard_map/all_to_all | solution.py:449
  93.7 2.5 %coef.1.refs_1_.coef_ref = f32[22,7,24,128]{3,2,1,0:T(8,128)S(1)} custom-call(f32[2]{0:T(128)S(1)} %convert_multiply_fusion.omega_ref, f32[4]{0:T(128)S(1)} %copy-done, f32[4]{0:T(128)S(1)} %copy-done.1, bf16[24,4,128]{2,1,0:T(4,128)(2,1)S(1)} %collective-permute-done.2.south_ref, bf16[24,16,128]{2,1,0:T(8,128)(2,1)S(1)} %pad_maximum_fusion.ids_ref, ...), custom_call_target="tpu_custom_call" | custom-call | tf_op jit(solution)/shard_map/coef/pallas_call | solution.py:452
  96.2 8.8 %all-to-all-done.2.mid_ref = bf16[16,64,128]{2,1,0:T(8,128)(2,1)S(1)} async-done(((bf16[16,64,128]{2,1,0:T(8,128)(2,1)}), bf16[16,64,128]{2,1,0:T(8,128)(2,1)S(1)}, u32[]{:S(2)}, u32[]{:S(2)}) %all-to-all-start.2) | async-done | bytes 262176 | tf_op jit(solution)/shard_map/all_to_all | solution.py:449
  105.2 4.0 %collective-permute-start.4 = (bf16[3,64,128]{2,1,0:T(8,128)(2,1)S(1)}, bf16[3,64,128]{2,1,0:T(8,128)(2,1)S(1)}, u32[]{:S(2)}, u32[]{:S(2)}) collective-permute-start(bf16[3,64,128]{2,1,0:T(8,128)(2,1)S(1)} %bitcast.14), channel_id=1, source_target_pairs={{0,1},{1,2},{2,3},{4,5},{5,6},{6,7},{8,9},{9,10},{10,11},{12,13},{... | collective-permute-start | bytes 147464 | tf_op jit(solution)/shard_map/ppermute | solution.py:374
  109.2 1.3 %collective-permute-start.5 = (bf16[3,64,128]{2,1,0:T(8,128)(2,1)S(1)}, bf16[3,64,128]{2,1,0:T(8,128)(2,1)S(1)}, u32[]{:S(2)}, u32[]{:S(2)}) collective-permute-start(bf16[3,64,128]{2,1,0:T(8,128)(2,1)S(1)} %bitcast.13), channel_id=1, source_target_pairs={{1,0},{2,1},{3,2},{5,4},{6,5},{7,6},{9,8},{10,9},{11,10},{13,12},{... | collective-permute-start | bytes 147464 | tf_op jit(solution)/shard_map/ppermute | solution.py:375
  111.3 4.1 %collective-permute-done.5.yhi_ref = bf16[3,64,128]{2,1,0:T(8,128)(2,1)S(1)} collective-permute-done((bf16[3,64,128]{2,1,0:T(8,128)(2,1)S(1)}, bf16[3,64,128]{2,1,0:T(8,128)(2,1)S(1)}, u32[]{:S(2)}, u32[]{:S(2)}) %collective-permute-start.5) | collective-permute-done | bytes 49184 | tf_op jit(solution)/shard_map/ppermute | solution.py:375
  115.6 4.0 %collective-permute-start.6 = (bf16[3,96,128]{2,1,0:T(8,128)(2,1)S(1)}, bf16[3,96,128]{2,1,0:T(8,128)(2,1)S(1)}, u32[]{:S(2)}, u32[]{:S(2)}) collective-permute-start(bf16[3,96,128]{2,1,0:T(8,128)(2,1)S(1)} %get-tuple-element.37), channel_id=1, source_target_pairs={{0,4},{4,8},{8,12},{12,16},{16,20},{20,24},{24,28},{1,5},{5,9},{9,... | collective-permute-start | bytes 221192 | tf_op jit(solution)/shard_map/ppermute | solution.py:480
  119.5 1.9 %collective-permute-start.7 = (bf16[3,96,128]{2,1,0:T(8,128)(2,1)S(1)}, bf16[3,96,128]{2,1,0:T(8,128)(2,1)S(1)}, u32[]{:S(2)}, u32[]{:S(2)}) collective-permute-start(bf16[3,96,128]{2,1,0:T(8,128)(2,1)S(1)} %get-tuple-element.38), channel_id=1, source_target_pairs={{4,0},{8,4},{12,8},{16,12},{20,16},{24,20},{28,24},{5,1},{9,5},{13... | collective-permute-start | bytes 221192 | tf_op jit(solution)/shard_map/ppermute | solution.py:481
  121.5 2.4 %inner.1 = (f32[16,4,24,128]{3,2,1,0:T(8,128)S(1)}, f32[16,4,24,128]{3,2,1,0:T(8,128)S(1)}, f32[16,4,24,128]{3,2,1,0:T(8,128)S(1)}, f32[2,2,10,16,128]{4,3,2,1,0:T(8,128)S(1)}) custom-call(f32[16,4,24,128]{3,2,1,0:T(8,128)S(1)} %get-tuple-element.39.refs_0_.s_ref, f32[22,7,24,128]{3,2,1,0:T(8,128)S(1)} %coef.1.refs_1_.coef_ref), custom_call_target="tpu_custom_call" | custom-call | tf_op jit(solution)/shard_map/inner/pallas_call | solution.py:482
  123.9 1.9 %collective-permute-done.7.xhi_ref = bf16[3,96,128]{2,1,0:T(8,128)(2,1)S(1)} collective-permute-done((bf16[3,96,128]{2,1,0:T(8,128)(2,1)S(1)}, bf16[3,96,128]{2,1,0:T(8,128)(2,1)S(1)}, u32[]{:S(2)}, u32[]{:S(2)}) %collective-permute-start.7) | collective-permute-done | bytes 73760 | tf_op jit(solution)/shard_map/ppermute | solution.py:481
  125.8 2.0 %outer.1 = f32[2,2,16,16,128]{4,3,2,1,0:T(8,128)} custom-call(bf16[3,96,128]{2,1,0:T(8,128)(2,1)S(1)} %collective-permute-done.6.xlo_ref, bf16[3,96,128]{2,1,0:T(8,128)(2,1)S(1)} %collective-permute-done.7.xhi_ref, f32[16,4,24,128]{3,2,1,0:T(8,128)S(1)} %get-tuple-element.39.refs_0_.s_ref, f32[16,4,24,128]{3,2,1,0:T(8,128)S(1)} %get-tuple-element.41.f1_ref, ...), custom_call_target="tpu_custom_call" | custom-call | tf_op jit(solution)/shard_map/outer/pallas_call | solution.py:492
  (25 shorter events, 1.9 us)
Async XLA Ops:
  4.5 11.0 %copy-start.2 = (s32[16,16,128]{2,1,0:T(8,128)S(1)}, s32[16,16,128]{2,1,0:T(8,128)}, u32[]{:S(2)}) copy-start(s32[16,16,128]{2,1,0:T(8,128)} %param.9) | copy-start | bytes 393220
  4.5 61.6 %all-to-all-start = ((bf16[32,264,128]{2,1,0:T(8,128)(2,1)}), bf16[32,264,128]{2,1,0:T(8,128)(2,1)S(1)}, u32[]{:S(2)}, u32[]{:S(2)}) async-start(bf16[32,264,128]{2,1,0:T(8,128)(2,1)} %pack.1), calls=%async_computation | async-start | bytes 4325376 | tf_op jit(solution)/shard_map/all_to_all | solution.py:412
  15.5 46.0 %collective-permute-start.1 = (bf16[4,16,128]{2,1,0:T(8,128)(2,1)S(1)}, bf16[4,16,128]{2,1,0:T(8,128)(2,1)S(1)}, u32[]{:S(2)}, u32[]{:S(2)}) collective-permute-start(bf16[4,16,128]{2,1,0:T(8,128)(2,1)S(1)} %get-tuple-element.51), channel_id=1, source_target_pairs={{4,0},{8,4},{12,8},{16,12},{20,16},{24,20},{28,24},{5,1},{9,5},{13... | collective-permute-start | bytes 49160 | tf_op jit(solution)/shard_map/ppermute | solution.py:375
  17.6 76.0 %copy-start = (f32[4]{0:T(128)S(1)}, f32[4]{0:T(128)}, u32[]{:S(2)}) copy-start(f32[4]{0:T(128)} %conductivity_ref.1) | copy-start | bytes 52
  17.6 76.0 %copy-start.1 = (f32[4]{0:T(128)S(1)}, f32[4]{0:T(128)}, u32[]{:S(2)}) copy-start(f32[4]{0:T(128)} %capacity_ref.1) | copy-start | bytes 52
  17.6 43.8 %collective-permute-start = (bf16[4,16,128]{2,1,0:T(8,128)(2,1)S(1)}, bf16[4,16,128]{2,1,0:T(8,128)(2,1)S(1)}, u32[]{:S(2)}, u32[]{:S(2)}) collective-permute-start(bf16[4,16,128]{2,1,0:T(8,128)(2,1)S(1)} %get-tuple-element.52), channel_id=1, source_target_pairs={{0,4},{4,8},{8,12},{12,16},{16,20},{20,24},{24,28},{1,5},{5,9},{9,... | collective-permute-start | bytes 49160 | tf_op jit(solution)/shard_map/ppermute | solution.py:374
  67.5 21.6 %all-to-all-start.1 = ((bf16[16,64,128]{2,1,0:T(8,128)(2,1)}), bf16[16,64,128]{2,1,0:T(8,128)(2,1)S(1)}, u32[]{:S(2)}, u32[]{:S(2)}) async-start(bf16[16,64,128]{2,1,0:T(8,128)(2,1)} %cell_sum.1), calls=%async_computation.1 | async-start | bytes 524288 | tf_op jit(solution)/shard_map/all_to_all | solution.py:438
  78.0 5.9 %collective-permute-start.3 = (bf16[24,4,128]{2,1,0:T(4,128)(2,1)S(1)}, bf16[24,4,128]{2,1,0:T(4,128)(2,1)S(1)}, u32[]{:S(2)}, u32[]{:S(2)}) collective-permute-start(bf16[24,4,128]{2,1,0:T(4,128)(2,1)S(1)} %get-tuple-element.49), channel_id=1, source_target_pairs={{1,0},{2,1},{3,2},{5,4},{6,5},{7,6},{9,8},{10,9},{11,10},{13,12},{... | collective-permute-start | bytes 73736 | tf_op jit(solution)/shard_map/ppermute | solution.py:375
  79.3 6.1 %collective-permute-start.2 = (bf16[24,4,128]{2,1,0:T(4,128)(2,1)S(1)}, bf16[24,4,128]{2,1,0:T(4,128)(2,1)S(1)}, u32[]{:S(2)}, u32[]{:S(2)}) collective-permute-start(bf16[24,4,128]{2,1,0:T(4,128)(2,1)S(1)} %get-tuple-element.50), channel_id=1, source_target_pairs={{0,1},{1,2},{2,3},{4,5},{5,6},{6,7},{8,9},{9,10},{10,11},{12,13},{... | collective-permute-start | bytes 73736 | tf_op jit(solution)/shard_map/ppermute | solution.py:374
  90.1 14.9 %all-to-all-start.2 = ((bf16[16,64,128]{2,1,0:T(8,128)(2,1)}), bf16[16,64,128]{2,1,0:T(8,128)(2,1)S(1)}, u32[]{:S(2)}, u32[]{:S(2)}) async-start(bf16[16,64,128]{2,1,0:T(8,128)(2,1)} %bitcast.4), calls=%async_computation.2 | async-start | bytes 524288 | tf_op jit(solution)/shard_map/all_to_all | solution.py:449
  105.2 6.1 %collective-permute-start.4 = (bf16[3,64,128]{2,1,0:T(8,128)(2,1)S(1)}, bf16[3,64,128]{2,1,0:T(8,128)(2,1)S(1)}, u32[]{:S(2)}, u32[]{:S(2)}) collective-permute-start(bf16[3,64,128]{2,1,0:T(8,128)(2,1)S(1)} %bitcast.14), channel_id=1, source_target_pairs={{0,1},{1,2},{2,3},{4,5},{5,6},{6,7},{8,9},{9,10},{10,11},{12,13},{... | collective-permute-start | bytes 147464 | tf_op jit(solution)/shard_map/ppermute | solution.py:374
  109.2 6.2 %collective-permute-start.5 = (bf16[3,64,128]{2,1,0:T(8,128)(2,1)S(1)}, bf16[3,64,128]{2,1,0:T(8,128)(2,1)S(1)}, u32[]{:S(2)}, u32[]{:S(2)}) collective-permute-start(bf16[3,64,128]{2,1,0:T(8,128)(2,1)S(1)} %bitcast.13), channel_id=1, source_target_pairs={{1,0},{2,1},{3,2},{5,4},{6,5},{7,6},{9,8},{10,9},{11,10},{13,12},{... | collective-permute-start | bytes 147464 | tf_op jit(solution)/shard_map/ppermute | solution.py:375
  115.6 8.3 %collective-permute-start.6 = (bf16[3,96,128]{2,1,0:T(8,128)(2,1)S(1)}, bf16[3,96,128]{2,1,0:T(8,128)(2,1)S(1)}, u32[]{:S(2)}, u32[]{:S(2)}) collective-permute-start(bf16[3,96,128]{2,1,0:T(8,128)(2,1)S(1)} %get-tuple-element.37), channel_id=1, source_target_pairs={{0,4},{4,8},{8,12},{12,16},{16,20},{20,24},{24,28},{1,5},{5,9},{9,... | collective-permute-start | bytes 221192 | tf_op jit(solution)/shard_map/ppermute | solution.py:480
  119.5 6.2 %collective-permute-start.7 = (bf16[3,96,128]{2,1,0:T(8,128)(2,1)S(1)}, bf16[3,96,128]{2,1,0:T(8,128)(2,1)S(1)}, u32[]{:S(2)}, u32[]{:S(2)}) collective-permute-start(bf16[3,96,128]{2,1,0:T(8,128)(2,1)S(1)} %get-tuple-element.38), channel_id=1, source_target_pairs={{4,0},{8,4},{12,8},{16,12},{20,16},{24,20},{28,24},{5,1},{9,5},{13... | collective-permute-start | bytes 221192 | tf_op jit(solution)/shard_map/ppermute | solution.py:481
